TPU v7x, 128 devices: a whole 4x4x4 slice. The times are simulated.
128 devices in a mesh: dp: 8 (over x, core), rows: 16 (over z, y).
Axes of the slice: x: 4, y: 4, z: 4, core: 2. Of those that a mesh axis runs over, the one named last changes fastest.
Arguments:
- item_table: float32 [524288, 128], P(('dp', 'rows')), may hold values from -3 to 3
- adagrad_state: float32 [524288, 128], P(('dp', 'rows')), may hold values from 0.0001 to 0.01
- history_ids: int32 [16384, 50], P(('dp', 'rows')), may hold values from 0 to 524287, as said below
- positive_ids: int32 [16384], P(('dp', 'rows')), may hold values from 0 to 524287, as said below
Outputs:
- new_table: float32 [524288, 128], P(('dp', 'rows'))
- new_state: float32 [524288, 128], P(('dp', 'rows'))
Inputs may be any that keep to these rules, and one draw needn't show every extreme that they name: `history_ids`: ids are counted over one device's 128 users (an aligned block of users), history and positive together, with repeats. In every such block, at most 128 ids have any one value of id // 4096, and some value has exactly 128; one value has exactly 128 in every block. Popular items repeat. `positive_ids`: counted together with history_ids as stated there.
All inputs are finite; a program needn't handle non-finite values.
Results may differ from a plain program's by a relative error of at most 0.00012.
Values sent between devices are 32-bit elements; how exact they have to be, the bound alone decides.
No kernel may reach another device: no remote copies, remote signals or barrier semaphores. Data moves between devices by JAX's collectives and lax.ppermute only.
A program may use at most 128 MiB of HBM per device.

v0:
```python
import jax
import jax.numpy as jnp
from jax import lax
from jax.sharding import Mesh
from jax.sharding import PartitionSpec as P

DP = ("dp_0", "dp_1")
ROWS = ("rows_0", "rows_1")
DP_ROWS = ("dp_0", "dp_1", "rows_0", "rows_1")


penalty_weight = 10.0
step_size = 0.05


def total_of_pieces(array, axis):
    blocks = lax.all_gather(array, axis)
    return blocks.sum(axis=0)


def one_axis_at_a_time(array, axes):
    for axis in axes:
        array = lax.psum(array, axis)
    return array


def owner_ranks(owner_dev, devices):
    total = owner_dev.shape[0]
    block = min(512, (total + 7) // 8 * 8)
    padded = (total + block - 1) // block * block
    owners_pad = jnp.concatenate([owner_dev, jnp.full((padded - total,), -1, jnp.int32)])
    owner_blocks = owners_pad.reshape(padded // block, block)
    lower = (
        jnp.arange(block, dtype=jnp.int32)[:, None] >= jnp.arange(block, dtype=jnp.int32)[None, :]
    ).astype(jnp.float32)
    columns = jnp.arange(devices, dtype=jnp.int32)[None, :]

    def step(carry, owners_blk):
        member = (owners_blk[:, None] == columns).astype(jnp.float32)
        prefix = jnp.dot(lower, member, preferred_element_type=jnp.float32)
        before = jnp.sum(member * carry[None, :], axis=1)
        ranks = jnp.sum(prefix * member, axis=1) + before - 1.0
        return (carry + jnp.sum(member, axis=0), ranks.astype(jnp.int32))

    start = jnp.zeros((devices,), jnp.float32)
    final, ranks = lax.scan(step, start, owner_blocks)
    return ranks.reshape(-1)[:total]


def shards(item_table, adagrad_state, history_ids, positive_ids):
    rows_dev, width = item_table.shape
    users_dev, hist_len = history_ids.shape
    n_data = lax.axis_size(DP)
    n_shard = lax.axis_size(ROWS)
    devices = n_data * n_shard
    requests = jnp.concatenate([history_ids, positive_ids[:, None]], axis=1).reshape(-1)
    request_count = requests.shape[0]
    capacity = max(8, (request_count * 5 // (2 * devices) + 7) // 8 * 8)
    owner_dev = requests // rows_dev
    local_row = requests % rows_dev
    slot_rank = owner_ranks(owner_dev, devices)
    flat_slot = owner_dev * capacity + slot_rank
    inverse = (
        jnp.full((devices * capacity,), request_count, jnp.int32)
        .at[flat_slot]
        .set(jnp.arange(request_count, dtype=jnp.int32))
    )
    local_pad = jnp.concatenate([local_row, jnp.full((1,), -1, jnp.int32)])
    wanted = jnp.take(local_pad, inverse, axis=0)
    item_gram = jnp.dot(
        item_table.T,
        item_table,
        precision=lax.Precision.HIGHEST,
        preferred_element_type=jnp.float32,
    )
    item_total = total_of_pieces(item_gram, DP_ROWS)
    asked = lax.all_to_all(
        wanted.reshape(devices, capacity), DP_ROWS, split_axis=0, concat_axis=0, tiled=True
    )
    present = asked >= 0
    picked = jnp.take(item_table, jnp.where(present, asked, 0), axis=0)
    fetched_rows = lax.all_to_all(
        picked * present[..., None].astype(jnp.float32),
        DP_ROWS,
        split_axis=0,
        concat_axis=0,
        tiled=True,
    )
    request_rows = jnp.take(
        fetched_rows.reshape(devices * capacity, width), flat_slot, axis=0
    ).reshape(users_dev, hist_len + 1, width)
    user_vecs = jnp.sum(request_rows[:, :hist_len], axis=1) / hist_len
    positive_vecs = request_rows[:, hist_len]
    score_gap = jnp.sum(user_vecs * positive_vecs, axis=1) - 1.0
    user_gram = jnp.dot(
        user_vecs.T, user_vecs, precision=lax.Precision.HIGHEST, preferred_element_type=jnp.float32
    )
    user_total = one_axis_at_a_time(user_gram, DP_ROWS)
    penalty_coef = penalty_weight / (rows_dev * devices)
    user_grad = 2.0 * score_gap[:, None] * positive_vecs + 2.0 * penalty_coef * jnp.dot(
        user_vecs, item_total, precision=lax.Precision.HIGHEST, preferred_element_type=jnp.float32
    )
    positive_grad = 2.0 * score_gap[:, None] * user_vecs
    per_history = jnp.broadcast_to((user_grad / hist_len)[:, None, :], (users_dev, hist_len, width))
    request_grad = jnp.concatenate([per_history, positive_grad[:, None, :]], axis=1).reshape(
        -1, width
    )
    grad_pad = jnp.concatenate([request_grad, jnp.zeros((1, width), jnp.float32)], axis=0)
    outgoing = jnp.take(grad_pad, inverse, axis=0)
    returned = lax.all_to_all(
        outgoing.reshape(devices, capacity, width), DP_ROWS, split_axis=0, concat_axis=0, tiled=True
    )
    present = asked >= 0
    target_rows = jnp.where(present, asked, 0).reshape(-1)
    masked_grad = (returned * present[..., None].astype(jnp.float32)).reshape(-1, width)
    row_grad = (
        2.0
        * penalty_coef
        * jnp.dot(
            item_table,
            user_total,
            precision=lax.Precision.HIGHEST,
            preferred_element_type=jnp.float32,
        )
    )
    row_grad = row_grad.at[target_rows].add(masked_grad)
    new_state = adagrad_state + row_grad * row_grad
    new_table = item_table - step_size * row_grad / jnp.sqrt(new_state)
    return (new_table, new_state)


def solution(mesh):
    finer = Mesh(mesh.devices.reshape(4, 2, 4, 4), ("dp_0", "dp_1", "rows_0", "rows_1"))
    placed = (P(DP_ROWS, None), P(DP_ROWS, None), P(DP_ROWS, None), P(DP_ROWS))
    return jax.shard_map(
        shards,
        mesh=finer,
        in_specs=placed,
        out_specs=(P(DP_ROWS, None), P(DP_ROWS, None)),
        check_vma=False,
    )
```

profile of v0, /device:TPU:1, one launch (start us, length us, event | category | flops | bytes accessed | tf_op | source)
XLA Modules:
  0.0 750.3 jit_solution(16251602117945407127)
XLA Ops:
  8.1 6.3 fusion.34
  14.4 0.1 copy.23
  14.5 0.2 reshape.200
  14.8 7.9 %while.15 = (s32[]{:T(128)}, f32[128]{0:T(128)S(1)}, s32[13,512]{1,0:T(8,128)S(1)}, s32[13,512]{1,0:T(8,128)S(1)}, s32[]{:T(128)}, /*index=5*/s32[]{:T(128)}) while((s32[]{:T(128)}, f32[128]{0:T(128)S(1)}, s32[13,512]{1,0:T(8,128)S(1)}, s32[13,512]{1,0:T(8,128)S(1)}, s32[]{:T(128)}, /*index=5*/s32[]{:T(128)}) %tuple.43), condition=%wide.region_4.5_spmd.clone, body=%wide.region_0.4_spmd.clone.sunk | while | flops 68223744 | bytes 26200 | solution.py:46
  14.9 0.1 fusion.46
  15.0 0.3 fusion.48
  15.5 0.1 fusion.46
  15.6 0.3 fusion.48
  16.1 0.1 fusion.46
  16.2 0.3 fusion.48
  16.7 0.1 fusion.46
  16.8 0.3 fusion.48
  17.3 0.1 fusion.46
  17.4 0.3 fusion.48
  17.9 0.1 fusion.46
  18.1 0.3 fusion.48
  18.5 0.1 fusion.46
  18.7 0.3 fusion.48
  19.1 0.1 fusion.46
  19.3 0.3 fusion.48
  19.7 0.1 fusion.46
  19.9 0.3 fusion.48
  20.4 0.1 fusion.46
  20.5 0.3 fusion.48
  21.0 0.1 fusion.46
  21.1 0.3 fusion.48
  21.6 0.1 fusion.46
  21.7 0.3 fusion.48
  22.2 0.1 fusion.46
  22.3 0.3 fusion.48
  22.8 31.1 %scatter_custom_fusion = s32[16384]{0:T(1024)S(1)} fusion(s32[6528]{0:T(1024)S(1)} %get-tuple-element.116, s32[6528]{0:T(1024)S(1)} %iota.16, s32[]{:T(128)} %constant.135.clone.1), kind=kCustom, calls=%fused_computation.68 | custom fusion | bytes 65540 | tf_op jit(solution)/shard_map/scatter | solution.py:66
  54.0 90.5 %gather_fusion = s32[16384]{0:T(1024)S(1)} fusion(s32[6529]{0:T(1024)S(1)} %pad_add_fusion.1, s32[16384]{0:T(1024)S(1)} %fusion.20), kind=kCustom, calls=%fused_computation | custom fusion | bytes 196608 | tf_op jit(solution)/shard_map/jit(_take)/gather | solution.py:69
  144.6 21.1 %all_to_all.25 = s32[128,1,128]{2,1,0:T(1,128)S(1)} all-to-all(s32[128,1,128]{2,1,0:T(1,128)S(1)} %bitcast.55), channel_id=1, replica_groups=mesh['dp_0'=4,'dp_1'=2,'rows_0'=4,'rows_1'=4] {'dp_0','dp_1','rows_0','r..., dimensions={0} | all-to-all | bytes 131072 | tf_op jit(solution)/shard_map/all_to_all | solution.py:77
  165.7 54.4 %gather_fusion.1 = f32[16384,128]{1,0:T(8,128)} fusion(f32[4096,128]{1,0:T(8,128)S(1)} %copy-done, s32[16384]{0:T(1024)S(1)} %fusion.16), kind=kCustom, calls=%fused_computation.1 | custom fusion | bytes 16842752 | tf_op jit(solution)/shard_map/jit(_take)/gather | solution.py:81
  220.1 7.5 %select_multiply_fusion = f32[128,128,128]{2,1,0:T(8,128)} fusion(f32[128,128,128]{2,1,0:T(8,128)} %bitcast.48, f32[128,128]{1,0:T(8,128)S(1)} %get-tuple-element.114, pred[128,128]{1,0:T(8,128)(4,1)S(1)} %get-tuple-element.113), kind=kLoop, calls=%fused_computation.22 | loop fusion | flops 4194304 | bytes 16859136 | tf_op jit(solution)/shard_map/mul | solution.py:83
  227.7 5.4 all-to-all-start.1
  233.1 0.2 slice.12
  233.5 102.0 %all-to-all-done.1 = f32[128,128,128]{2,1,0:T(8,128)} async-done(((f32[128,128,128]{2,1,0:T(8,128)}), f32[128,128,128]{2,1,0:T(8,128)}, u32[]{:S(2)}, u32[]{:S(2)}) %all-to-all-start.1) | async-done | bytes 8388640 | tf_op jit(solution)/shard_map/all_to_all | solution.py:82
  335.4 16.3 %gather_fusion.2 = f32[6528,128]{1,0:T(8,128)} fusion(f32[16384,128]{1,0:T(8,128)} %bitcast.6, s32[7168]{0:T(1024)S(1)} %pad_clamp_fusion), kind=kCustom, calls=%fused_computation.2 | custom fusion | bytes 6710784 | tf_op jit(solution)/shard_map/jit(_take)/gather | solution.py:89
  351.7 4.6 gather.23
  356.3 3.6 copy_select_fusion
  359.9 0.2 slice_reduce_fusion
  360.0 1.6 copy-done.1
  361.7 0.1 multiply_reduce_fusion
  361.9 3.8 reduce_sum.67
  365.7 1.0 fusion.14
  366.8 0.2 broadcast_in_dim.90
  367.0 2.1 pad_maximum_fusion
  369.1 4.6 reshape.204
  373.7 4.0 concatenate.19
  377.6 56.4 %gather_fusion.3 = f32[16384,128]{1,0:T(8,128)} fusion(f32[6529,128]{1,0:T(8,128)} %concatenate.19, s32[16384]{0:T(1024)S(1)} %fusion.20), kind=kCustom, calls=%fused_computation.3 | custom fusion | bytes 16842752 | tf_op jit(solution)/shard_map/jit(_take)/gather | solution.py:109
  434.0 9.9 %broadcast_select_fusion.1 = f32[128,128,128]{2,1,0:T(8,128)} fusion(f32[128,128,128]{2,1,0:T(8,128)} %bitcast.49, pred[128,128]{1,0:T(8,128)(4,1)S(1)} %bitcast.59), kind=kLoop, calls=%fused_computation.26 | loop fusion | flops 2097152 | bytes 16793600 | tf_op jit(solution)/shard_map/jit(_take)/select_n | solution.py:109
  443.9 10.2 %all-to-all-start.2 = ((f32[128,128,128]{2,1,0:T(8,128)}), f32[128,128,128]{2,1,0:T(8,128)}, u32[]{:S(2)}, u32[]{:S(2)}) async-start(f32[128,128,128]{2,1,0:T(8,128)} %broadcast_select_fusion.1), calls=%async_computation.2 | async-start | bytes 16777216 | tf_op jit(solution)/shard_map/all_to_all | solution.py:110
  454.2 0.9 fusion.18
  455.2 44.9 %all-reduce.7.cloned.1.call-done = f32[128,128]{1,0:T(8,128)} async-done(((f32[128,128]{1,0:T(8,128)}), f32[128,128]{1,0:T(8,128)}) %all-reduce.7.cloned.1.call-update) | async-done | bytes 65552 | tf_op jit(solution)/shard_map/psum | solution.py:23
  500.1 28.8 %all-reduce.9.cloned.1.call-done = f32[128,128]{1,0:T(8,128)} async-done(((f32[128,128]{1,0:T(8,128)}), f32[128,128]{1,0:T(8,128)}) %all-reduce.9.cloned.1.call-update) | async-done | bytes 65552 | tf_op jit(solution)/shard_map/psum | solution.py:23
  529.0 48.4 %all-reduce.11.cloned.1.call-done = f32[128,128]{1,0:T(8,128)} async-done(((f32[128,128]{1,0:T(8,128)}), f32[128,128]{1,0:T(8,128)}) %all-reduce.11.cloned.1.call-update) | async-done | bytes 65552 | tf_op jit(solution)/shard_map/psum | solution.py:23
  577.4 0.1 compare_select_fusion
  577.5 43.1 %all-reduce.13.cloned.1.call-done = f32[128,128]{1,0:T(8,128)} async-done(((f32[128,128]{1,0:T(8,128)}), f32[128,128]{1,0:T(8,128)}) %all-reduce.13.cloned.1.call-update) | async-done | bytes 65552 | tf_op jit(solution)/shard_map/psum | solution.py:23
  620.6 4.1 fusion.12
  624.7 2.9 copy.27
  627.5 7.9 %broadcast_multiply_fusion = f32[128,128,128]{2,1,0:T(8,128)} fusion(f32[128,128,128]{2,1,0:T(8,128)} %all-to-all-done.2, f32[128,128]{1,0:T(8,128)S(1)} %get-tuple-element.114), kind=kLoop, calls=%fused_computation.25 | loop fusion | flops 2097152 | bytes 16842752 | tf_op jit(solution)/shard_map/mul | solution.py:115
  635.4 102.6 %scatter_fusion = f32[4096,128]{1,0:T(8,128)} fusion(f32[4096,128]{1,0:T(8,128)} %copy.27, s32[16384]{0:T(1024)S(1)} %bitcast.53, f32[16384,128]{1,0:T(8,128)} %bitcast.47), kind=kCustom, calls=%fused_computation.5 | custom fusion | flops 2097152 | bytes 25231360 | tf_op jit(solution)/shard_map/scatter-add | solution.py:126
  738.0 4.6 multiply_subtract_fusion
  (103 shorter events, 2.0 us)
Async XLA Ops:
  8.0 6.4 copy-start.3
  8.0 6.4 copy-start.2
  8.0 353.9 %all-gather.3.cloned.1.call-start = ((), (), s32[]{:S(2)}) async-start(), calls=%async_computation.7 | async-start | bytes 8454144 | tf_op jit(solution)/shard_map/all_gather | solution.py:17
  54.0 111.7 %copy-start = (f32[4096,128]{1,0:T(8,128)S(1)}, f32[4096,128]{1,0:T(8,128)}, u32[]{:S(2)}) copy-start(f32[4096,128]{1,0:T(8,128)} %param.6) | copy-start | bytes 6291460
  227.7 107.8 %all-to-all-start.1 = ((f32[128,128,128]{2,1,0:T(8,128)}), f32[128,128,128]{2,1,0:T(8,128)}, u32[]{:S(2)}, u32[]{:S(2)}) async-start(f32[128,128,128]{2,1,0:T(8,128)} %select_multiply_fusion), calls=%async_computation.1 | async-start | bytes 16777216 | tf_op jit(solution)/shard_map/all_to_all | solution.py:82
  359.9 1.8 copy-start.1
  443.9 183.6 %all-to-all-start.2 = ((f32[128,128,128]{2,1,0:T(8,128)}), f32[128,128,128]{2,1,0:T(8,128)}, u32[]{:S(2)}, u32[]{:S(2)}) async-start(f32[128,128,128]{2,1,0:T(8,128)} %broadcast_select_fusion.1), calls=%async_computation.2 | async-start | bytes 16777216 | tf_op jit(solution)/shard_map/all_to_all | solution.py:110
  454.1 45.9 %all-reduce.7.cloned.1.call-start = ((), (), s32[]{:S(2)}) async-start(), calls=%async_computation.3 | async-start | bytes 131072 | tf_op jit(solution)/shard_map/psum | solution.py:23
  455.1 73.8 %all-reduce.9.cloned.1.call-start = ((), (), s32[]{:S(2)}) async-start(), calls=%async_computation.4 | async-start | bytes 131072 | tf_op jit(solution)/shard_map/psum | solution.py:23
  500.1 77.3 %all-reduce.11.cloned.1.call-start = ((), (), s32[]{:S(2)}) async-start(), calls=%async_computation.5 | async-start | bytes 131072 | tf_op jit(solution)/shard_map/psum | solution.py:23
  528.9 91.7 %all-reduce.13.cloned.1.call-start = ((), (), s32[]{:S(2)}) async-start(), calls=%async_computation.6 | async-start | bytes 131072 | tf_op jit(solution)/shard_map/psum | solution.py:23
Sparse Core Ops, SparseCore 0:
  14.5 73.8 all-gather.2
Sparse Core Ops, SparseCore 1:
  457.5 42.5 all-reduce.6
  502.4 26.4 all-reduce.8
  531.2 46.1 all-reduce.10
  579.7 40.8 all-reduce.12
where the time goes:
time: 753 us; the launch traced here: 750 us
  local copies, waits for them, and re-layouts  268 us (36%)
  waiting for transfers between devices  267 us (35%)
  other arithmetic  145 us (19%)
  blocking collectives  21.1 us (3%)
  matrix products  16.4 us (2%)
  between operations  16 us (2%)
  starting transfers between devices  15.8 us (2%)
    psum x4, waiting for transfers between devices, one_axis_at_a_time(): array = lax.psum(array, axis)  165 us
    scatter-add x1, other arithmetic, shards(): row_grad = row_grad.at[target_rows].add(masked_grad)  103 us
    all_to_all x1, waiting for transfers between devices, shards(): lax.all_to_all(picked * present[..., None].astype(jnp.float32), DP_ROWS,...  102 us
    gather x1, local copies, waits for them, and re-layouts, shards(): wanted = jnp.take(local_pad, inverse, axis=0)  90.5 us
    gather x1, local copies, waits for them, and re-layouts, shards(): outgoing = jnp.take(grad_pad, inverse, axis=0)  56.4 us
    gather x1, local copies, waits for them, and re-layouts, shards(): picked = jnp.take(item_table, jnp.where(present, asked, 0), axis=0)  54.4 us
    scatter x1, local copies, waits for them, and re-layouts, shards(): inverse = jnp.full((devices * capacity,), request_count, jnp.int32).at[fl...  31.1 us
    all_to_all x1, blocking collectives, shards(): lax.all_to_all(wanted.reshape(devices, capacity), DP_ROWS, split_axis=0,...  21.1 us
  transfers between devices with their start and end apart: 7, of which 5 were waited for; matrix products, arithmetic and copies ran while one was open for 30% of the time, Pallas kernels for 0%

commit v1 on v0

v1 whole, which is shorter than its diff:
```python
import functools

import jax
import jax.numpy as jnp
from jax import lax
from jax.experimental import pallas as pl
from jax.experimental.pallas import tpu as pltpu
from jax.sharding import Mesh
from jax.sharding import PartitionSpec as P

DP_ROWS = ("dp_0", "dp_1", "rows_0", "rows_1")

penalty_weight = 10.0
step_size = 0.05

LANES = 128
BLOCK_ROWS = 264
CHAINS = 4

bf16 = jnp.bfloat16
f32 = jnp.float32
i32 = jnp.int32


def iota2(shape, dim):
    return lax.broadcasted_iota(i32, shape, dim)


def split2(x):
    hi = x.astype(bf16)
    lo = (x - hi.astype(f32)).astype(bf16)
    return hi, lo


def dot_f32(a, b):
    return jnp.dot(a, b, preferred_element_type=f32)


def dot_split(a, b):
    ah, al = split2(a)
    bh, bl = split2(b)
    return dot_f32(ah, bh) + (dot_f32(ah, bl) + dot_f32(al, bh))


def dot_split_t(a, b):
    dims = (((0,), (0,)), ((), ()))
    ah, al = split2(a)
    bh, bl = split2(b)
    dg = functools.partial(lax.dot_general, dimension_numbers=dims, preferred_element_type=f32)
    return dg(ah, bh) + (dg(ah, bl) + dg(al, bh))


def list_kernel(ids_c_ref, ids_r_ref, out_ref, code_ref, *, slots, rows_dev):
    sq = (LANES, LANES)
    lane = iota2(sq, 1)
    sub = iota2(sq, 0)
    lane_f = lane.astype(f32)
    one = jnp.ones(sq, f32)
    zero = jnp.zeros(sq, f32)
    lower = jnp.concatenate([jnp.where(sub > lane, one, zero), one], axis=0).astype(bf16)
    ones = one.astype(bf16)
    users = iota2((1, LANES), 1)
    carry = jnp.zeros(sq, f32)
    acc = jnp.zeros((3 * LANES, LANES), f32)
    for h in range(slots):
        owner_c = ids_c_ref[:, h : h + 1] // rows_dev
        member = owner_c == lane
        counts = dot_f32(lower, jnp.where(member, one, zero).astype(bf16))
        mine = jnp.where(member, counts[:LANES] + carry, zero).astype(bf16)
        rank = dot_f32(mine, ones)
        place = jnp.where(rank == lane_f, one, zero).astype(bf16)
        ids = ids_r_ref[h : h + 1, :]
        local = ids % rows_dev
        at_owner = ids // rows_dev == sub
        high = (local // 64 + 1).astype(f32)
        low = (local % 64).astype(f32)
        code = (users + (LANES if h == slots - 1 else 0)).astype(f32)
        vals = jnp.concatenate(
            [
                jnp.where(at_owner, jnp.broadcast_to(high, sq), zero),
                jnp.where(at_owner, jnp.broadcast_to(low, sq), zero),
                jnp.where(at_owner, jnp.broadcast_to(code, sq), zero),
            ],
            axis=0,
        ).astype(bf16)
        acc = acc + dot_f32(vals, place)
        carry = carry + counts[LANES:]
    high = acc[:LANES].astype(i32)
    low = acc[LANES : 2 * LANES].astype(i32)
    code = acc[2 * LANES :].astype(i32)
    present = high > 0
    out_ref[:, 0, :] = jnp.where(present, (high - 1) * 64 + low, rows_dev)
    code = jnp.where(present, code, -1)
    out_ref[:, 1, :] = code
    code_ref[...] = code


def request_lists(ids_c, ids_r, rows_dev, slots):
    return pl.pallas_call(
        functools.partial(list_kernel, slots=slots, rows_dev=rows_dev),
        out_shape=(
            jax.ShapeDtypeStruct((LANES, 2, LANES), i32),
            jax.ShapeDtypeStruct((LANES, LANES), i32),
        ),
        name="request_lists",
    )(ids_c, ids_r)


def pick_kernel(rows_ref, table_ref, out_ref, *, per_step):
    g = pl.program_id(0)

    def body(j, carry):
        for k in range(16):
            i = j * 16 + k
            row = rows_ref[g * (per_step // LANES) + j // 8, (j % 8) * 16 + k]
            out_ref[i] = table_ref[row]
        return carry

    lax.fori_loop(0, per_step // 16, body, 0)


def pick_rows(rows_idx, table, devices):
    rows_dev, width = table.shape
    total = devices * LANES
    per_step = 1024
    return pl.pallas_call(
        functools.partial(pick_kernel, per_step=per_step),
        grid_spec=pltpu.PrefetchScalarGridSpec(
            num_scalar_prefetch=1,
            grid=(total // per_step,),
            in_specs=[pl.BlockSpec((rows_dev, 1, width), lambda g, r: (0, 0, 0))],
            out_specs=pl.BlockSpec((per_step, 1, width), lambda g, r: (g, 0, 0)),
        ),
        out_shape=jax.ShapeDtypeStruct((total, 1, width), f32),
        compiler_params=pltpu.CompilerParams(vmem_limit_bytes=32 * 2**20),
        name="pick_rows",
    )(rows_idx, table.reshape(rows_dev, 1, width))


def user_kernel(code_ref, rows_ref, gram_ref, out_ref, acc_ref, *, hist_len, coef, owners):
    g = pl.program_id(0)

    @pl.when(g == 0)
    def _():
        acc_ref[...] = jnp.zeros_like(acc_ref)

    sub = iota2((2 * LANES, LANES), 0)
    one = jnp.ones((2 * LANES, LANES), f32)
    zero = jnp.zeros((2 * LANES, LANES), f32)
    total = acc_ref[...]
    for o in range(owners):
        weight = jnp.where(code_ref[o : o + 1, :] == sub, one, zero).astype(bf16)
        total = total + dot_f32(weight, jnp.concatenate(split2(rows_ref[o]), axis=1))
    acc_ref[...] = total

    @pl.when(g == pl.num_programs(0) - 1)
    def _():
        sums = acc_ref[:, :LANES] + acc_ref[:, LANES:]
        user = sums[:LANES] / hist_len
        positive = sums[LANES:]
        gap = jnp.sum(user * positive, axis=1, keepdims=True) - 1.0
        grad = 2.0 * gap * positive + 2.0 * coef * dot_split(user, gram_ref[...])
        out_ref[:LANES, :] = grad / hist_len
        out_ref[LANES : 2 * LANES, :] = user
        sq = (LANES, LANES)
        gap_row = jnp.sum(
            jnp.where(iota2(sq, 0) == iota2(sq, 1), jnp.broadcast_to(gap, sq), 0.0),
            axis=0,
            keepdims=True,
        )
        out_ref[2 * LANES :, :] = jnp.broadcast_to(gap_row, (8, LANES))


def user_block(codes, fetched, item_total, hist_len, coef):
    devices, capacity, width = fetched.shape
    owners = 8
    return pl.pallas_call(
        functools.partial(user_kernel, hist_len=hist_len, coef=coef, owners=owners),
        grid=(devices // owners,),
        in_specs=[
            pl.BlockSpec((owners, capacity), lambda g: (g, 0)),
            pl.BlockSpec((owners, capacity, width), lambda g: (g, 0, 0)),
            pl.BlockSpec((width, width), lambda g: (0, 0)),
        ],
        out_specs=pl.BlockSpec((BLOCK_ROWS, width), lambda g: (0, 0)),
        out_shape=jax.ShapeDtypeStruct((BLOCK_ROWS, width), f32),
        scratch_shapes=[pltpu.VMEM((2 * LANES, 2 * LANES), f32)],
        name="user_block",
    )(codes, fetched, item_total)


def update_kernel(
    idx_ref, blocks_ref, table_ref, state_ref, new_table_ref, new_state_ref,
    stage_ref, gram_ref, *acc_refs, sources, coef,
):
    g = pl.program_id(0)
    rows_dev = table_ref.shape[0]
    sq = (LANES, LANES)

    @pl.when(g == 0)
    def _():
        gram_ref[...] = jnp.zeros_like(gram_ref)
        for acc in acc_refs:
            acc[...] = jnp.zeros_like(acc)

    diagonal = iota2(sq, 0) == iota2(sq, 1)
    gram = gram_ref[...]
    for s in range(sources):
        user = blocks_ref[s, LANES : 2 * LANES, :]
        gap_row = blocks_ref[s, 2 * LANES : 2 * LANES + 1, :]
        gap = jnp.sum(
            jnp.where(diagonal, jnp.broadcast_to(gap_row, sq), 0.0), axis=1, keepdims=True
        )
        stage_ref[2 * LANES * s : 2 * LANES * s + LANES, :] = blocks_ref[s, :LANES, :]
        stage_ref[2 * LANES * s + LANES : 2 * LANES * (s + 1), :] = 2.0 * gap * user
        gram = gram + dot_split_t(user, user)
    gram_ref[...] = gram

    def body(j, carry):
        for k in range(8):
            packed = idx_ref[g * sources + j // 16, (j % 16) * 8 + k]
            row = packed // 2048
            src = packed % 2048
            acc = acc_refs[k % CHAINS]
            acc[pl.ds(row, 1), :] += stage_ref[pl.ds(src, 1), :]
        return carry

    lax.fori_loop(0, sources * LANES // 8, body, 0)

    @pl.when(g == pl.num_programs(0) - 1)
    def _():
        step = 512

        def finish(i, carry):
            at = pl.ds(pl.multiple_of(i * step, step), step)
            table = table_ref[at, :]
            grad = 2.0 * coef * dot_split(table, gram_ref[...])
            for acc in acc_refs:
                grad = grad + acc[at, :]
            new_state = state_ref[at, :] + grad * grad
            new_state_ref[at, :] = new_state
            new_table_ref[at, :] = table - step_size * grad / jnp.sqrt(new_state)
            return carry

        lax.fori_loop(0, rows_dev // step, finish, 0)


def update_rows(packed, blocks, table, state, coef):
    rows_dev, width = table.shape
    devices = packed.shape[0]
    sources = 8
    whole = pl.BlockSpec((rows_dev, width), lambda g, r: (0, 0))
    return pl.pallas_call(
        functools.partial(update_kernel, sources=sources, coef=coef),
        grid_spec=pltpu.PrefetchScalarGridSpec(
            num_scalar_prefetch=1,
            grid=(devices // sources,),
            in_specs=[
                pl.BlockSpec((sources, BLOCK_ROWS, width), lambda g, r: (g, 0, 0)),
                whole,
                whole,
            ],
            out_specs=[whole, whole],
            scratch_shapes=[
                pltpu.VMEM((sources * 2 * LANES, width), f32),
                pltpu.VMEM((width, width), f32),
            ]
            + [pltpu.VMEM((rows_dev + 8, width), f32)] * CHAINS,
        ),
        out_shape=(
            jax.ShapeDtypeStruct((rows_dev, width), f32),
            jax.ShapeDtypeStruct((rows_dev, width), f32),
        ),
        compiler_params=pltpu.CompilerParams(vmem_limit_bytes=48 * 2**20),
        name="update_rows",
    )(packed, blocks, table, state)


def shards(item_table, adagrad_state, history_ids, positive_ids):
    rows_dev, width = item_table.shape
    users_dev, hist_len = history_ids.shape
    devices = lax.axis_size(DP_ROWS)
    coef = penalty_weight / (rows_dev * devices)
    item_gram = jnp.dot(
        item_table.T,
        item_table,
        precision=lax.Precision.HIGHEST,
        preferred_element_type=f32,
    )
    item_total = lax.psum(item_gram, DP_ROWS)
    ids = jnp.concatenate([history_ids, positive_ids[:, None]], axis=1)
    lists, codes = request_lists(ids, ids.T, rows_dev, hist_len + 1)
    asked = lax.all_to_all(lists, DP_ROWS, split_axis=0, concat_axis=0, tiled=True)
    rows = asked[:, 0, :]
    source = jnp.maximum(asked[:, 1, :], 0)
    place = (jnp.arange(devices, dtype=i32) % 8 * (2 * LANES))[:, None]
    packed = rows * 2048 + place + source
    picked = pick_rows(jnp.where(rows < rows_dev, rows, 0), item_table, devices)
    fetched = lax.all_to_all(
        picked.reshape(devices, LANES, width), DP_ROWS, split_axis=0, concat_axis=0, tiled=True
    )
    block = user_block(codes, fetched, item_total, hist_len, coef)
    blocks = lax.all_gather(block, DP_ROWS)
    return update_rows(packed, blocks, item_table, adagrad_state, coef)


def solution(mesh):
    finer = Mesh(mesh.devices.reshape(4, 2, 4, 4), DP_ROWS)
    rows = P(DP_ROWS, None)
    return jax.shard_map(
        shards,
        mesh=finer,
        in_specs=(rows, rows, rows, P(DP_ROWS)),
        out_specs=(rows, rows),
        check_vma=False,
    )
```

time: 753 us -> 569 us (0.76)
  local copies, waits for them, and re-layouts: 268 us -> 7.25 us
  Pallas kernels: 0 us -> 230 us
  other arithmetic: 145 us -> 2.25 us
  waiting for transfers between devices: 267 us -> 294 us
  blocking collectives: 21.1 us -> 0 us
  matrix products: 16.4 us -> 4.09 us
    pallas_call x0 -> x4, Pallas kernels: none -> 230 us  [the longest x1 160 us: update_rows(): pl.pallas_call(functools.partial(update_kernel, sources=sources, coef=coe...]
    gather x5 -> x0, local copies, waits for them, and re-layouts: 222 us -> none  [the longest x1 90.5 us: shards(): wanted = jnp.take(local_pad, inverse, axis=0)]
    scatter-add x1 -> x0, other arithmetic: 103 us -> none  [shards(): row_grad = row_grad.at[target_rows].add(masked_grad)]
    all_to_all x2, waiting for transfers between devices: 102 us -> 10.2 us  [the longest x1 10.2 us: shards(): lax.all_to_all(lists, DP_ROWS, split_axis=0, concat_axis=0, tiled=True)]
    all_gather x1, waiting for transfers between devices: 0.02 us -> 78.4 us  [shards(): blocks = lax.all_gather(block, DP_ROWS)]
    psum x4 -> x1, waiting for transfers between devices: 165 us -> 205 us  [shards(): item_total = lax.psum(item_gram, DP_ROWS)]
    scatter x1 -> x0, local copies, waits for them, and re-layouts: 31.1 us -> none  [shards(): inverse = jnp.full((devices * capacity,), request_count, jnp.int32).at[fl...]
    all_to_all x1 -> x0, blocking collectives: 21.1 us -> none  [shards(): lax.all_to_all(wanted.reshape(devices, capacity), DP_ROWS, split_axis=0,...]
  transfers between devices with their start and end apart: 7 -> 4, of which waited for: 5 -> 3; matrix products, arithmetic and copies ran while one was open for 30% -> 1% of each run, Pallas kernels for 0% -> 0%
where the time goes in v1:
time: 569 us; the launch traced here: 568 us
  waiting for transfers between devices  294 us (52%)
  Pallas kernels  230 us (40%)
  starting transfers between devices  16.8 us (3%)
  between operations  14.1 us (2%)
  local copies, waits for them, and re-layouts  7.25 us (1%)
    psum x1, waiting for transfers between devices, shards(): item_total = lax.psum(item_gram, DP_ROWS)  205 us
    pallas_call x1, Pallas kernels, update_rows(): pl.pallas_call(functools.partial(update_kernel, sources=sources, coef=coe...  160 us
    all_gather x1, waiting for transfers between devices, shards(): blocks = lax.all_gather(block, DP_ROWS)  78.4 us
    pallas_call x1, Pallas kernels, pick_rows(): pl.pallas_call(functools.partial(pick_kernel, per_step=per_step), grid_sp...  47.1 us
    pallas_call x1, Pallas kernels, user_block(): pl.pallas_call(functools.partial(user_kernel, hist_len=hist_len, coef=coe...  13.4 us
    all_to_all x1, starting transfers between devices, shards(): lax.all_to_all(lists, DP_ROWS, split_axis=0, concat_axis=0, tiled=True)  11.5 us
  transfers between devices with their start and end apart: 4, of which 3 were waited for; matrix products, arithmetic and copies ran while one was open for 1% of the time, Pallas kernels for 0%

profile of v1, /device:TPU:1, one launch (start us, length us, event | category | flops | bytes accessed | tf_op | source)
XLA Modules:
  0.0 568.0 jit_solution(5491056986695211095)
XLA Ops:
  7.2 1.4 fusion.5.ids_r_ref
  8.5 0.8 pad_add_fusion
  9.3 0.7 copy.8.ids_c_ref
  10.1 9.3 %request_lists.1 = (s32[128,2,128]{2,1,0:T(2,128)}, s32[128,128]{1,0:T(8,128)}) custom-call(s32[128,51]{1,0:T(8,128)} %copy.8.ids_c_ref, s32[51,128]{1,0:T(8,128)} %fusion.5.ids_r_ref), custom_call_target="tpu_custom_call" | custom-call | tf_op jit(solution)/shard_map/request_lists/pallas_call | solution.py:99
  19.4 11.5 %all-to-all-start = ((s32[128,2,128]{2,1,0:T(2,128)}), s32[128,2,128]{2,1,0:T(2,128)S(1)}, u32[]{:S(2)}, u32[]{:S(2)}) async-start(s32[128,2,128]{2,1,0:T(2,128)} %get-tuple-element.4), calls=%async_computation | async-start | bytes 262144 | tf_op jit(solution)/shard_map/all_to_all | solution.py:293
  30.9 10.2 %all-to-all-done = s32[128,2,128]{2,1,0:T(2,128)S(1)} async-done(((s32[128,2,128]{2,1,0:T(2,128)}), s32[128,2,128]{2,1,0:T(2,128)S(1)}, u32[]{:S(2)}, u32[]{:S(2)}) %all-to-all-start) | async-done | bytes 131104 | tf_op jit(solution)/shard_map/all_to_all | solution.py:293
  41.1 0.1 fusion.1
  41.2 0.1 compare_select_fusion
  41.3 0.0 copy-start.1
  41.3 1.6 copy-done.1
  42.9 47.1 %pick_rows.1 = f32[16384,1,128]{2,1,0:T(1,128)S(1)} custom-call(s32[128,128]{1,0:T(8,128)S(1)} %get-tuple-element.8.rows_ref, f32[4096,1,128]{2,1,0:T(1,128)S(1)} %bitcast.15), custom_call_target="tpu_custom_call" | custom-call | tf_op jit(solution)/shard_map/pick_rows/pallas_call | solution.py:126
  89.9 0.0 copy-start
  89.9 3.2 copy-done
  93.2 0.0 copy-start.2
  93.2 5.2 all-to-all-start.1
  98.4 0.0 all-reduce.2.cloned.1.call-start
  98.5 0.0 copy-done.2
  98.5 4.1 fusion.2
  102.6 0.0 all-reduce.2.cloned.1.call-update
  102.6 0.0 all-gather.3.cloned.1.call-start
  102.6 205.1 %all-reduce.2.cloned.1.call-done.gram_ref = f32[128,128]{1,0:T(8,128)} async-done(((f32[128,128]{1,0:T(8,128)}), f32[128,128]{1,0:T(8,128)}) %all-reduce.2.cloned.1.call-update) | async-done | bytes 65552 | tf_op jit(solution)/shard_map/psum | solution.py:290
  307.8 0.0 all-to-all-done.1.rows_ref
  307.8 13.4 %user_block.1 = f32[264,128]{1,0:T(8,128)} custom-call(s32[128,128]{1,0:T(8,128)} %get-tuple-element.5.code_ref, f32[128,128,128]{2,1,0:T(8,128)} %all-to-all-done.1.rows_ref, f32[128,128]{1,0:T(8,128)} %all-reduce.2.cloned.1.call-done.gram_ref), custom_call_target="tpu_custom_call" | custom-call | tf_op jit(solution)/shard_map/user_block/pallas_call | solution.py:177
  321.2 0.0 all-gather.3.cloned.1.call-update
  321.2 78.4 %all-gather.3.cloned.1.call-done = f32[33792,128]{1,0:T(8,128)} async-done(((f32[264,128]{1,0:T(8,128)}), f32[33792,128]{1,0:T(8,128)}) %all-gather.3.cloned.1.call-update) | async-done | bytes 17301520 | tf_op jit(solution)/shard_map/all_gather | solution.py:303
  399.6 0.0 copy-start.3
  399.6 1.6 copy-done.3
  401.2 160.0 %update_rows.1 = (f32[4096,128]{1,0:T(8,128)}, f32[4096,128]{1,0:T(8,128)}) custom-call(s32[128,128]{1,0:T(8,128)S(1)} %get-tuple-element.9.idx_ref, f32[128,264,128]{2,1,0:T(8,128)} %bitcast.16, f32[4096,128]{1,0:T(8,128)S(1)} %copy-done.2, f32[4096,128]{1,0:T(8,128)S(1)} %copy-done.3), custom_call_target="tpu_custom_call" | custom-call | tf_op jit(solution)/shard_map/update_rows/pallas_call | solution.py:253
  (1 shorter events, 0.0 us)
Async XLA Ops:
  19.4 21.7 %all-to-all-start = ((s32[128,2,128]{2,1,0:T(2,128)}), s32[128,2,128]{2,1,0:T(2,128)S(1)}, u32[]{:S(2)}, u32[]{:S(2)}) async-start(s32[128,2,128]{2,1,0:T(2,128)} %get-tuple-element.4), calls=%async_computation | async-start | bytes 262144 | tf_op jit(solution)/shard_map/all_to_all | solution.py:293
  41.3 1.6 copy-start.1
  89.9 3.2 copy-start
  93.2 5.3 copy-start.2
  93.2 214.6 %all-to-all-start.1 = ((f32[128,128,128]{2,1,0:T(8,128)}), f32[128,128,128]{2,1,0:T(8,128)}, u32[]{:S(2)}, u32[]{:S(2)}) async-start(f32[128,128,128]{2,1,0:T(8,128)} %bitcast.14), calls=%async_computation.1 | async-start | bytes 16777216 | tf_op jit(solution)/shard_map/all_to_all | solution.py:299
  98.4 209.3 %all-reduce.2.cloned.1.call-start = ((), (), s32[]{:S(2)}) async-start(), calls=%async_computation.2 | async-start | bytes 131072 | tf_op jit(solution)/shard_map/psum | solution.py:290
  102.6 297.0 %all-gather.3.cloned.1.call-start = ((), (), s32[]{:S(2)}) async-start(), calls=%async_computation.3 | async-start | bytes 17436672 | tf_op jit(solution)/shard_map/all_gather | solution.py:303
  399.6 1.6 copy-start.3
Sparse Core Ops, SparseCore 0:
  104.6 203.1 all-reduce.1
  321.3 78.2 all-gather.2

commit v2 on v1

v2 whole, which is shorter than its diff:
```python
import functools

import jax
import jax.numpy as jnp
from jax import lax
from jax.experimental import pallas as pl
from jax.experimental.pallas import tpu as pltpu
from jax.sharding import Mesh
from jax.sharding import PartitionSpec as P

DP_ROWS = ("dp_0", "dp_1", "rows_0", "rows_1")

penalty_weight = 10.0
step_size = 0.05

LANES = 128
BLOCK_ROWS = 264
CHAINS = 8
ROW_BLOCK = 136

bf16 = jnp.bfloat16
f32 = jnp.float32
i32 = jnp.int32


def iota2(shape, dim):
    return lax.broadcasted_iota(i32, shape, dim)


def split2(x):
    hi = x.astype(bf16)
    lo = (x - hi.astype(f32)).astype(bf16)
    return hi, lo


def dot_f32(a, b):
    return jnp.dot(a, b, preferred_element_type=f32)


def dot_split(a, b):
    ah, al = split2(a)
    bh, bl = split2(b)
    return dot_f32(ah, bh) + (dot_f32(ah, bl) + dot_f32(al, bh))


def half_gram(a):
    hi, lo = split2(a)
    return lax.dot_general(
        hi,
        jnp.concatenate([hi, lo], axis=1),
        (((0,), (0,)), ((), ())),
        preferred_element_type=f32,
    )


def whole_gram(halves):
    cross = halves[:, LANES:]
    return halves[:, :LANES] + (cross + cross.T)


def list_kernel(ids_c_ref, ids_r_ref, gram_ref, out_ref, code_ref, *, slots, rows_dev):
    sq = (LANES, LANES)
    lane = iota2(sq, 1)
    sub = iota2(sq, 0)
    lane_f = lane.astype(f32)
    one = jnp.ones(sq, f32)
    zero = jnp.zeros(sq, f32)
    lower = jnp.concatenate([jnp.where(sub > lane, one, zero), one], axis=0).astype(bf16)
    ones = one.astype(bf16)
    users = iota2((1, LANES), 1)
    carry = jnp.zeros(sq, f32)
    acc = jnp.zeros((3 * LANES, LANES), f32)
    for h in range(slots):
        owner_c = ids_c_ref[:, h : h + 1] // rows_dev
        member = owner_c == lane
        counts = dot_f32(lower, jnp.where(member, one, zero).astype(bf16))
        mine = jnp.where(member, counts[:LANES] + carry, zero).astype(bf16)
        rank = dot_f32(mine, ones)
        place = jnp.where(rank == lane_f, one, zero).astype(bf16)
        ids = ids_r_ref[h : h + 1, :]
        local = ids % rows_dev
        at_owner = ids // rows_dev == sub
        high = (local // 64 + 1).astype(f32)
        low = (local % 64).astype(f32)
        code = (users + (LANES if h == slots - 1 else 0)).astype(f32)
        vals = jnp.concatenate(
            [
                jnp.where(at_owner, jnp.broadcast_to(high, sq), zero),
                jnp.where(at_owner, jnp.broadcast_to(low, sq), zero),
                jnp.where(at_owner, jnp.broadcast_to(code, sq), zero),
            ],
            axis=0,
        ).astype(bf16)
        acc = acc + dot_f32(vals, place)
        carry = carry + counts[LANES:]
    high = acc[:LANES].astype(i32)
    low = acc[LANES : 2 * LANES].astype(i32)
    code = acc[2 * LANES :].astype(i32)
    present = high > 0
    code = jnp.where(present, code, -1)
    out_ref[:, 0, :] = jnp.where(present, (high - 1) * 64 + low, rows_dev).astype(f32)
    out_ref[:, 1, :] = code.astype(f32)
    out_ref[:, 2, :] = gram_ref[...]
    out_ref[:, 3, :] = zero
    code_ref[...] = code


def request_lists(ids_c, ids_r, gram, rows_dev, slots):
    return pl.pallas_call(
        functools.partial(list_kernel, slots=slots, rows_dev=rows_dev),
        out_shape=(
            jax.ShapeDtypeStruct((LANES, 4, LANES), f32),
            jax.ShapeDtypeStruct((LANES, LANES), i32),
        ),
        name="request_lists",
    )(ids_c, ids_r, gram)


def pick_kernel(rows_ref, table_ref, total_ref, out_ref, *, dests):
    base = pl.program_id(0) * (dests * LANES)
    unroll = 64

    for d in range(dests):

        def body(j, carry, d=d):
            at = j * unroll
            picked = [
                table_ref[rows_ref[base + (d * LANES + at + k)]] for k in range(unroll)
            ]
            for k in range(unroll):
                out_ref[d * ROW_BLOCK + at + k] = picked[k]
            return carry

        lax.fori_loop(0, LANES // unroll, body, 0)
        for k in range(LANES, ROW_BLOCK):
            out_ref[d * ROW_BLOCK + k] = total_ref[0]


def pick_rows(rows_idx, table, total_row, devices):
    rows_dev, width = table.shape
    dests = 8
    return pl.pallas_call(
        functools.partial(pick_kernel, dests=dests),
        grid_spec=pltpu.PrefetchScalarGridSpec(
            num_scalar_prefetch=1,
            grid=(devices // dests,),
            in_specs=[
                pl.BlockSpec((rows_dev, 1, width), lambda g, r: (0, 0, 0)),
                pl.BlockSpec((1, 1, width), lambda g, r: (0, 0, 0)),
            ],
            out_specs=pl.BlockSpec((dests * ROW_BLOCK, 1, width), lambda g, r: (g, 0, 0)),
        ),
        out_shape=jax.ShapeDtypeStruct((devices * ROW_BLOCK, 1, width), f32),
        compiler_params=pltpu.CompilerParams(vmem_limit_bytes=32 * 2**20),
        name="pick_rows",
    )(rows_idx, table.reshape(rows_dev, 1, width), total_row.reshape(1, 1, width))


def user_kernel(code_ref, rows_ref, out_ref, acc_ref, gram_ref, *, hist_len, coef, owners):
    g = pl.program_id(0)

    @pl.when(g == 0)
    def _():
        acc_ref[...] = jnp.zeros_like(acc_ref)

    sub = iota2((2 * LANES, LANES), 0)
    one = jnp.ones((2 * LANES, LANES), f32)
    zero = jnp.zeros((2 * LANES, LANES), f32)
    total = acc_ref[...]
    for o in range(owners):
        weight = jnp.where(code_ref[o : o + 1, :] == sub, one, zero).astype(bf16)
        rows = rows_ref[o, :LANES, :]
        total = total + dot_f32(weight, jnp.concatenate(split2(rows), axis=1))
        gram_ref[pl.ds(g * owners + o, 1), :] = rows_ref[o, LANES : LANES + 1, :]
    acc_ref[...] = total

    @pl.when(g == pl.num_programs(0) - 1)
    def _():
        sums = acc_ref[:, :LANES] + acc_ref[:, LANES:]
        user = sums[:LANES] / hist_len
        positive = sums[LANES:]
        gap = jnp.sum(user * positive, axis=1, keepdims=True) - 1.0
        grad = 2.0 * gap * positive + 2.0 * coef * dot_split(user, gram_ref[...])
        out_ref[:LANES, :] = grad / hist_len
        out_ref[LANES : 2 * LANES, :] = user
        sq = (LANES, LANES)
        gap_row = jnp.sum(
            jnp.where(iota2(sq, 0) == iota2(sq, 1), jnp.broadcast_to(gap, sq), 0.0),
            axis=0,
            keepdims=True,
        )
        out_ref[2 * LANES :, :] = jnp.broadcast_to(gap_row, (8, LANES))


def user_block(codes, fetched, hist_len, coef):
    devices, _, width = fetched.shape
    owners = 8
    return pl.pallas_call(
        functools.partial(user_kernel, hist_len=hist_len, coef=coef, owners=owners),
        grid=(devices // owners,),
        in_specs=[
            pl.BlockSpec((owners, LANES), lambda g: (g, 0)),
            pl.BlockSpec((owners, ROW_BLOCK, width), lambda g: (g, 0, 0)),
        ],
        out_specs=pl.BlockSpec((BLOCK_ROWS, width), lambda g: (0, 0)),
        out_shape=jax.ShapeDtypeStruct((BLOCK_ROWS, width), f32),
        scratch_shapes=[pltpu.VMEM((2 * LANES, 2 * LANES), f32), pltpu.VMEM((width, width), f32)],
        name="user_block",
    )(codes, fetched)


def update_kernel(
    row_idx_ref, src_idx_ref, blocks_ref, table_ref, state_ref, new_table_ref, new_state_ref,
    stage_ref, gram_ref, *acc_refs, sources, coef,
):
    g = pl.program_id(0)
    rows_dev = table_ref.shape[0]
    sq = (LANES, LANES)

    @pl.when(g == 0)
    def _():
        gram_ref[...] = jnp.zeros_like(gram_ref)
        for acc in acc_refs:
            acc[...] = jnp.zeros_like(acc)

    diagonal = iota2(sq, 0) == iota2(sq, 1)
    users = []
    for s in range(sources):
        user = blocks_ref[s, LANES : 2 * LANES, :]
        gap_row = blocks_ref[s, 2 * LANES : 2 * LANES + 1, :]
        gap = jnp.sum(
            jnp.where(diagonal, jnp.broadcast_to(gap_row, sq), 0.0), axis=1, keepdims=True
        )
        stage_ref[2 * LANES * s : 2 * LANES * s + LANES, :] = blocks_ref[s, :LANES, :]
        stage_ref[2 * LANES * s + LANES : 2 * LANES * (s + 1), :] = 2.0 * gap * user
        users.append(user)
    gram_ref[...] += half_gram(jnp.concatenate(users, axis=0))

    base = g * (sources * LANES)
    unroll = 16

    def body(j, carry):
        for at in range(0, unroll, CHAINS):
            first = base + j * unroll + at
            rows = [row_idx_ref[first + k] for k in range(CHAINS)]
            srcs = [src_idx_ref[first + k] for k in range(CHAINS)]
            grads = [stage_ref[pl.ds(srcs[k], 1), :] for k in range(CHAINS)]
            sums = [acc_refs[k][pl.ds(rows[k], 1), :] + grads[k] for k in range(CHAINS)]
            for k in range(CHAINS):
                acc_refs[k][pl.ds(rows[k], 1), :] = sums[k]
        return carry

    lax.fori_loop(0, sources * LANES // unroll, body, 0)

    @pl.when(g == pl.num_programs(0) - 1)
    def _():
        step = 512
        gram = whole_gram(gram_ref[...])

        def finish(i, carry):
            at = pl.ds(pl.multiple_of(i * step, step), step)
            table = table_ref[at, :]
            grad = 2.0 * coef * dot_split(table, gram)
            for acc in acc_refs:
                grad = grad + acc[at, :]
            new_state = state_ref[at, :] + grad * grad
            new_state_ref[at, :] = new_state
            new_table_ref[at, :] = table - step_size * grad / jnp.sqrt(new_state)
            return carry

        lax.fori_loop(0, rows_dev // step, finish, 0)


def update_rows(row_idx, src_idx, blocks, table, state, coef):
    rows_dev, width = table.shape
    devices = blocks.shape[0]
    sources = 8
    whole = pl.BlockSpec((rows_dev, width), lambda g, r, s: (0, 0))
    return pl.pallas_call(
        functools.partial(update_kernel, sources=sources, coef=coef),
        grid_spec=pltpu.PrefetchScalarGridSpec(
            num_scalar_prefetch=2,
            grid=(devices // sources,),
            in_specs=[
                pl.BlockSpec((sources, BLOCK_ROWS, width), lambda g, r, s: (g, 0, 0)),
                whole,
                whole,
            ],
            out_specs=[whole, whole],
            scratch_shapes=[
                pltpu.VMEM((sources * 2 * LANES, width), f32),
                pltpu.VMEM((width, 2 * width), f32),
            ]
            + [pltpu.VMEM((rows_dev + 8, width), f32)] * CHAINS,
        ),
        out_shape=(
            jax.ShapeDtypeStruct((rows_dev, width), f32),
            jax.ShapeDtypeStruct((rows_dev, width), f32),
        ),
        compiler_params=pltpu.CompilerParams(vmem_limit_bytes=48 * 2**20),
        name="update_rows",
    )(row_idx, src_idx, blocks, table, state)


def shards(item_table, adagrad_state, history_ids, positive_ids):
    rows_dev, width = item_table.shape
    users_dev, hist_len = history_ids.shape
    devices = lax.axis_size(DP_ROWS)
    coef = penalty_weight / (rows_dev * devices)
    item_gram = jnp.dot(
        item_table.T,
        item_table,
        precision=lax.Precision.HIGHEST,
        preferred_element_type=f32,
    )
    ids = jnp.concatenate([history_ids, positive_ids[:, None]], axis=1)
    lists, codes = request_lists(ids, ids.T, item_gram, rows_dev, hist_len + 1)
    asked = lax.all_to_all(lists, DP_ROWS, split_axis=0, concat_axis=0, tiled=True)
    rows = asked[:, 0, :].astype(i32).reshape(-1)
    code = asked[:, 1, :].astype(i32).reshape(-1)
    total_row = asked[:, 2, :].sum(axis=0)
    place = jnp.arange(devices * LANES, dtype=i32) // LANES % 8 * (2 * LANES)
    src_idx = place + jnp.maximum(code, 0)
    picked = pick_rows(jnp.where(rows < rows_dev, rows, 0), item_table, total_row, devices)
    fetched = lax.all_to_all(
        picked.reshape(devices, ROW_BLOCK, width),
        DP_ROWS,
        split_axis=0,
        concat_axis=0,
        tiled=True,
    )
    block = user_block(codes, fetched, hist_len, coef)
    blocks = lax.all_gather(block, DP_ROWS)
    return update_rows(rows, src_idx, blocks, item_table, adagrad_state, coef)


def solution(mesh):
    finer = Mesh(mesh.devices.reshape(4, 2, 4, 4), DP_ROWS)
    rows = P(DP_ROWS, None)
    return jax.shard_map(
        shards,
        mesh=finer,
        in_specs=(rows, rows, rows, P(DP_ROWS)),
        out_specs=(rows, rows),
        check_vma=False,
    )
```

time: 569 us -> 324 us (0.57)
  waiting for transfers between devices: 294 us -> 78.3 us
  Pallas kernels: 230 us -> 88 us
  blocking collectives: 0 us -> 132 us
  starting transfers between devices: 16.8 us -> 0.04 us
    psum x1 -> x0, waiting for transfers between devices: 205 us -> none  [shards(): item_total = lax.psum(item_gram, DP_ROWS)]
    all_to_all x0 -> x2, blocking collectives: none -> 132 us  [the longest x1 109 us: shards(): lax.all_to_all(picked.reshape(devices, ROW_BLOCK, width), DP_ROWS, split_...]
    pallas_call x1, Pallas kernels: 160 us -> 44.5 us  [update_rows(): pl.pallas_call(functools.partial(update_kernel, sources=sources, coef=coe...]
    pallas_call x1, Pallas kernels: 47.1 us -> 20.6 us  [pick_rows(): pl.pallas_call(functools.partial(pick_kernel, dests=dests), grid_spec=plt...]
    all_to_all x2 -> x0, starting transfers between devices: 16.7 us -> none  [the longest x1 11.5 us: shards(): lax.all_to_all(lists, DP_ROWS, split_axis=0, concat_axis=0, tiled=True)]
    all_to_all x2 -> x0, waiting for transfers between devices: 10.2 us -> none  [the longest x1 10.2 us: shards(): lax.all_to_all(lists, DP_ROWS, split_axis=0, concat_axis=0, tiled=True)]
  transfers between devices with their start and end apart: 4 -> 1, of which waited for: 3 -> 1; matrix products, arithmetic and copies ran while one was open for 1% -> 0% of each run, Pallas kernels for 0% -> 0%
where the time goes in v2:
time: 324 us
  blocking collectives  132 us (41%)
  Pallas kernels  88 us (27%)
  waiting for transfers between devices  78.3 us (24%)
  between operations  14.1 us (4%)
  matrix products  6.44 us (2%)
    all_to_all x1, blocking collectives, shards(): lax.all_to_all(picked.reshape(devices, ROW_BLOCK, width), DP_ROWS, split_...  109 us
    all_gather x1, waiting for transfers between devices, shards(): blocks = lax.all_gather(block, DP_ROWS)  78.3 us
    pallas_call x1, Pallas kernels, update_rows(): pl.pallas_call(functools.partial(update_kernel, sources=sources, coef=coe...  44.5 us
    all_to_all x1, blocking collectives, shards(): lax.all_to_all(lists, DP_ROWS, split_axis=0, concat_axis=0, tiled=True)  22.9 us
    pallas_call x1, Pallas kernels, pick_rows(): pl.pallas_call(functools.partial(pick_kernel, dests=dests), grid_spec=plt...  20.6 us
    pallas_call x1, Pallas kernels, user_block(): pl.pallas_call(functools.partial(user_kernel, hist_len=hist_len, coef=coe...  13.5 us
    pallas_call x1, Pallas kernels, request_lists(): pl.pallas_call(functools.partial(list_kernel, slots=slots, rows_dev=rows_...  9.46 us
  transfers between devices with their start and end apart: 1, of which 1 were waited for; matrix products, arithmetic and copies ran while one was open for 0% of the time, Pallas kernels for 0%

profile of v2, /device:TPU:1, one launch (start us, length us, event | category | flops | bytes accessed | tf_op | source)
XLA Modules:
  0.0 323.6 jit_solution(4066315342474896146)
XLA Ops:
  7.2 0.0 all-gather.3.cloned.1.call-start
  7.2 1.4 fusion.10.ids_r_ref
  8.6 0.8 pad_add_fusion
  9.4 0.7 copy.6.ids_c_ref
  10.1 0.0 copy-start
  10.1 6.4 %fusion.7.gram_ref = f32[128,128]{1,0:T(8,128)} fusion(f32[4096,128]{1,0:T(8,128)} %table_ref.1), kind=kOutput, calls=%fused_computation.19 | convolution fusion | flops 805306368 | bytes 2162688 | tf_op jit(solution)/shard_map/dot_general | solution.py:310
  16.5 9.5 %request_lists.1 = (f32[128,4,128]{2,1,0:T(4,128)}, s32[128,128]{1,0:T(8,128)}) custom-call(s32[128,51]{1,0:T(8,128)} %copy.6.ids_c_ref, s32[51,128]{1,0:T(8,128)} %fusion.10.ids_r_ref, f32[128,128]{1,0:T(8,128)} %fusion.7.gram_ref), custom_call_target="tpu_custom_call" | custom-call | tf_op jit(solution)/shard_map/request_lists/pallas_call | solution.py:109
  26.0 22.9 %all_to_all.10 = f32[128,4,128]{2,1,0:T(4,128)S(1)} all-to-all(f32[128,4,128]{2,1,0:T(4,128)} %get-tuple-element.4), channel_id=1, replica_groups=mesh['dp_0'=4,'dp_1'=2,'rows_0'=4,'rows_1'=4] {'dp_0','dp_1','rows_0','r..., dimensions={0} | all-to-all | bytes 524288 | tf_op jit(solution)/shard_map/all_to_all | solution.py:318
  48.9 0.2 slice_reduce_fusion
  49.1 0.0 copy-done
  49.1 20.6 %pick_rows.1 = f32[17408,1,128]{2,1,0:T(1,128)S(1)} custom-call(s32[16384]{0:T(1024)S(1)} %compare_select_fusion.rows_ref, f32[4096,1,128]{2,1,0:T(1,128)S(1)} %bitcast.12, f32[1,1,128]{2,1,0:T(1,128)S(1)} %bitcast.15), custom_call_target="tpu_custom_call" | custom-call | tf_op jit(solution)/shard_map/pick_rows/pallas_call | solution.py:142
  69.7 109.0 %all_to_all.11.rows_ref = f32[128,136,128]{2,1,0:T(8,128)} all-to-all(f32[128,136,128]{2,1,0:T(8,128)S(1)} %bitcast.11), channel_id=1, replica_groups=mesh['dp_0'=4,'dp_1'=2,'rows_0'=4,'rows_1'=4] {'dp_0','dp_1','rows_0','r..., dimensions={0} | all-to-all | bytes 17825792 | tf_op jit(solution)/shard_map/all_to_all | solution.py:325
  178.7 13.5 %user_block.1 = f32[264,128]{1,0:T(8,128)} custom-call(s32[128,128]{1,0:T(8,128)} %get-tuple-element.5.code_ref, f32[128,136,128]{2,1,0:T(8,128)} %all_to_all.11.rows_ref), custom_call_target="tpu_custom_call" | custom-call | tf_op jit(solution)/shard_map/user_block/pallas_call | solution.py:198
  192.2 0.0 all-gather.3.cloned.1.call-update
  192.2 0.1 fusion.5
  192.4 78.3 %all-gather.3.cloned.1.call-done = f32[33792,128]{1,0:T(8,128)} async-done(((f32[264,128]{1,0:T(8,128)}), f32[33792,128]{1,0:T(8,128)}) %all-gather.3.cloned.1.call-update) | async-done | bytes 17301520 | tf_op jit(solution)/shard_map/all_gather | solution.py:333
  270.7 0.0 copy-start.1
  270.7 1.6 copy-done.1
  272.2 44.5 %update_rows.1 = (f32[4096,128]{1,0:T(8,128)}, f32[4096,128]{1,0:T(8,128)}) custom-call(s32[16384]{0:T(1024)S(1)} %bitcast.14, s32[16384]{0:T(1024)S(1)} %fusion.2.src_idx_ref, f32[128,264,128]{2,1,0:T(8,128)} %bitcast.16, f32[4096,128]{1,0:T(8,128)S(1)} %copy-done, f32[4096,128]{1,0:T(8,128)S(1)} %copy-done.1), custom_call_target="tpu_custom_call" | custom-call | tf_op jit(solution)/shard_map/update_rows/pallas_call | solution.py:279
  (2 shorter events, 0.0 us)
Async XLA Ops:
  7.2 263.5 %all-gather.3.cloned.1.call-start = ((), (), s32[]{:S(2)}) async-start(), calls=%async_computation.2 | async-start | bytes 17436672 | tf_op jit(solution)/shard_map/all_gather | solution.py:333
  10.1 39.0 %copy-start = (f32[4096,128]{1,0:T(8,128)S(1)}, f32[4096,128]{1,0:T(8,128)}, u32[]{:S(2)}) copy-start(f32[4096,128]{1,0:T(8,128)} %table_ref.1) | copy-start | bytes 6291460
  270.7 1.6 copy-start.1
Sparse Core Ops, SparseCore 0:
  192.3 78.2 all-gather.2

commit v3 on v2

v3 whole, which is shorter than its diff:
```python
import functools

import jax
import jax.numpy as jnp
from jax import lax
from jax.experimental import pallas as pl
from jax.experimental.pallas import tpu as pltpu
from jax.sharding import Mesh
from jax.sharding import PartitionSpec as P

X, CORE, Z, Y = "x", "core", "z", "y"
DP_ROWS = (X, CORE, Z, Y)

penalty_weight = 10.0
step_size = 0.05

LANES = 128
BLOCK_ROWS = 264
CHAINS = 8
PARTS = ((0, 88), (88, 176), (176, 256))

bf16 = jnp.bfloat16
f32 = jnp.float32
i32 = jnp.int32


def iota2(shape, dim):
    return lax.broadcasted_iota(i32, shape, dim)


def split2(x):
    hi = x.astype(bf16)
    lo = (x - hi.astype(f32)).astype(bf16)
    return hi, lo


def dot_f32(a, b):
    return jnp.dot(a, b, preferred_element_type=f32)


def dot_split(a, b):
    ah, al = split2(a)
    bh, bl = split2(b)
    return dot_f32(ah, bh) + (dot_f32(ah, bl) + dot_f32(al, bh))


def half_gram(a):
    hi, lo = split2(a)
    return lax.dot_general(
        hi,
        jnp.concatenate([hi, lo], axis=1),
        (((0,), (0,)), ((), ())),
        preferred_element_type=f32,
    )


def whole_gram(halves):
    cross = halves[:, LANES:]
    return halves[:, :LANES] + (cross + cross.T)


def list_kernel(ids_c_ref, ids_r_ref, gram_ref, out_ref, *, slots, rows_dev):
    sq = (LANES, LANES)
    lane = iota2(sq, 1)
    sub = iota2(sq, 0)
    lane_f = lane.astype(f32)
    one = jnp.ones(sq, f32)
    zero = jnp.zeros(sq, f32)
    lower = jnp.concatenate([jnp.where(sub > lane, one, zero), one], axis=0).astype(bf16)
    ones = one.astype(bf16)
    users = iota2((1, LANES), 1)
    carry = jnp.zeros(sq, f32)
    acc = jnp.zeros((3 * LANES, LANES), f32)
    for h in range(slots):
        owner_c = ids_c_ref[:, h : h + 1] // rows_dev
        member = owner_c == lane
        counts = dot_f32(lower, jnp.where(member, one, zero).astype(bf16))
        mine = jnp.where(member, counts[:LANES] + carry, zero).astype(bf16)
        rank = dot_f32(mine, ones)
        place = jnp.where(rank == lane_f, one, zero).astype(bf16)
        ids = ids_r_ref[h : h + 1, :]
        local = ids % rows_dev
        at_owner = ids // rows_dev == sub
        high = (local // 64 + 1).astype(f32)
        low = (local % 64).astype(f32)
        code = (users + (LANES if h == slots - 1 else 0)).astype(f32)
        vals = jnp.concatenate(
            [
                jnp.where(at_owner, jnp.broadcast_to(high, sq), zero),
                jnp.where(at_owner, jnp.broadcast_to(low, sq), zero),
                jnp.where(at_owner, jnp.broadcast_to(code, sq), zero),
            ],
            axis=0,
        ).astype(bf16)
        acc = acc + dot_f32(vals, place)
        carry = carry + counts[LANES:]
    high = acc[:LANES].astype(i32)
    low = acc[LANES : 2 * LANES].astype(i32)
    code = acc[2 * LANES :].astype(i32)
    present = high > 0
    code = jnp.where(present, code, -1)
    out_ref[:, 0, :] = jnp.where(present, (high - 1) * 64 + low, rows_dev).astype(f32)
    out_ref[:, 1, :] = code.astype(f32)
    out_ref[:, 2, :] = gram_ref[...]
    out_ref[:, 3, :] = zero


def request_lists(ids_c, ids_r, gram, rows_dev, slots):
    return pl.pallas_call(
        functools.partial(list_kernel, slots=slots, rows_dev=rows_dev),
        out_shape=jax.ShapeDtypeStruct((LANES, 4, LANES), f32),
        name="request_lists",
    )(ids_c, ids_r, gram)


def partial_kernel(rows_ref, here_ref, table_ref, codes_ref, *refs, half, other_core):
    if other_core:
        (out_ref,) = refs[:1]
        scratch = refs[1:]
    else:
        from_ref = refs[0]
        outs = refs[1:11]
        scratch = refs[11:]
    picked_refs, block_refs = scratch[:4], scratch[4:]
    dx = pl.program_id(0)
    dz = pl.program_id(1)
    at_x = (here_ref[0] + (dx + 2 * half)) & 3
    at_core = here_ref[1] ^ 1 if other_core else here_ref[1]
    at_z = (here_ref[2] + dz) & 3
    code_of = iota2((2 * LANES, LANES), 0).astype(f32)
    one = jnp.ones((2 * LANES, LANES), f32)
    zero = jnp.zeros((2 * LANES, LANES), f32)
    unroll = 32
    for dy in range(4):
        at_y = (here_ref[3] + dy) & 3
        source = ((at_x * 2 + at_core) * 4 + at_z) * 4 + at_y
        base = source * LANES
        picked_ref = picked_refs[dy]
        for at in range(0, LANES, unroll):
            picked = [table_ref[pl.ds(rows_ref[base + (at + k)], 1), :] for k in range(unroll)]
            for k in range(unroll):
                picked_ref[at + k : at + k + 1, :] = picked[k]
        weight = jnp.where(codes_ref[pl.ds(source, 1), :] == code_of, one, zero).astype(bf16)
        block = dot_f32(
            jnp.concatenate([weight, weight], axis=1),
            jnp.concatenate(split2(picked_ref[...]), axis=0),
        )
        if other_core:
            out_ref[0, 0, dy] = block
        else:
            block_refs[dy][...] = block + from_ref[0, 0, dy]
    if other_core:
        return
    (a0, a1), (b0, b1), (c0, c1) = PARTS
    for i in range(2):

        @pl.when(dx == i)
        def _(i=i):
            for dy in range(4):
                outs[i][dz, dy] = block_refs[dy][a0:a1, :]

    for j in range(4):

        @pl.when(dz == j)
        def _(j=j):
            for dy in range(4):
                outs[2 + j][dy, dx] = block_refs[dy][b0:b1, :]

    for dy in range(4):
        outs[6 + dy][dx, dz] = block_refs[dy][c0:c1, :]


def partial_sums(rows_idx, here, table, codes, half, received=None):
    rows_dev, width = table.shape
    other_core = received is None
    blocks = pl.BlockSpec((1, 1, 4, 2 * LANES, width), lambda dx, dz, r, h: (dx, dz, 0, 0, 0))

    def whole(shape):
        return pl.BlockSpec(shape, lambda dx, dz, r, h: (0,) * len(shape))

    in_specs = [whole((rows_dev, width)), whole(codes.shape)]
    operands = (rows_idx, here, table, codes)
    scratch = [pltpu.VMEM((LANES, width), f32)] * 4
    if other_core:
        shapes = [(2, 4, 4, 2 * LANES, width)]
        out_specs = [blocks]
    else:
        in_specs.append(blocks)
        operands += (received,)
        la, lb, lc = (end - start for start, end in PARTS)
        shapes = [(4, 4, la, width)] * 2 + [(4, 2, lb, width)] * 4 + [(2, 4, lc, width)] * 4
        out_specs = [whole(shape) for shape in shapes]
        scratch = scratch + [pltpu.VMEM((2 * LANES, width), f32)] * 4
    return pl.pallas_call(
        functools.partial(partial_kernel, half=half, other_core=other_core),
        grid_spec=pltpu.PrefetchScalarGridSpec(
            num_scalar_prefetch=2,
            grid=(2, 4),
            in_specs=in_specs,
            out_specs=out_specs,
            scratch_shapes=scratch,
        ),
        out_shape=[jax.ShapeDtypeStruct(shape, f32) for shape in shapes],
        compiler_params=pltpu.CompilerParams(vmem_limit_bytes=40 * 2**20),
        name="partial_other" if other_core else "partial_own",
    )(*operands)


def split_sum_kernel(*refs, halves):
    at = 0
    outs = refs[4 * sum(halves) :]
    for part, n in enumerate(halves):
        pieces = [refs[at + d * n : at + (d + 1) * n] for d in range(4)]
        at += 4 * n
        for i in range(4):
            out_ref = outs[4 * part + i]
            if n == 1:
                spots = [(0, i, slice(None))]
            elif pieces[0][0].shape[0] == 2:
                spots = [(i // 2, i % 2, slice(None))]
            else:
                spots = [(half, i, slice(2 * half, 2 * half + 2)) for half in range(2)]
            for half, place, into in spots:
                total = pieces[0][half][place] + pieces[1][half][place]
                total = total + (pieces[2][half][place] + pieces[3][half][place])
                out_ref[into] = total


def split_sums(parts, name):
    operands = [half for part in parts for pieces in part for half in pieces]
    out_shape = [
        jax.ShapeDtypeStruct((4,) * (part[0][0].ndim - 3) + part[0][0].shape[-2:], f32)
        for part in parts
        for _ in range(4)
    ]
    outs = pl.pallas_call(
        functools.partial(split_sum_kernel, halves=tuple(len(part[0]) for part in parts)),
        out_shape=out_shape,
        compiler_params=pltpu.CompilerParams(vmem_limit_bytes=40 * 2**20),
        name=name,
    )(*operands)
    return [outs[4 * part : 4 * part + 4] for part in range(3)]


def shifted(array, axis, by):
    return lax.ppermute(array, axis, [(i, (i + by) % 4) for i in range(4)])


def to_sources(rows_idx, here, table, codes):
    swap = [(0, 1), (1, 0)]
    received = []
    for half in range(2):
        (mine,) = partial_sums(rows_idx, here, table, codes, half)
        received.append(lax.ppermute(mine, CORE, swap))
    first, second, third = [[], [], [], []], [[], [], [], []], [[], [], [], []]
    for half in range(2):
        outs = partial_sums(rows_idx, here, table, codes, half, received[half])
        for i in range(2):
            d = 2 * half + i
            first[d].append(outs[i] if d == 0 else shifted(outs[i], X, d))
        for d in range(4):
            second[d].append(outs[2 + d] if d == 0 else shifted(outs[2 + d], Z, d))
            third[d].append(outs[6 + d] if d == 0 else shifted(outs[6 + d], Y, d))
    first, second, third = split_sums([first, second, third], "sum_stage_1")
    moved = [
        [[piece if d == 0 else shifted(piece, axis, d)] for d, piece in enumerate(part)]
        for part, axis in ((first, Z), (second, Y), (third, X))
    ]
    first, second, third = split_sums(moved, "sum_stage_2")
    return [
        [piece if d == 0 else shifted(piece, axis, d) for d, piece in enumerate(part)]
        for part, axis in ((first, Y), (second, X), (third, Z))
    ]


def user_kernel(*refs, hist_len):
    total_ref, out_ref = refs[12:]
    sums = []
    for part in range(3):
        piece = refs[4 * part : 4 * part + 4]
        sums.append((piece[0][...] + piece[1][...]) + (piece[2][...] + piece[3][...]))
    sums = jnp.concatenate(sums, axis=0)
    user = sums[:LANES] / hist_len
    positive = sums[LANES:]
    gap = jnp.sum(user * positive, axis=1, keepdims=True) - 1.0
    sq = (LANES, LANES)
    gap_row = jnp.sum(
        jnp.where(iota2(sq, 0) == iota2(sq, 1), jnp.broadcast_to(gap, sq), 0.0),
        axis=0,
        keepdims=True,
    )
    out_ref[:LANES, :] = positive
    out_ref[LANES : 2 * LANES, :] = user
    tail = (8, LANES)
    out_ref[2 * LANES :, :] = jnp.where(
        iota2(tail, 0) == 0,
        jnp.broadcast_to(gap_row, tail),
        jnp.broadcast_to(total_ref[...], tail),
    )


def user_block(parts, total_row, hist_len):
    width = total_row.shape[-1]
    return pl.pallas_call(
        functools.partial(user_kernel, hist_len=hist_len),
        out_shape=jax.ShapeDtypeStruct((BLOCK_ROWS, width), f32),
        name="user_block",
    )(*[piece for part in parts for piece in part], total_row)


def update_kernel(
    row_idx_ref, src_idx_ref, blocks_ref, item_ref, table_ref, state_ref, new_table_ref, new_state_ref,
    stage_ref, gram_ref, *acc_refs, sources, coef, hist_len,
):
    g = pl.program_id(0)
    rows_dev = table_ref.shape[0]
    sq = (LANES, LANES)

    @pl.when(g == 0)
    def _():
        gram_ref[...] = jnp.zeros_like(gram_ref)
        for acc in acc_refs:
            acc[...] = jnp.zeros_like(acc)

    diagonal = iota2(sq, 0) == iota2(sq, 1)
    users = jnp.concatenate(
        [blocks_ref[s, LANES : 2 * LANES, :] for s in range(sources)], axis=0
    )
    pulls = dot_split(users, item_ref[...])
    for s in range(sources):
        user = blocks_ref[s, LANES : 2 * LANES, :]
        gap_row = blocks_ref[s, 2 * LANES : 2 * LANES + 1, :]
        gap = 2.0 * jnp.sum(
            jnp.where(diagonal, jnp.broadcast_to(gap_row, sq), 0.0), axis=1, keepdims=True
        )
        pull = pulls[LANES * s : LANES * (s + 1)]
        grad = gap * blocks_ref[s, :LANES, :] + 2.0 * coef * pull
        stage_ref[2 * LANES * s : 2 * LANES * s + LANES, :] = grad / hist_len
        stage_ref[2 * LANES * s + LANES : 2 * LANES * (s + 1), :] = gap * user
    gram_ref[...] += half_gram(users)

    base = g * (sources * LANES)
    unroll = 16

    def body(j, carry):
        for at in range(0, unroll, CHAINS):
            first = base + j * unroll + at
            rows = [row_idx_ref[first + k] for k in range(CHAINS)]
            srcs = [src_idx_ref[first + k] for k in range(CHAINS)]
            grads = [stage_ref[pl.ds(srcs[k], 1), :] for k in range(CHAINS)]
            sums = [acc_refs[k][pl.ds(rows[k], 1), :] + grads[k] for k in range(CHAINS)]
            for k in range(CHAINS):
                acc_refs[k][pl.ds(rows[k], 1), :] = sums[k]
        return carry

    lax.fori_loop(0, sources * LANES // unroll, body, 0)

    @pl.when(g == pl.num_programs(0) - 1)
    def _():
        step = 512
        gram = whole_gram(gram_ref[...])

        def finish(i, carry):
            at = pl.ds(pl.multiple_of(i * step, step), step)
            table = table_ref[at, :]
            grad = 2.0 * coef * dot_split(table, gram)
            for acc in acc_refs:
                grad = grad + acc[at, :]
            new_state = state_ref[at, :] + grad * grad
            new_state_ref[at, :] = new_state
            new_table_ref[at, :] = table - step_size * grad / jnp.sqrt(new_state)
            return carry

        lax.fori_loop(0, rows_dev // step, finish, 0)


def update_rows(row_idx, src_idx, blocks, item_total, table, state, coef, hist_len):
    rows_dev, width = table.shape
    devices = blocks.shape[0]
    sources = 8
    whole = pl.BlockSpec((rows_dev, width), lambda g, r, s: (0, 0))
    return pl.pallas_call(
        functools.partial(update_kernel, sources=sources, coef=coef, hist_len=hist_len),
        grid_spec=pltpu.PrefetchScalarGridSpec(
            num_scalar_prefetch=2,
            grid=(devices // sources,),
            in_specs=[
                pl.BlockSpec((sources, BLOCK_ROWS, width), lambda g, r, s: (g, 0, 0)),
                pl.BlockSpec((width, width), lambda g, r, s: (0, 0)),
                whole,
                whole,
            ],
            out_specs=[whole, whole],
            scratch_shapes=[
                pltpu.VMEM((sources * 2 * LANES, width), f32),
                pltpu.VMEM((width, 2 * width), f32),
            ]
            + [pltpu.VMEM((rows_dev + 8, width), f32)] * CHAINS,
        ),
        out_shape=(
            jax.ShapeDtypeStruct((rows_dev, width), f32),
            jax.ShapeDtypeStruct((rows_dev, width), f32),
        ),
        compiler_params=pltpu.CompilerParams(vmem_limit_bytes=48 * 2**20),
        name="update_rows",
    )(row_idx, src_idx, blocks, item_total, table, state)


def shards(item_table, adagrad_state, history_ids, positive_ids):
    rows_dev, width = item_table.shape
    users_dev, hist_len = history_ids.shape
    devices = lax.axis_size(DP_ROWS)
    coef = penalty_weight / (rows_dev * devices)
    item_gram = jnp.dot(
        item_table.T,
        item_table,
        precision=lax.Precision.HIGHEST,
        preferred_element_type=f32,
    )
    ids = jnp.concatenate([history_ids, positive_ids[:, None]], axis=1)
    lists = request_lists(ids, ids.T, item_gram, rows_dev, hist_len + 1)
    asked = lax.all_to_all(lists, DP_ROWS, split_axis=0, concat_axis=0, tiled=True)
    rows = asked[:, 0, :].astype(i32).reshape(-1)
    codes = asked[:, 1, :]
    total_row = asked[:, 2, :].sum(axis=0, keepdims=True)
    place = jnp.arange(devices * LANES, dtype=i32) // LANES % 8 * (2 * LANES)
    src_idx = place + jnp.maximum(codes.astype(i32).reshape(-1), 0)
    here = jnp.stack([lax.axis_index(axis) for axis in DP_ROWS]).astype(i32)
    parts = to_sources(jnp.where(rows < rows_dev, rows, 0), here, item_table, codes)
    block = user_block(parts, total_row, hist_len)
    blocks = lax.all_gather(block, DP_ROWS)
    item_total = blocks[:, 2 * LANES + 1, :]
    return update_rows(
        rows, src_idx, blocks, item_total, item_table, adagrad_state, coef, hist_len
    )


def solution(mesh):
    finer = Mesh(mesh.devices.reshape(4, 2, 4, 4), DP_ROWS)
    rows = P(DP_ROWS, None)
    return jax.shard_map(
        shards,
        mesh=finer,
        in_specs=(rows, rows, rows, P(DP_ROWS)),
        out_specs=(rows, rows),
        check_vma=False,
    )
```

time: 324 us -> 324 us (level)
  blocking collectives: 132 us -> 0 us
  waiting for transfers between devices: 78.3 us -> 150 us
  starting transfers between devices: 0.04 us -> 54.5 us
  local copies, waits for them, and re-layouts: 2.33 us -> 5.87 us
    all_to_all x2 -> x0, blocking collectives: 132 us -> none  [the longest x1 109 us: shards(): lax.all_to_all(picked.reshape(devices, ROW_BLOCK, width), DP_ROWS, split_...]
    ppermute x0 -> x35, waiting for transfers between devices: none -> 55.1 us  [the longest x33 55.1 us: shifted(): return lax.ppermute(array, axis, [(i, (i + by) % 4) for i in range(4)])]
    ppermute x0 -> x35, starting transfers between devices: none -> 42.9 us  [the longest x33 42.2 us: shifted(): return lax.ppermute(array, axis, [(i, (i + by) % 4) for i in range(4)])]
    all_to_all x0 -> x1, starting transfers between devices: none -> 11.5 us  [shards(): lax.all_to_all(lists, DP_ROWS, split_axis=0, concat_axis=0, tiled=True)]
    all_to_all x0 -> x1, waiting for transfers between devices: none -> 11.3 us  [shards(): lax.all_to_all(lists, DP_ROWS, split_axis=0, concat_axis=0, tiled=True)]
    all_gather x1, waiting for transfers between devices: 78.3 us -> 83.8 us  [shards(): blocks = lax.all_gather(block, DP_ROWS)]
    pallas_call x2 -> x7, Pallas kernels: 34.1 us -> 33.1 us  [the longest x4 30.8 us: partial_sums(): pl.pallas_call(functools.partial(partial_kernel, half=half, other_core=ot...]
  transfers between devices with their start and end apart: 1 -> 37, of which waited for: 1 -> 20; matrix products, arithmetic and copies ran while one was open for 0% -> 0% of each run, Pallas kernels for 0% -> 7%
where the time goes in v3:
time: 324 us; the launch traced here: 323 us
  waiting for transfers between devices  150 us (46%)
  Pallas kernels  88.9 us (27%)
  starting transfers between devices  54.5 us (17%)
  between operations  14.2 us (4%)
  matrix products  6.45 us (2%)
  local copies, waits for them, and re-layouts  5.87 us (2%)
    all_gather x1, waiting for transfers between devices, shards(): blocks = lax.all_gather(block, DP_ROWS)  83.8 us
    ppermute x33, waiting for transfers between devices, shifted(): return lax.ppermute(array, axis, [(i, (i + by) % 4) for i in range(4)])  55.1 us
    pallas_call x1, Pallas kernels, update_rows(): pl.pallas_call(functools.partial(update_kernel, sources=sources, coef=coe...  46.3 us
    ppermute x33, starting transfers between devices, shifted(): return lax.ppermute(array, axis, [(i, (i + by) % 4) for i in range(4)])  42.2 us
    pallas_call x4, Pallas kernels, partial_sums(): pl.pallas_call(functools.partial(partial_kernel, half=half, other_core=ot...  30.8 us
    all_to_all x1, starting transfers between devices, shards(): lax.all_to_all(lists, DP_ROWS, split_axis=0, concat_axis=0, tiled=True)  11.5 us
    all_to_all x1, waiting for transfers between devices, shards(): lax.all_to_all(lists, DP_ROWS, split_axis=0, concat_axis=0, tiled=True)  11.3 us
    pallas_call x1, Pallas kernels, request_lists(): pl.pallas_call(functools.partial(list_kernel, slots=slots, rows_dev=rows_...  9.46 us
  transfers between devices with their start and end apart: 37, of which 20 were waited for; matrix products, arithmetic and copies ran while one was open for 0% of the time, Pallas kernels for 7%

profile of v3, /device:TPU:1, one launch (start us, length us, event | category | flops | bytes accessed | tf_op | source)
XLA Modules:
  0.0 323.0 jit_solution(11985163149565772659)
XLA Ops:
  7.2 1.4 fusion.9.ids_r_ref
  8.6 0.8 pad_add_fusion
  9.3 0.7 copy.12.ids_c_ref
  10.1 6.4 %fusion.6.gram_ref = f32[128,128]{1,0:T(8,128)} fusion(f32[4096,128]{1,0:T(8,128)} %table_ref.9), kind=kOutput, calls=%fused_computation.18 | convolution fusion | flops 805306368 | bytes 2162688 | tf_op jit(solution)/shard_map/dot_general | solution.py:414
  16.5 9.5 %request_lists.1 = f32[128,4,128]{2,1,0:T(4,128)} custom-call(s32[128,51]{1,0:T(8,128)} %copy.12.ids_c_ref, s32[51,128]{1,0:T(8,128)} %fusion.9.ids_r_ref, f32[128,128]{1,0:T(8,128)} %fusion.6.gram_ref), custom_call_target="tpu_custom_call" | custom-call | tf_op jit(solution)/shard_map/request_lists/pallas_call | solution.py:109
  26.0 11.5 %all-to-all-start = ((f32[128,4,128]{2,1,0:T(4,128)}), f32[128,4,128]{2,1,0:T(4,128)S(1)}, u32[]{:S(2)}, u32[]{:S(2)}) async-start(f32[128,4,128]{2,1,0:T(4,128)} %request_lists.1), calls=%async_computation | async-start | bytes 524288 | tf_op jit(solution)/shard_map/all_to_all | solution.py:422
  37.6 11.3 %all-to-all-done = f32[128,4,128]{2,1,0:T(4,128)S(1)} async-done(((f32[128,4,128]{2,1,0:T(4,128)}), f32[128,4,128]{2,1,0:T(4,128)S(1)}, u32[]{:S(2)}, u32[]{:S(2)}) %all-to-all-start) | async-done | bytes 262176 | tf_op jit(solution)/shard_map/all_to_all | solution.py:422
  48.9 0.7 slice_reduce_fusion
  49.6 7.5 %partial_other.2 = f32[2,4,4,256,128]{4,3,2,1,0:T(8,128)S(1)} custom-call(s32[16384]{0:T(1024)S(1)} %compare_select_fusion.rows_ref, s32[4]{0:T(128)S(1)} %pad_add_fusion.1.here_ref, f32[4096,128]{1,0:T(8,128)S(1)} %copy-done, f32[128,128]{1,0:T(8,128)S(1)} %bitcast.20), custom_call_target="tpu_custom_call" | custom-call | tf_op jit(solution)/shard_map/partial_other/pallas_call | solution.py:194
  57.1 0.6 collective-permute-start
  57.7 7.4 %partial_other.3 = f32[2,4,4,256,128]{4,3,2,1,0:T(8,128)S(1)} custom-call(s32[16384]{0:T(1024)S(1)} %compare_select_fusion.rows_ref, s32[4]{0:T(128)S(1)} %pad_add_fusion.1.here_ref, f32[4096,128]{1,0:T(8,128)S(1)} %copy-done, f32[128,128]{1,0:T(8,128)S(1)} %bitcast.21), custom_call_target="tpu_custom_call" | custom-call | tf_op jit(solution)/shard_map/partial_other/pallas_call | solution.py:194
  65.2 8.0 %partial_own.2 = (f32[4,4,88,128]{3,2,1,0:T(8,128)S(1)}, f32[4,4,88,128]{3,2,1,0:T(8,128)S(1)}, f32[4,2,88,128]{3,2,1,0:T(8,128)S(1)}, f32[4,2,88,128]{3,2,1,0:T...) custom-call(s32[16384]{0:T(1024)S(1)} %compare_select_fusion.rows_re, ...), custom_call_target="tpu_custom_call" | custom-call | tf_op jit(solution)/shard_map/partial_own/pallas_call | solution.py:194
  73.2 0.4 collective-permute-start.11
  73.6 1.6 collective-permute-start.13
  75.2 0.8 collective-permute-start.15
  76.1 0.6 collective-permute-start.5
  76.6 1.1 collective-permute-start.7
  77.8 7.9 %partial_own.3 = (f32[4,4,88,128]{3,2,1,0:T(8,128)S(1)}, f32[4,4,88,128]{3,2,1,0:T(8,128)S(1)}, f32[4,2,88,128]{3,2,1,0:T(8,128)S(1)}, f32[4,2,88,128]{3,2,1,0:T...) custom-call(s32[16384]{0:T(1024)S(1)} %compare_select_fusion.rows_re, ...), custom_call_target="tpu_custom_call" | custom-call | tf_op jit(solution)/shard_map/partial_own/pallas_call | solution.py:194
  85.7 0.5 collective-permute-start.12
  86.2 3.4 %collective-permute-done.13.refs_16_ = f32[2,4,80,128]{3,2,1,0:T(8,128)S(1)} collective-permute-done((f32[2,4,80,128]{3,2,1,0:T(8,128)S(1)}, f32[2,4,80,128]{3,2,1,0:T(8,128)S(1)}, u32[]{:S(2)}, u32[]{:S(2)}) %collective-permute-start.13) | collective-permute-done | bytes 327712 | tf_op jit(solution)/shard_map/ppermute | solution.py:246
  89.6 1.3 collective-permute-start.14
  90.9 3.7 %collective-permute-start.16 = (f32[2,4,80,128]{3,2,1,0:T(8,128)S(1)}, f32[2,4,80,128]{3,2,1,0:T(8,128)S(1)}, u32[]{:S(2)}, u32[]{:S(2)}) collective-permute-start(f32[2,4,80,128]{3,2,1,0:T(8,128)S(1)} %get-tuple-element.65), channel_id=1, source_target_pairs={{0,3},{1,0},{2,1},{3,2},{4,7},{5,4},{6,5},{7,6},{8,11},{9,8},{10,9... | collective-permute-start | bytes 983048 | tf_op jit(solution)/shard_map/ppermute | solution.py:246
  94.6 0.8 collective-permute-done.12.refs_15_
  95.4 5.4 %collective-permute-done.14.refs_17_ = f32[2,4,80,128]{3,2,1,0:T(8,128)S(1)} collective-permute-done((f32[2,4,80,128]{3,2,1,0:T(8,128)S(1)}, f32[2,4,80,128]{3,2,1,0:T(8,128)S(1)}, u32[]{:S(2)}, u32[]{:S(2)}) %collective-permute-start.14) | collective-permute-done | bytes 327712 | tf_op jit(solution)/shard_map/ppermute | solution.py:246
  101.1 3.2 collective-permute-done.16.refs_19_
  104.3 4.0 %collective-permute-start.6 = (f32[4,2,88,128]{3,2,1,0:T(8,128)S(1)}, f32[4,2,88,128]{3,2,1,0:T(8,128)S(1)}, u32[]{:S(2)}, u32[]{:S(2)}) collective-permute-start(f32[4,2,88,128]{3,2,1,0:T(8,128)S(1)} %get-tuple-element.53), channel_id=1, source_target_pairs={{0,4},{4,8},{8,12},{12,0},{1,5},{5,9},{9,13},{13,1},{2,6},{6,10},{... | collective-permute-start | bytes 1081352 | tf_op jit(solution)/shard_map/ppermute | solution.py:246
  108.2 1.6 collective-permute-start.3
  109.8 1.2 collective-permute-start.4
  111.0 3.9 %collective-permute-done.9.refs_10_ = f32[4,2,88,128]{3,2,1,0:T(8,128)S(1)} collective-permute-done((f32[4,2,88,128]{3,2,1,0:T(8,128)S(1)}, f32[4,2,88,128]{3,2,1,0:T(8,128)S(1)}, u32[]{:S(2)}, u32[]{:S(2)}) %collective-permute-start.9) | collective-permute-done | bytes 360480 | tf_op jit(solution)/shard_map/ppermute | solution.py:246
  114.9 0.8 collective-permute-start.8
  115.7 2.8 collective-permute-start.10
  118.5 5.7 %collective-permute-done.8.refs_9_ = f32[4,2,88,128]{3,2,1,0:T(8,128)S(1)} collective-permute-done((f32[4,2,88,128]{3,2,1,0:T(8,128)S(1)}, f32[4,2,88,128]{3,2,1,0:T(8,128)S(1)}, u32[]{:S(2)}, u32[]{:S(2)}) %collective-permute-start.8) | collective-permute-done | bytes 360480 | tf_op jit(solution)/shard_map/ppermute | solution.py:246
  124.2 7.1 %collective-permute-done.10.refs_11_ = f32[4,2,88,128]{3,2,1,0:T(8,128)S(1)} collective-permute-done((f32[4,2,88,128]{3,2,1,0:T(8,128)S(1)}, f32[4,2,88,128]{3,2,1,0:T(8,128)S(1)}, u32[]{:S(2)}, u32[]{:S(2)}) %collective-permute-start.10) | collective-permute-done | bytes 360480 | tf_op jit(solution)/shard_map/ppermute | solution.py:246
  131.3 7.7 %collective-permute-done.3.refs_2_ = f32[4,4,88,128]{3,2,1,0:T(8,128)S(1)} collective-permute-done((f32[4,4,88,128]{3,2,1,0:T(8,128)S(1)}, f32[4,4,88,128]{3,2,1,0:T(8,128)S(1)}, u32[]{:S(2)}, u32[]{:S(2)}) %collective-permute-start.3) | collective-permute-done | bytes 720928 | tf_op jit(solution)/shard_map/ppermute | solution.py:246
  139.0 2.9 collective-permute-done.4.refs_3_
  142.0 0.4 sum_stage_1.1
  142.4 1.2 collective-permute-start.17
  143.6 1.5 collective-permute-start.23
  145.1 3.1 collective-permute-start.24
  148.2 0.5 collective-permute-start.18
  148.7 1.3 collective-permute-done.23.refs_9_
  150.0 1.7 collective-permute-start.19
  151.7 3.3 %collective-permute-done.24.refs_10_ = f32[4,80,128]{2,1,0:T(8,128)S(1)} collective-permute-done((f32[4,80,128]{2,1,0:T(8,128)S(1)}, f32[4,80,128]{2,1,0:T(8,128)S(1)}, u32[]{:S(2)}, u32[]{:S(2)}) %collective-permute-start.24) | collective-permute-done | bytes 163872 | tf_op jit(solution)/shard_map/ppermute | solution.py:246
  155.0 2.6 collective-permute-start.21
  157.8 2.8 collective-permute-done.20.refs_5_
  160.6 3.6 %collective-permute-done.21.refs_6_ = f32[4,88,128]{2,1,0:T(8,128)S(1)} collective-permute-done((f32[4,88,128]{2,1,0:T(8,128)S(1)}, f32[4,88,128]{2,1,0:T(8,128)S(1)}, u32[]{:S(2)}, u32[]{:S(2)}) %collective-permute-start.21) | collective-permute-done | bytes 180256 | tf_op jit(solution)/shard_map/ppermute | solution.py:246
  164.2 1.0 collective-permute-done.22.refs_7_
  165.2 0.6 copy-done.2
  165.9 0.6 copy-done.3
  166.5 0.6 copy-done.4
  167.1 0.6 collective-permute-start.26
  167.9 2.9 collective-permute-start.33
  171.0 4.2 %collective-permute-start.27 = (f32[88,128]{1,0:T(8,128)S(1)}, f32[88,128]{1,0:T(8,128)S(1)}, u32[]{:S(2)}, u32[]{:S(2)}) collective-permute-start(f32[88,128]{1,0:T(8,128)S(1)} %get-tuple-element.80), channel_id=1, source_target_pairs={{0,2},{1,3},{2,0},{3,1},{4,6},{5,7},{6,4},{7,5},{8,10},{9,11},{10,... | collective-permute-start | bytes 135176 | tf_op jit(solution)/shard_map/ppermute | solution.py:246
  175.5 2.4 collective-permute-start.30
  178.1 0.3 collective-permute-done.28.refs_3_
  178.4 1.0 collective-permute-done.29.refs_5_
  179.4 0.5 collective-permute-done.30.refs_6_
  179.9 1.1 collective-permute-done.31.refs_7_
  181.0 0.6 copy-done.10
  181.6 1.8 user_block.1
  183.4 83.8 %all-gather.3.cloned.1.call-done = f32[33792,128]{1,0:T(8,128)} async-done(((f32[264,128]{1,0:T(8,128)}), f32[33792,128]{1,0:T(8,128)}) %all-gather.3.cloned.1.call-update) | async-done | bytes 17301520 | tf_op jit(solution)/shard_map/all_gather | solution.py:431
  267.2 1.1 slice.19
  268.3 1.6 copy-done.1
  269.9 46.3 %update_rows.1 = (f32[4096,128]{1,0:T(8,128)}, f32[4096,128]{1,0:T(8,128)}) custom-call(s32[16384]{0:T(1024)S(1)} %bitcast.26, s32[16384]{0:T(1024)S(1)} %fusion.2.src_idx_ref, f32[128,264,128]{2,1,0:T(8,128)} %bitcast.29, f32[128,128]{1,0:T(8,128)S(1)} %bitcast.27, f32[4096,128]{1,0:T(8,128)S(1)} %copy-done, f32[4096,128]{1,0:T(8,128)S(1)} %copy-done.1), custom_call_target="tpu_custom_call" | custom-call | tf_op jit(solution)/shard_map/update_rows/pallas_call | solution.py:382
  (57 shorter events, 1.7 us)
Async XLA Ops:
  10.1 39.5 %copy-start = (f32[4096,128]{1,0:T(8,128)S(1)}, f32[4096,128]{1,0:T(8,128)}, u32[]{:S(2)}) copy-start(f32[4096,128]{1,0:T(8,128)} %table_ref.9) | copy-start | bytes 6291460
  26.0 22.9 %all-to-all-start = ((f32[128,4,128]{2,1,0:T(4,128)}), f32[128,4,128]{2,1,0:T(4,128)S(1)}, u32[]{:S(2)}, u32[]{:S(2)}) async-start(f32[128,4,128]{2,1,0:T(4,128)} %request_lists.1), calls=%async_computation | async-start | bytes 524288 | tf_op jit(solution)/shard_map/all_to_all | solution.py:422
  37.5 229.7 %all-gather.3.cloned.1.call-start = ((), (), s32[]{:S(2)}) async-start(), calls=%async_computation.1 | async-start | bytes 17436672 | tf_op jit(solution)/shard_map/all_gather | solution.py:431
  57.1 8.1 %collective-permute-start = (f32[2,4,4,256,128]{4,3,2,1,0:T(8,128)S(1)}, f32[2,4,4,256,128]{4,3,2,1,0:T(8,128)S(1)}, u32[]{:S(2)}, u32[]{:S(2)}) collective-permute-start(f32[2,4,4,256,128]{4,3,2,1,0:T(8,128)S(1)} %partial_other.2), channel_id=1, source_target_pairs={{0,16},{16,0},{1,17},{17,1},{2,18},{18,2},{3,19},{19,3},{4,20},{20... | collective-permute-start | bytes 12582920 | tf_op jit(solution)/shard_map/ppermute | solution.py:254
  65.1 11.5 %collective-permute-start.2 = (f32[2,4,4,256,128]{4,3,2,1,0:T(8,128)S(1)}, f32[2,4,4,256,128]{4,3,2,1,0:T(8,128)S(1)}, u32[]{:S(2)}, u32[]{:S(2)}) collective-permute-start(f32[2,4,4,256,128]{4,3,2,1,0:T(8,128)S(1)} %partial_other.3), channel_id=1, source_target_pairs={{0,16},{16,0},{1,17},{17,1},{2,18},{18,2},{3,19},{19,3},{4,20},{20... | collective-permute-start | bytes 12582920 | tf_op jit(solution)/shard_map/ppermute | solution.py:254
  73.2 12.6 %collective-permute-start.11 = (f32[2,4,80,128]{3,2,1,0:T(8,128)S(1)}, f32[2,4,80,128]{3,2,1,0:T(8,128)S(1)}, u32[]{:S(2)}, u32[]{:S(2)}) collective-permute-start(f32[2,4,80,128]{3,2,1,0:T(8,128)S(1)} %get-tuple-element.60), channel_id=1, source_target_pairs={{0,1},{1,2},{2,3},{3,0},{4,5},{5,6},{6,7},{7,4},{8,9},{9,10},{10,1... | collective-permute-start | bytes 983048 | tf_op jit(solution)/shard_map/ppermute | solution.py:246
  73.6 16.0 %collective-permute-start.13 = (f32[2,4,80,128]{3,2,1,0:T(8,128)S(1)}, f32[2,4,80,128]{3,2,1,0:T(8,128)S(1)}, u32[]{:S(2)}, u32[]{:S(2)}) collective-permute-start(f32[2,4,80,128]{3,2,1,0:T(8,128)S(1)} %get-tuple-element.62), channel_id=1, source_target_pairs={{0,2},{1,3},{2,0},{3,1},{4,6},{5,7},{6,4},{7,5},{8,10},{9,11},{10,... | collective-permute-start | bytes 983048 | tf_op jit(solution)/shard_map/ppermute | solution.py:246
  75.2 15.7 %collective-permute-start.15 = (f32[2,4,80,128]{3,2,1,0:T(8,128)S(1)}, f32[2,4,80,128]{3,2,1,0:T(8,128)S(1)}, u32[]{:S(2)}, u32[]{:S(2)}) collective-permute-start(f32[2,4,80,128]{3,2,1,0:T(8,128)S(1)} %get-tuple-element.64), channel_id=1, source_target_pairs={{0,3},{1,0},{2,1},{3,2},{4,7},{5,4},{6,5},{7,6},{8,11},{9,8},{10,9... | collective-permute-start | bytes 983048 | tf_op jit(solution)/shard_map/ppermute | solution.py:246
  76.1 32.1 %collective-permute-start.5 = (f32[4,2,88,128]{3,2,1,0:T(8,128)S(1)}, f32[4,2,88,128]{3,2,1,0:T(8,128)S(1)}, u32[]{:S(2)}, u32[]{:S(2)}) collective-permute-start(f32[4,2,88,128]{3,2,1,0:T(8,128)S(1)} %get-tuple-element.52), channel_id=1, source_target_pairs={{0,4},{4,8},{8,12},{12,0},{1,5},{5,9},{9,13},{13,1},{2,6},{6,10},{... | collective-permute-start | bytes 1081352 | tf_op jit(solution)/shard_map/ppermute | solution.py:246
  76.6 33.2 %collective-permute-start.7 = (f32[4,2,88,128]{3,2,1,0:T(8,128)S(1)}, f32[4,2,88,128]{3,2,1,0:T(8,128)S(1)}, u32[]{:S(2)}, u32[]{:S(2)}) collective-permute-start(f32[4,2,88,128]{3,2,1,0:T(8,128)S(1)} %get-tuple-element.54), channel_id=1, source_target_pairs={{0,8},{4,12},{8,0},{12,4},{1,9},{5,13},{9,1},{13,5},{2,10},{6,14},... | collective-permute-start | bytes 1081352 | tf_op jit(solution)/shard_map/ppermute | solution.py:246
  85.7 9.6 %collective-permute-start.12 = (f32[2,4,80,128]{3,2,1,0:T(8,128)S(1)}, f32[2,4,80,128]{3,2,1,0:T(8,128)S(1)}, u32[]{:S(2)}, u32[]{:S(2)}) collective-permute-start(f32[2,4,80,128]{3,2,1,0:T(8,128)S(1)} %get-tuple-element.61), channel_id=1, source_target_pairs={{0,1},{1,2},{2,3},{3,0},{4,5},{5,6},{6,7},{7,4},{8,9},{9,10},{10,1... | collective-permute-start | bytes 983048 | tf_op jit(solution)/shard_map/ppermute | solution.py:246
  89.6 11.2 %collective-permute-start.14 = (f32[2,4,80,128]{3,2,1,0:T(8,128)S(1)}, f32[2,4,80,128]{3,2,1,0:T(8,128)S(1)}, u32[]{:S(2)}, u32[]{:S(2)}) collective-permute-start(f32[2,4,80,128]{3,2,1,0:T(8,128)S(1)} %get-tuple-element.63), channel_id=1, source_target_pairs={{0,2},{1,3},{2,0},{3,1},{4,6},{5,7},{6,4},{7,5},{8,10},{9,11},{10,... | collective-permute-start | bytes 983048 | tf_op jit(solution)/shard_map/ppermute | solution.py:246
  90.9 13.3 %collective-permute-start.16 = (f32[2,4,80,128]{3,2,1,0:T(8,128)S(1)}, f32[2,4,80,128]{3,2,1,0:T(8,128)S(1)}, u32[]{:S(2)}, u32[]{:S(2)}) collective-permute-start(f32[2,4,80,128]{3,2,1,0:T(8,128)S(1)} %get-tuple-element.65), channel_id=1, source_target_pairs={{0,3},{1,0},{2,1},{3,2},{4,7},{5,4},{6,5},{7,6},{8,11},{9,8},{10,9... | collective-permute-start | bytes 983048 | tf_op jit(solution)/shard_map/ppermute | solution.py:246
  95.4 19.6 %collective-permute-start.9 = (f32[4,2,88,128]{3,2,1,0:T(8,128)S(1)}, f32[4,2,88,128]{3,2,1,0:T(8,128)S(1)}, u32[]{:S(2)}, u32[]{:S(2)}) collective-permute-start(f32[4,2,88,128]{3,2,1,0:T(8,128)S(1)} %get-tuple-element.56), channel_id=1, source_target_pairs={{0,12},{4,0},{8,4},{12,8},{1,13},{5,1},{9,5},{13,9},{2,14},{6,2},{... | collective-permute-start | bytes 1081352 | tf_op jit(solution)/shard_map/ppermute | solution.py:246
  100.8 30.5 %collective-permute-start.1 = (f32[4,4,88,128]{3,2,1,0:T(8,128)S(1)}, f32[4,4,88,128]{3,2,1,0:T(8,128)S(1)}, u32[]{:S(2)}, u32[]{:S(2)}) collective-permute-start(f32[4,4,88,128]{3,2,1,0:T(8,128)S(1)} %get-tuple-element.47), channel_id=1, source_target_pairs={{0,32},{32,64},{64,96},{96,0},{1,33},{33,65},{65,97},{97,1},{2,34}... | collective-permute-start | bytes 2162696 | tf_op jit(solution)/shard_map/ppermute | solution.py:246
  104.3 11.4 %collective-permute-start.6 = (f32[4,2,88,128]{3,2,1,0:T(8,128)S(1)}, f32[4,2,88,128]{3,2,1,0:T(8,128)S(1)}, u32[]{:S(2)}, u32[]{:S(2)}) collective-permute-start(f32[4,2,88,128]{3,2,1,0:T(8,128)S(1)} %get-tuple-element.53), channel_id=1, source_target_pairs={{0,4},{4,8},{8,12},{12,0},{1,5},{5,9},{9,13},{13,1},{2,6},{6,10},{... | collective-permute-start | bytes 1081352 | tf_op jit(solution)/shard_map/ppermute | solution.py:246
  108.2 30.8 %collective-permute-start.3 = (f32[4,4,88,128]{3,2,1,0:T(8,128)S(1)}, f32[4,4,88,128]{3,2,1,0:T(8,128)S(1)}, u32[]{:S(2)}, u32[]{:S(2)}) collective-permute-start(f32[4,4,88,128]{3,2,1,0:T(8,128)S(1)} %get-tuple-element.48), channel_id=1, source_target_pairs={{0,64},{32,96},{64,0},{96,32},{1,65},{33,97},{65,1},{97,33},{2,66}... | collective-permute-start | bytes 2162696 | tf_op jit(solution)/shard_map/ppermute | solution.py:246
  109.8 32.2 %collective-permute-start.4 = (f32[4,4,88,128]{3,2,1,0:T(8,128)S(1)}, f32[4,4,88,128]{3,2,1,0:T(8,128)S(1)}, u32[]{:S(2)}, u32[]{:S(2)}) collective-permute-start(f32[4,4,88,128]{3,2,1,0:T(8,128)S(1)} %get-tuple-element.49), channel_id=1, source_target_pairs={{0,96},{32,0},{64,32},{96,64},{1,97},{33,1},{65,33},{97,65},{2,98}... | collective-permute-start | bytes 2162696 | tf_op jit(solution)/shard_map/ppermute | solution.py:246
  114.9 9.3 %collective-permute-start.8 = (f32[4,2,88,128]{3,2,1,0:T(8,128)S(1)}, f32[4,2,88,128]{3,2,1,0:T(8,128)S(1)}, u32[]{:S(2)}, u32[]{:S(2)}) collective-permute-start(f32[4,2,88,128]{3,2,1,0:T(8,128)S(1)} %get-tuple-element.55), channel_id=1, source_target_pairs={{0,8},{4,12},{8,0},{12,4},{1,9},{5,13},{9,1},{13,5},{2,10},{6,14},... | collective-permute-start | bytes 1081352 | tf_op jit(solution)/shard_map/ppermute | solution.py:246
  115.7 15.6 %collective-permute-start.10 = (f32[4,2,88,128]{3,2,1,0:T(8,128)S(1)}, f32[4,2,88,128]{3,2,1,0:T(8,128)S(1)}, u32[]{:S(2)}, u32[]{:S(2)}) collective-permute-start(f32[4,2,88,128]{3,2,1,0:T(8,128)S(1)} %get-tuple-element.57), channel_id=1, source_target_pairs={{0,12},{4,0},{8,4},{12,8},{1,13},{5,1},{9,5},{13,9},{2,14},{6,2},{... | collective-permute-start | bytes 1081352 | tf_op jit(solution)/shard_map/ppermute | solution.py:246
  142.4 15.2 %collective-permute-start.17 = (f32[4,88,128]{2,1,0:T(8,128)S(1)}, f32[4,88,128]{2,1,0:T(8,128)S(1)}, u32[]{:S(2)}, u32[]{:S(2)}) collective-permute-start(f32[4,88,128]{2,1,0:T(8,128)S(1)} %get-tuple-element.67), channel_id=1, source_target_pairs={{0,4},{4,8},{8,12},{12,0},{1,5},{5,9},{9,13},{13,1},{2,6},{6,10},{... | collective-permute-start | bytes 540680 | tf_op jit(solution)/shard_map/ppermute | solution.py:246
  143.6 6.4 %collective-permute-start.23 = (f32[4,80,128]{2,1,0:T(8,128)S(1)}, f32[4,80,128]{2,1,0:T(8,128)S(1)}, u32[]{:S(2)}, u32[]{:S(2)}) collective-permute-start(f32[4,80,128]{2,1,0:T(8,128)S(1)} %get-tuple-element.75), channel_id=1, source_target_pairs={{0,32},{32,64},{64,96},{96,0},{1,33},{33,65},{65,97},{97,1},{2,34}... | collective-permute-start | bytes 491528 | tf_op jit(solution)/shard_map/ppermute | solution.py:246
  145.1 9.9 %collective-permute-start.24 = (f32[4,80,128]{2,1,0:T(8,128)S(1)}, f32[4,80,128]{2,1,0:T(8,128)S(1)}, u32[]{:S(2)}, u32[]{:S(2)}) collective-permute-start(f32[4,80,128]{2,1,0:T(8,128)S(1)} %get-tuple-element.76), channel_id=1, source_target_pairs={{0,64},{32,96},{64,0},{96,32},{1,65},{33,97},{65,1},{97,33},{2,66}... | collective-permute-start | bytes 491528 | tf_op jit(solution)/shard_map/ppermute | solution.py:246
  148.2 6.8 %collective-permute-start.25 = (f32[4,80,128]{2,1,0:T(8,128)S(1)}, f32[4,80,128]{2,1,0:T(8,128)S(1)}, u32[]{:S(2)}, u32[]{:S(2)}) collective-permute-start(f32[4,80,128]{2,1,0:T(8,128)S(1)} %get-tuple-element.77), channel_id=1, source_target_pairs={{0,96},{32,0},{64,32},{96,64},{1,97},{33,1},{65,33},{97,65},{2,98}... | collective-permute-start | bytes 491528 | tf_op jit(solution)/shard_map/ppermute | solution.py:246
  148.2 9.6 %collective-permute-start.18 = (f32[4,88,128]{2,1,0:T(8,128)S(1)}, f32[4,88,128]{2,1,0:T(8,128)S(1)}, u32[]{:S(2)}, u32[]{:S(2)}) collective-permute-start(f32[4,88,128]{2,1,0:T(8,128)S(1)} %get-tuple-element.68), channel_id=1, source_target_pairs={{0,8},{4,12},{8,0},{12,4},{1,9},{5,13},{9,1},{13,5},{2,10},{6,14},... | collective-permute-start | bytes 540680 | tf_op jit(solution)/shard_map/ppermute | solution.py:246
  150.0 7.8 %collective-permute-start.19 = (f32[4,88,128]{2,1,0:T(8,128)S(1)}, f32[4,88,128]{2,1,0:T(8,128)S(1)}, u32[]{:S(2)}, u32[]{:S(2)}) collective-permute-start(f32[4,88,128]{2,1,0:T(8,128)S(1)} %get-tuple-element.69), channel_id=1, source_target_pairs={{0,12},{4,0},{8,4},{12,8},{1,13},{5,1},{9,5},{13,9},{2,14},{6,2},{... | collective-permute-start | bytes 540680 | tf_op jit(solution)/shard_map/ppermute | solution.py:246
  155.0 5.6 %collective-permute-start.20 = (f32[4,88,128]{2,1,0:T(8,128)S(1)}, f32[4,88,128]{2,1,0:T(8,128)S(1)}, u32[]{:S(2)}, u32[]{:S(2)}) collective-permute-start(f32[4,88,128]{2,1,0:T(8,128)S(1)} %get-tuple-element.71), channel_id=1, source_target_pairs={{0,1},{1,2},{2,3},{3,0},{4,5},{5,6},{6,7},{7,4},{8,9},{9,10},{10,1... | collective-permute-start | bytes 540680 | tf_op jit(solution)/shard_map/ppermute | solution.py:246
  155.0 9.2 %collective-permute-start.21 = (f32[4,88,128]{2,1,0:T(8,128)S(1)}, f32[4,88,128]{2,1,0:T(8,128)S(1)}, u32[]{:S(2)}, u32[]{:S(2)}) collective-permute-start(f32[4,88,128]{2,1,0:T(8,128)S(1)} %get-tuple-element.72), channel_id=1, source_target_pairs={{0,2},{1,3},{2,0},{3,1},{4,6},{5,7},{6,4},{7,5},{8,10},{9,11},{10,... | collective-permute-start | bytes 540680 | tf_op jit(solution)/shard_map/ppermute | solution.py:246
  157.6 7.5 %collective-permute-start.22 = (f32[4,88,128]{2,1,0:T(8,128)S(1)}, f32[4,88,128]{2,1,0:T(8,128)S(1)}, u32[]{:S(2)}, u32[]{:S(2)}) collective-permute-start(f32[4,88,128]{2,1,0:T(8,128)S(1)} %get-tuple-element.73), channel_id=1, source_target_pairs={{0,3},{1,0},{2,1},{3,2},{4,7},{5,4},{6,5},{7,6},{8,11},{9,8},{10,9... | collective-permute-start | bytes 540680 | tf_op jit(solution)/shard_map/ppermute | solution.py:246
  165.2 0.6 copy-start.2
  165.9 0.6 copy-start.3
  166.5 0.6 copy-start.4
  167.1 10.8 %collective-permute-start.26 = (f32[88,128]{1,0:T(8,128)S(1)}, f32[88,128]{1,0:T(8,128)S(1)}, u32[]{:S(2)}, u32[]{:S(2)}) collective-permute-start(f32[88,128]{1,0:T(8,128)S(1)} %get-tuple-element.79), channel_id=1, source_target_pairs={{0,1},{1,2},{2,3},{3,0},{4,5},{5,6},{6,7},{7,4},{8,9},{9,10},{10,1... | collective-permute-start | bytes 135176 | tf_op jit(solution)/shard_map/ppermute | solution.py:246
  167.7 7.5 %collective-permute-start.32 = (f32[80,128]{1,0:T(8,128)S(1)}, f32[80,128]{1,0:T(8,128)S(1)}, u32[]{:S(2)}, u32[]{:S(2)}) collective-permute-start(f32[80,128]{1,0:T(8,128)S(1)} %get-tuple-element.87), channel_id=1, source_target_pairs={{0,4},{4,8},{8,12},{12,0},{1,5},{5,9},{9,13},{13,1},{2,6},{6,10},{... | collective-permute-start | bytes 122888 | tf_op jit(solution)/shard_map/ppermute | solution.py:246
  167.9 7.3 %collective-permute-start.33 = (f32[80,128]{1,0:T(8,128)S(1)}, f32[80,128]{1,0:T(8,128)S(1)}, u32[]{:S(2)}, u32[]{:S(2)}) collective-permute-start(f32[80,128]{1,0:T(8,128)S(1)} %get-tuple-element.88), channel_id=1, source_target_pairs={{0,8},{4,12},{8,0},{12,4},{1,9},{5,13},{9,1},{13,5},{2,10},{6,14},... | collective-permute-start | bytes 122888 | tf_op jit(solution)/shard_map/ppermute | solution.py:246
  170.8 4.7 %collective-permute-start.34 = (f32[80,128]{1,0:T(8,128)S(1)}, f32[80,128]{1,0:T(8,128)S(1)}, u32[]{:S(2)}, u32[]{:S(2)}) collective-permute-start(f32[80,128]{1,0:T(8,128)S(1)} %get-tuple-element.89), channel_id=1, source_target_pairs={{0,12},{4,0},{8,4},{12,8},{1,13},{5,1},{9,5},{13,9},{2,14},{6,2},{... | collective-permute-start | bytes 122888 | tf_op jit(solution)/shard_map/ppermute | solution.py:246
  171.0 7.1 %collective-permute-start.27 = (f32[88,128]{1,0:T(8,128)S(1)}, f32[88,128]{1,0:T(8,128)S(1)}, u32[]{:S(2)}, u32[]{:S(2)}) collective-permute-start(f32[88,128]{1,0:T(8,128)S(1)} %get-tuple-element.80), channel_id=1, source_target_pairs={{0,2},{1,3},{2,0},{3,1},{4,6},{5,7},{6,4},{7,5},{8,10},{9,11},{10,... | collective-permute-start | bytes 135176 | tf_op jit(solution)/shard_map/ppermute | solution.py:246
  175.2 5.8 %copy-start.11 = (f32[80,128]{1,0:T(8,128)}, f32[80,128]{1,0:T(8,128)S(1)}, u32[]{:S(2)}) copy-start(f32[80,128]{1,0:T(8,128)S(1)} %collective-permute-done.32.refs_9_) | copy-start | bytes 122884
  175.2 3.2 collective-permute-start.28
  175.2 5.8 %copy-start.12 = (f32[80,128]{1,0:T(8,128)}, f32[80,128]{1,0:T(8,128)S(1)}, u32[]{:S(2)}) copy-start(f32[80,128]{1,0:T(8,128)S(1)} %collective-permute-done.33.refs_10_) | copy-start | bytes 122884
  175.2 4.2 %collective-permute-start.29 = (f32[88,128]{1,0:T(8,128)S(1)}, f32[88,128]{1,0:T(8,128)S(1)}, u32[]{:S(2)}, u32[]{:S(2)}) collective-permute-start(f32[88,128]{1,0:T(8,128)S(1)} %get-tuple-element.83), channel_id=1, source_target_pairs={{0,32},{32,64},{64,96},{96,0},{1,33},{33,65},{65,97},{97,1},{2,34}... | collective-permute-start | bytes 135176 | tf_op jit(solution)/shard_map/ppermute | solution.py:246
  175.5 5.5 %copy-start.13 = (f32[80,128]{1,0:T(8,128)}, f32[80,128]{1,0:T(8,128)S(1)}, u32[]{:S(2)}) copy-start(f32[80,128]{1,0:T(8,128)S(1)} %collective-permute-done.34.refs_11_) | copy-start | bytes 122884
  175.5 4.4 %collective-permute-start.30 = (f32[88,128]{1,0:T(8,128)S(1)}, f32[88,128]{1,0:T(8,128)S(1)}, u32[]{:S(2)}, u32[]{:S(2)}) collective-permute-start(f32[88,128]{1,0:T(8,128)S(1)} %get-tuple-element.84), channel_id=1, source_target_pairs={{0,64},{32,96},{64,0},{96,32},{1,65},{33,97},{65,1},{97,33},{2,66}... | collective-permute-start | bytes 135176 | tf_op jit(solution)/shard_map/ppermute | solution.py:246
  177.9 3.1 copy-start.5
  177.9 3.1 collective-permute-start.31
  178.1 2.9 copy-start.6
  178.4 2.6 copy-start.7
  179.4 1.6 copy-start.8
  179.9 1.1 copy-start.9
  181.0 0.6 copy-start.10
  268.3 1.6 copy-start.1
Sparse Core Ops, SparseCore 0:
  183.5 83.6 all-gather.2

commit v4 on v3

--- a/solution.py
+++ b/solution.py
@@ -16,8 +16,9 @@
 
 LANES = 128
 BLOCK_ROWS = 264
+IN_FLIGHT = 5
 CHAINS = 8
-PARTS = ((0, 88), (88, 176), (176, 256))
+PART_ROWS = 88
 
 bf16 = jnp.bfloat16
 f32 = jnp.float32
@@ -59,7 +60,11 @@
     return halves[:, :LANES] + (cross + cross.T)
 
 
-def list_kernel(ids_c_ref, ids_r_ref, gram_ref, out_ref, *, slots, rows_dev):
+def list_kernel(history_ref, positive_ref, out_ref, *, slots, rows_dev):
+    ids_r = jnp.concatenate(
+        [history_ref[...], positive_ref[...], jnp.zeros((LANES - slots, LANES), i32)], axis=0
+    )
+    ids_c = ids_r.T
     sq = (LANES, LANES)
     lane = iota2(sq, 1)
     sub = iota2(sq, 0)
@@ -72,13 +77,13 @@
     carry = jnp.zeros(sq, f32)
     acc = jnp.zeros((3 * LANES, LANES), f32)
     for h in range(slots):
-        owner_c = ids_c_ref[:, h : h + 1] // rows_dev
+        owner_c = ids_c[:, h : h + 1] // rows_dev
         member = owner_c == lane
         counts = dot_f32(lower, jnp.where(member, one, zero).astype(bf16))
         mine = jnp.where(member, counts[:LANES] + carry, zero).astype(bf16)
         rank = dot_f32(mine, ones)
         place = jnp.where(rank == lane_f, one, zero).astype(bf16)
-        ids = ids_r_ref[h : h + 1, :]
+        ids = ids_r[h : h + 1, :]
         local = ids % rows_dev
         at_owner = ids // rows_dev == sub
         high = (local // 64 + 1).astype(f32)
@@ -101,26 +106,26 @@
     code = jnp.where(present, code, -1)
     out_ref[:, 0, :] = jnp.where(present, (high - 1) * 64 + low, rows_dev).astype(f32)
     out_ref[:, 1, :] = code.astype(f32)
-    out_ref[:, 2, :] = gram_ref[...]
-    out_ref[:, 3, :] = zero
-
-
-def request_lists(ids_c, ids_r, gram, rows_dev, slots):
+
+
+def request_lists(history_ids, positive_ids, rows_dev):
+    users, hist_len = history_ids.shape
     return pl.pallas_call(
-        functools.partial(list_kernel, slots=slots, rows_dev=rows_dev),
-        out_shape=jax.ShapeDtypeStruct((LANES, 4, LANES), f32),
+        functools.partial(list_kernel, slots=hist_len + 1, rows_dev=rows_dev),
+        out_shape=jax.ShapeDtypeStruct((LANES, 2, LANES), f32),
         name="request_lists",
-    )(ids_c, ids_r, gram)
-
-
-def partial_kernel(rows_ref, here_ref, table_ref, codes_ref, *refs, half, other_core):
+    )(history_ids.T, positive_ids.reshape(1, users))
+
+
+def partial_kernel(rows_ref, here_ref, table_ref, codes_ref, gram_ref, *refs, half, other_core):
     if other_core:
-        (out_ref,) = refs[:1]
+        out_ref = refs[0]
         scratch = refs[1:]
     else:
         from_ref = refs[0]
-        outs = refs[1:11]
-        scratch = refs[11:]
+        earlier = refs[1 : 1 + 8 * half]
+        outs = refs[1 + 8 * half : 11 + 8 * half]
+        scratch = refs[11 + 8 * half :]
     picked_refs, block_refs = scratch[:4], scratch[4:]
     dx = pl.program_id(0)
     dz = pl.program_id(1)
@@ -145,52 +150,69 @@
             jnp.concatenate([weight, weight], axis=1),
             jnp.concatenate(split2(picked_ref[...]), axis=0),
         )
+        gram = jnp.broadcast_to(gram_ref[pl.ds(source, 1), :], (8, LANES))
         if other_core:
-            out_ref[0, 0, dy] = block
+            out_ref[0, 0, dy, : 2 * LANES, :] = block
+            out_ref[0, 0, dy, 2 * LANES :, :] = gram
         else:
-            block_refs[dy][...] = block + from_ref[0, 0, dy]
+            block_refs[dy][: 2 * LANES, :] = block + from_ref[0, 0, dy, : 2 * LANES, :]
+            block_refs[dy][2 * LANES :, :] = gram + from_ref[0, 0, dy, 2 * LANES :, :]
     if other_core:
         return
-    (a0, a1), (b0, b1), (c0, c1) = PARTS
+    n = PART_ROWS
     for i in range(2):
 
         @pl.when(dx == i)
         def _(i=i):
             for dy in range(4):
-                outs[i][dz, dy] = block_refs[dy][a0:a1, :]
+                outs[i][dz, dy] = block_refs[dy][:n, :]
 
     for j in range(4):
 
         @pl.when(dz == j)
         def _(j=j):
             for dy in range(4):
-                outs[2 + j][dy, dx] = block_refs[dy][b0:b1, :]
+                outs[2 + j][dy, dx + 2 * half] = block_refs[dy][n : 2 * n, :]
 
     for dy in range(4):
-        outs[6 + dy][dx, dz] = block_refs[dy][c0:c1, :]
-
-
-def partial_sums(rows_idx, here, table, codes, half, received=None):
+        outs[6 + dy][dx + 2 * half, dz] = block_refs[dy][2 * n :, :]
+
+    if half:
+
+        @pl.when((dx == 0) & (dz == 0))
+        def _():
+            for j in range(4):
+                for k in range(4):
+                    for m in range(2):
+                        outs[2 + j][k, m] = earlier[j][k, m]
+                        outs[6 + j][m, k] = earlier[4 + j][m, k]
+
+
+def partial_sums(rows_idx, here, table, codes, gram, half, received=None, earlier=()):
     rows_dev, width = table.shape
     other_core = received is None
-    blocks = pl.BlockSpec((1, 1, 4, 2 * LANES, width), lambda dx, dz, r, h: (dx, dz, 0, 0, 0))
+    blocks = pl.BlockSpec((1, 1, 4, BLOCK_ROWS, width), lambda dx, dz, r, h: (dx, dz, 0, 0, 0))
 
     def whole(shape):
         return pl.BlockSpec(shape, lambda dx, dz, r, h: (0,) * len(shape))
 
-    in_specs = [whole((rows_dev, width)), whole(codes.shape)]
-    operands = (rows_idx, here, table, codes)
+    in_specs = [whole((rows_dev, width)), whole(codes.shape), whole(gram.shape)]
+    operands = (rows_idx, here, table, codes, gram)
     scratch = [pltpu.VMEM((LANES, width), f32)] * 4
     if other_core:
-        shapes = [(2, 4, 4, 2 * LANES, width)]
+        shapes = [(2, 4, 4, BLOCK_ROWS, width)]
         out_specs = [blocks]
     else:
-        in_specs.append(blocks)
-        operands += (received,)
-        la, lb, lc = (end - start for start, end in PARTS)
-        shapes = [(4, 4, la, width)] * 2 + [(4, 2, lb, width)] * 4 + [(2, 4, lc, width)] * 4
+        in_specs += [blocks] + [whole(piece.shape) for piece in earlier]
+        operands += (received, *earlier)
+        end = (PART_ROWS, width)
+        shapes = [(4, 4) + end] * 2
+        if half:
+            shapes += [(4, 4) + end] * 8
+        else:
+            shapes += [(4, 2) + end] * 4 + [(2, 4) + end] * 4
         out_specs = [whole(shape) for shape in shapes]
-        scratch = scratch + [pltpu.VMEM((2 * LANES, width), f32)] * 4
+        scratch = scratch + [pltpu.VMEM((BLOCK_ROWS, width), f32)] * 4
     return pl.pallas_call(
         functools.partial(partial_kernel, half=half, other_core=other_core),
         grid_spec=pltpu.PrefetchScalarGridSpec(
@@ -206,36 +228,20 @@
     )(*operands)
 
 
-def split_sum_kernel(*refs, halves):
-    at = 0
-    outs = refs[4 * sum(halves) :]
-    for part, n in enumerate(halves):
-        pieces = [refs[at + d * n : at + (d + 1) * n] for d in range(4)]
-        at += 4 * n
+def split_sum_kernel(*refs):
+    outs = refs[12:]
+    for part in range(3):
+        pieces = refs[4 * part : 4 * part + 4]
         for i in range(4):
-            out_ref = outs[4 * part + i]
-            if n == 1:
-                spots = [(0, i, slice(None))]
-            elif pieces[0][0].shape[0] == 2:
-                spots = [(i // 2, i % 2, slice(None))]
-            else:
-                spots = [(half, i, slice(2 * half, 2 * half + 2)) for half in range(2)]
-            for half, place, into in spots:
-                total = pieces[0][half][place] + pieces[1][half][place]
-                total = total + (pieces[2][half][place] + pieces[3][half][place])
-                out_ref[into] = total
+            total = (pieces[0][i] + pieces[1][i]) + (pieces[2][i] + pieces[3][i])
+            outs[4 * part + i][...] = total
 
 
 def split_sums(parts, name):
-    operands = [half for part in parts for pieces in part for half in pieces]
-    out_shape = [
-        jax.ShapeDtypeStruct((4,) * (part[0][0].ndim - 3) + part[0][0].shape[-2:], f32)
-        for part in parts
-        for _ in range(4)
-    ]
+    operands = [piece for part in parts for piece in part]
     outs = pl.pallas_call(
-        functools.partial(split_sum_kernel, halves=tuple(len(part[0]) for part in parts)),
-        out_shape=out_shape,
+        split_sum_kernel,
+        out_shape=[jax.ShapeDtypeStruct(operands[0].shape[1:], f32)] * 12,
         compiler_params=pltpu.CompilerParams(vmem_limit_bytes=40 * 2**20),
         name=name,
     )(*operands)
@@ -246,42 +252,40 @@
     return lax.ppermute(array, axis, [(i, (i + by) % 4) for i in range(4)])
 
 
-def to_sources(rows_idx, here, table, codes):
+def moved(parts, axes):
+    order = [(part, d) for d in (1, 3, 2) for part in range(3)]
+    results = [[part[0], None, None, None] for part in parts]
+    done = []
+    for k, (part, d) in enumerate(order):
+        piece = parts[part][d]
+        if k >= IN_FLIGHT:
+            piece, _ = lax.optimization_barrier((piece, done[k - IN_FLIGHT]))
+        done.append(shifted(piece, axes[part], d))
+        results[part][d] = done[-1]
+    return results
+
+
+def to_sources(rows_idx, here, table, codes, gram):
     swap = [(0, 1), (1, 0)]
-    received = []
-    for half in range(2):
-        (mine,) = partial_sums(rows_idx, here, table, codes, half)
-        received.append(lax.ppermute(mine, CORE, swap))
-    first, second, third = [[], [], [], []], [[], [], [], []], [[], [], [], []]
-    for half in range(2):
-        outs = partial_sums(rows_idx, here, table, codes, half, received[half])
-        for i in range(2):
-            d = 2 * half + i
-            first[d].append(outs[i] if d == 0 else shifted(outs[i], X, d))
-        for d in range(4):
-            second[d].append(outs[2 + d] if d == 0 else shifted(outs[2 + d], Z, d))
-            third[d].append(outs[6 + d] if d == 0 else shifted(outs[6 + d], Y, d))
-    first, second, third = split_sums([first, second, third], "sum_stage_1")
-    moved = [
-        [[piece if d == 0 else shifted(piece, axis, d)] for d, piece in enumerate(part)]
-        for part, axis in ((first, Z), (second, Y), (third, X))
-    ]
-    first, second, third = split_sums(moved, "sum_stage_2")
-    return [
-        [piece if d == 0 else shifted(piece, axis, d) for d, piece in enumerate(part)]
-        for part, axis in ((first, Y), (second, X), (third, Z))
-    ]
+    call = functools.partial(partial_sums, rows_idx, here, table, codes, gram)
+    received = [lax.ppermute(call(half)[0], CORE, swap) for half in range(2)]
+    early = call(0, received[0])
+    late = call(1, received[1], early[2:])
+    parts = [[early[0], early[1], late[0], late[1]], late[2:6], late[6:10]]
+    parts = split_sums(moved(parts, (X, Z, Y)), "sum_stage_1")
+    parts = split_sums(moved(parts, (Z, Y, X)), "sum_stage_2")
+    return moved(parts, (Y, X, Z))
 
 
 def user_kernel(*refs, hist_len):
-    total_ref, out_ref = refs[12:]
+    out_ref = refs[12]
     sums = []
     for part in range(3):
         piece = refs[4 * part : 4 * part + 4]
         sums.append((piece[0][...] + piece[1][...]) + (piece[2][...] + piece[3][...]))
     sums = jnp.concatenate(sums, axis=0)
     user = sums[:LANES] / hist_len
-    positive = sums[LANES:]
+    positive = sums[LANES : 2 * LANES]
     gap = jnp.sum(user * positive, axis=1, keepdims=True) - 1.0
     sq = (LANES, LANES)
     gap_row = jnp.sum(
@@ -295,17 +299,17 @@
     out_ref[2 * LANES :, :] = jnp.where(
         iota2(tail, 0) == 0,
         jnp.broadcast_to(gap_row, tail),
-        jnp.broadcast_to(total_ref[...], tail),
-    )
-
-
-def user_block(parts, total_row, hist_len):
-    width = total_row.shape[-1]
+        sums[2 * LANES :],
+    )
+
+
+def user_block(parts, hist_len):
+    pieces = [piece for part in parts for piece in part]
     return pl.pallas_call(
         functools.partial(user_kernel, hist_len=hist_len),
-        out_shape=jax.ShapeDtypeStruct((BLOCK_ROWS, width), f32),
+        out_shape=jax.ShapeDtypeStruct((BLOCK_ROWS, pieces[0].shape[-1]), f32),
         name="user_block",
-    )(*[piece for part in parts for piece in part], total_row)
+    )(*pieces)
 
 
 def update_kernel(
@@ -417,17 +421,15 @@
         precision=lax.Precision.HIGHEST,
         preferred_element_type=f32,
     )
-    ids = jnp.concatenate([history_ids, positive_ids[:, None]], axis=1)
-    lists = request_lists(ids, ids.T, item_gram, rows_dev, hist_len + 1)
+    lists = request_lists(history_ids, positive_ids, rows_dev)
     asked = lax.all_to_all(lists, DP_ROWS, split_axis=0, concat_axis=0, tiled=True)
     rows = asked[:, 0, :].astype(i32).reshape(-1)
     codes = asked[:, 1, :]
-    total_row = asked[:, 2, :].sum(axis=0, keepdims=True)
     place = jnp.arange(devices * LANES, dtype=i32) // LANES % 8 * (2 * LANES)
     src_idx = place + jnp.maximum(codes.astype(i32).reshape(-1), 0)
     here = jnp.stack([lax.axis_index(axis) for axis in DP_ROWS]).astype(i32)
-    parts = to_sources(jnp.where(rows < rows_dev, rows, 0), here, item_table, codes)
-    block = user_block(parts, total_row, hist_len)
+    parts = to_sources(jnp.where(rows < rows_dev, rows, 0), here, item_table, codes, item_gram)
+    block = user_block(parts, hist_len)
     blocks = lax.all_gather(block, DP_ROWS)
     item_total = blocks[:, 2 * LANES + 1, :]
     return update_rows(

time: 324 us -> 302 us (0.932)
  waiting for transfers between devices: 150 us -> 133 us
    ppermute x33 -> x27, waiting for transfers between devices: 55.1 us -> 34.2 us  [shifted(): return lax.ppermute(array, axis, [(i, (i + by) % 4) for i in range(4)])]
    all_gather x1, waiting for transfers between devices: 83.8 us -> 94.6 us  [shards(): blocks = lax.all_gather(block, DP_ROWS)]
    all_to_all x1, waiting for transfers between devices: 11.3 us -> 4.25 us  [shards(): lax.all_to_all(lists, DP_ROWS, split_axis=0, concat_axis=0, tiled=True)]
    ppermute x33 -> x27, starting transfers between devices: 42.2 us -> 39.6 us  [shifted(): return lax.ppermute(array, axis, [(i, (i + by) % 4) for i in range(4)])]
  transfers between devices with their start and end apart: 37 -> 31, of which waited for: 20 -> 16; matrix products, arithmetic and copies ran while one was open for 0% -> 2% of each run, Pallas kernels for 7% -> 8%
where the time goes in v4:
time: 302 us; the launch traced here: 301 us
  waiting for transfers between devices  133 us (44%)
  Pallas kernels  91 us (30%)
  starting transfers between devices  51.8 us (17%)
  between operations  14.3 us (5%)
  matrix products  5.8 us (2%)
  local copies, waits for them, and re-layouts  5.1 us (2%)
    all_gather x1, waiting for transfers between devices, shards(): blocks = lax.all_gather(block, DP_ROWS)  94.6 us
    pallas_call x1, Pallas kernels, update_rows(): pl.pallas_call(functools.partial(update_kernel, sources=sources, coef=coe...  46.3 us
    ppermute x27, starting transfers between devices, shifted(): return lax.ppermute(array, axis, [(i, (i + by) % 4) for i in range(4)])  39.6 us
    ppermute x27, waiting for transfers between devices, shifted(): return lax.ppermute(array, axis, [(i, (i + by) % 4) for i in range(4)])  34.2 us
    pallas_call x4, Pallas kernels, partial_sums(): pl.pallas_call(functools.partial(partial_kernel, half=half, other_core=ot...  33.1 us
    all_to_all x1, starting transfers between devices, shards(): lax.all_to_all(lists, DP_ROWS, split_axis=0, concat_axis=0, tiled=True)  11.5 us
    pallas_call x1, Pallas kernels, request_lists(): pl.pallas_call(functools.partial(list_kernel, slots=hist_len + 1, rows_de...  9.3 us
  transfers between devices with their start and end apart: 31, of which 16 were waited for; matrix products, arithmetic and copies ran while one was open for 2% of the time, Pallas kernels for 8%

profile of v4, /device:TPU:1, one launch (start us, length us, event | category | flops | bytes accessed | tf_op | source)
XLA Modules:
  0.0 301.3 jit_solution(3174277035774063774)
XLA Ops:
  7.2 9.3 %request_lists.1 = f32[128,2,128]{2,1,0:T(2,128)} custom-call(s32[50,128]{1,0:T(8,128)} %bitcast.28, s32[1,128]{1,0:T(1,128)} %bitcast.29), custom_call_target="tpu_custom_call" | custom-call | tf_op jit(solution)/shard_map/request_lists/pallas_call | solution.py:113
  16.5 11.5 %all-to-all-start = ((f32[128,2,128]{2,1,0:T(2,128)}), f32[128,2,128]{2,1,0:T(2,128)S(1)}, u32[]{:S(2)}, u32[]{:S(2)}) async-start(f32[128,2,128]{2,1,0:T(2,128)} %request_lists.1), calls=%async_computation | async-start | bytes 262144 | tf_op jit(solution)/shard_map/all_to_all | solution.py:425
  28.0 0.0 copy-start
  28.0 0.0 all-gather.3.cloned.1.call-start
  28.0 5.8 %fusion.7.gram_ref = f32[128,128]{1,0:T(8,128)S(1)} fusion(f32[4096,128]{1,0:T(8,128)} %table_ref.9), kind=kOutput, calls=%fused_computation.17 | convolution fusion | flops 805306368 | bytes 2162688 | tf_op jit(solution)/shard_map/dot_general | solution.py:418
  33.8 0.1 pad_add_fusion.here_ref
  33.9 4.2 %all-to-all-done = f32[128,2,128]{2,1,0:T(2,128)S(1)} async-done(((f32[128,2,128]{2,1,0:T(2,128)}), f32[128,2,128]{2,1,0:T(2,128)S(1)}, u32[]{:S(2)}, u32[]{:S(2)}) %all-to-all-start) | async-done | bytes 131104 | tf_op jit(solution)/shard_map/all_to_all | solution.py:425
  38.2 0.1 fusion.6
  38.3 7.5 %partial_other.2 = f32[2,4,4,264,128]{4,3,2,1,0:T(8,128)S(1)} custom-call(s32[16384]{0:T(1024)S(1)} %compare_select_fusion.rows_ref, s32[4]{0:T(128)S(1)} %pad_add_fusion.here_ref, f32[4096,128]{1,0:T(8,128)S(1)} %copy-done, f32[128,128]{1,0:T(8,128)S(1)} %bitcast.18, f32[128,128]{1,0:T(8,128)S(1)} %fusion.7.gram_ref), custom_call_target="tpu_custom_call" | custom-call | tf_op jit(solution)/shard_map/partial_other/pallas_call | solution.py:216
  45.8 0.5 collective-permute-start
  46.3 7.5 %partial_other.3 = f32[2,4,4,264,128]{4,3,2,1,0:T(8,128)S(1)} custom-call(s32[16384]{0:T(1024)S(1)} %compare_select_fusion.rows_ref, s32[4]{0:T(128)S(1)} %pad_add_fusion.here_ref, f32[4096,128]{1,0:T(8,128)S(1)} %copy-done, f32[128,128]{1,0:T(8,128)S(1)} %bitcast.19, f32[128,128]{1,0:T(8,128)S(1)} %fusion.7.gram_ref), custom_call_target="tpu_custom_call" | custom-call | tf_op jit(solution)/shard_map/partial_other/pallas_call | solution.py:216
  53.8 0.1 collective-permute-start.2
  53.9 8.0 %partial_own.2 = (f32[4,4,88,128]{3,2,1,0:T(8,128)S(1)}, f32[4,4,88,128]{3,2,1,0:T(8,128)S(1)}, f32[4,2,88,128]{3,2,1,0:T(8,128)S(1)}, f32[4,2,88,128]{3,2,1,0:T...) custom-call(s32[16384]{0:T(1024)S(1)} %compare_select_fusion.rows_re, ...), custom_call_target="tpu_custom_call" | custom-call | tf_op jit(solution)/shard_map/partial_own/pallas_call | solution.py:216
  61.9 0.6 collective-permute-start.1
  62.5 10.2 %partial_own.3 = (f32[4,4,88,128]{3,2,1,0:T(8,128)S(1)}, f32[4,4,88,128]{3,2,1,0:T(8,128)S(1)}, f32[4,4,88,128]{3,2,1,0:T(8,128)S(1)}, f32[4,4,88,128]{3,2,1,0:T...) custom-call(s32[16384]{0:T(1024)S(1)} %compare_select_fusion.rows_re, ...), custom_call_target="tpu_custom_call" | custom-call | tf_op jit(solution)/shard_map/partial_own/pallas_call | solution.py:216
  72.6 0.6 collective-permute-start.3
  73.2 2.4 collective-permute-start.5
  75.6 0.3 collective-permute-start.6
  75.9 2.1 collective-permute-start.8
  78.1 2.5 collective-permute-done.1.refs_1_
  80.6 0.8 collective-permute-start.10
  81.3 9.5 %collective-permute-done.3.refs_5_ = f32[4,4,88,128]{3,2,1,0:T(8,128)S(1)} collective-permute-done((f32[4,4,88,128]{3,2,1,0:T(8,128)S(1)}, f32[4,4,88,128]{3,2,1,0:T(8,128)S(1)}, u32[]{:S(2)}, u32[]{:S(2)}) %collective-permute-start.3) | collective-permute-done | bytes 720928 | tf_op jit(solution)/shard_map/ppermute | solution.py:252
  90.9 1.8 collective-permute-start.4
  92.7 0.8 collective-permute-start.9
  93.5 1.4 collective-permute-start.7
  94.9 2.0 collective-permute-done.10.refs_11_
  96.9 11.5 %collective-permute-done.4.refs_2_ = f32[4,4,88,128]{3,2,1,0:T(8,128)S(1)} collective-permute-done((f32[4,4,88,128]{3,2,1,0:T(8,128)S(1)}, f32[4,4,88,128]{3,2,1,0:T(8,128)S(1)}, u32[]{:S(2)}, u32[]{:S(2)}) %collective-permute-start.4) | collective-permute-done | bytes 720928 | tf_op jit(solution)/shard_map/ppermute | solution.py:252
  108.4 1.5 collective-permute-done.9.refs_10_
  109.9 0.6 collective-permute-done.7.refs_6_
  110.5 0.4 sum_stage_1.1
  110.9 0.1 collective-permute-start.11
  111.0 2.5 collective-permute-start.12
  113.5 2.4 collective-permute-start.14
  115.9 1.9 collective-permute-start.17
  117.9 2.7 collective-permute-start.19
  120.6 0.5 collective-permute-done.14.refs_3_
  121.1 0.4 collective-permute-done.15.refs_9_
  121.5 3.1 %collective-permute-start.16 = (f32[4,88,128]{2,1,0:T(8,128)S(1)}, f32[4,88,128]{2,1,0:T(8,128)S(1)}, u32[]{:S(2)}, u32[]{:S(2)}) collective-permute-start(f32[4,88,128]{2,1,0:T(8,128)S(1)} %get-tuple-element.91), channel_id=1, source_target_pairs={{0,2},{1,3},{2,0},{3,1},{4,6},{5,7},{6,4},{7,5},{8,10},{9,11},{10,... | collective-permute-start | bytes 540680 | tf_op jit(solution)/shard_map/ppermute | solution.py:252
  124.6 0.3 collective-permute-done.19.refs_11_
  124.9 1.5 collective-permute-done.13.refs_2_
  126.4 0.5 collective-permute-done.18.refs_10_
  126.9 0.7 collective-permute-done.16.refs_6_
  127.6 0.1 sum_stage_2.1
  127.7 0.6 copy-done.2
  128.3 0.6 copy-done.3
  128.9 0.6 copy-done.4
  129.6 0.2 collective-permute-start.20
  129.8 5.7 %collective-permute-start.21 = (f32[88,128]{1,0:T(8,128)S(1)}, f32[88,128]{1,0:T(8,128)S(1)}, u32[]{:S(2)}, u32[]{:S(2)}) collective-permute-start(f32[88,128]{1,0:T(8,128)S(1)} %get-tuple-element.101), channel_id=1, source_target_pairs={{0,32},{32,64},{64,96},{96,0},{1,33},{33,65},{65,97},{97,1},{2,34}... | collective-permute-start | bytes 135176 | tf_op jit(solution)/shard_map/ppermute | solution.py:252
  135.4 2.4 collective-permute-start.23
  137.8 1.1 collective-permute-start.26
  139.0 2.1 collective-permute-start.28
  141.0 1.6 collective-permute-start.22
  142.7 1.3 collective-permute-start.27
  144.0 1.7 collective-permute-start.25
  145.7 1.4 collective-permute-done.27.refs_10_
  147.1 1.3 collective-permute-done.25.refs_6_
  148.4 0.5 copy-done.13
  149.0 1.8 user_block.1
  150.8 0.0 all-gather.3.cloned.1.call-update
  150.8 94.6 %all-gather.3.cloned.1.call-done = f32[33792,128]{1,0:T(8,128)} async-done(((f32[264,128]{1,0:T(8,128)}), f32[33792,128]{1,0:T(8,128)}) %all-gather.3.cloned.1.call-update) | async-done | bytes 17301520 | tf_op jit(solution)/shard_map/all_gather | solution.py:433
  245.4 1.1 slice.14
  246.5 0.0 copy-start.1
  246.5 1.6 copy-done.1
  248.1 46.3 %update_rows.1 = (f32[4096,128]{1,0:T(8,128)}, f32[4096,128]{1,0:T(8,128)}) custom-call(s32[16384]{0:T(1024)S(1)} %bitcast.24, s32[16384]{0:T(1024)S(1)} %fusion.2.src_idx_ref, f32[128,264,128]{2,1,0:T(8,128)} %bitcast.27, f32[128,128]{1,0:T(8,128)S(1)} %bitcast.25, f32[4096,128]{1,0:T(8,128)S(1)} %copy-done, f32[4096,128]{1,0:T(8,128)S(1)} %copy-done.1), custom_call_target="tpu_custom_call" | custom-call | tf_op jit(solution)/shard_map/update_rows/pallas_call | solution.py:386
  (42 shorter events, 0.1 us)
Async XLA Ops:
  16.5 21.7 %all-to-all-start = ((f32[128,2,128]{2,1,0:T(2,128)}), f32[128,2,128]{2,1,0:T(2,128)S(1)}, u32[]{:S(2)}, u32[]{:S(2)}) async-start(f32[128,2,128]{2,1,0:T(2,128)} %request_lists.1), calls=%async_computation | async-start | bytes 262144 | tf_op jit(solution)/shard_map/all_to_all | solution.py:425
  28.0 10.3 %copy-start = (f32[4096,128]{1,0:T(8,128)S(1)}, f32[4096,128]{1,0:T(8,128)}, u32[]{:S(2)}) copy-start(f32[4096,128]{1,0:T(8,128)} %table_ref.9) | copy-start | bytes 6291460
  28.0 217.4 %all-gather.3.cloned.1.call-start = ((), (), s32[]{:S(2)}) async-start(), calls=%async_computation.1 | async-start | bytes 17436672 | tf_op jit(solution)/shard_map/all_gather | solution.py:433
  45.8 8.1 %collective-permute-start = (f32[2,4,4,264,128]{4,3,2,1,0:T(8,128)S(1)}, f32[2,4,4,264,128]{4,3,2,1,0:T(8,128)S(1)}, u32[]{:S(2)}, u32[]{:S(2)}) collective-permute-start(f32[2,4,4,264,128]{4,3,2,1,0:T(8,128)S(1)} %partial_other.2), channel_id=1, source_target_pairs={{0,16},{16,0},{1,17},{17,1},{2,18},{18,2},{3,19},{19,3},{4,20},{20... | collective-permute-start | bytes 12976136 | tf_op jit(solution)/shard_map/ppermute | solution.py:271
  53.8 8.7 %collective-permute-start.2 = (f32[2,4,4,264,128]{4,3,2,1,0:T(8,128)S(1)}, f32[2,4,4,264,128]{4,3,2,1,0:T(8,128)}, u32[]{:S(2)}, u32[]{:S(2)}) collective-permute-start(f32[2,4,4,264,128]{4,3,2,1,0:T(8,128)S(1)} %partial_other.3), channel_id=1, source_target_pairs={{0,16},{16,0},{1,17},{17,1},{2,18},{18,2},{3,19},{19,3},{4,20},{20... | collective-permute-start | bytes 12976136 | tf_op jit(solution)/shard_map/ppermute | solution.py:271
  61.9 18.7 %collective-permute-start.1 = (f32[4,4,88,128]{3,2,1,0:T(8,128)S(1)}, f32[4,4,88,128]{3,2,1,0:T(8,128)S(1)}, u32[]{:S(2)}, u32[]{:S(2)}) collective-permute-start(f32[4,4,88,128]{3,2,1,0:T(8,128)S(1)} %get-tuple-element.59), channel_id=1, source_target_pairs={{0,32},{32,64},{64,96},{96,0},{1,33},{33,65},{65,97},{97,1},{2,34}... | collective-permute-start | bytes 2162696 | tf_op jit(solution)/shard_map/ppermute | solution.py:252
  72.6 18.2 %collective-permute-start.3 = (f32[4,4,88,128]{3,2,1,0:T(8,128)S(1)}, f32[4,4,88,128]{3,2,1,0:T(8,128)S(1)}, u32[]{:S(2)}, u32[]{:S(2)}) collective-permute-start(f32[4,4,88,128]{3,2,1,0:T(8,128)S(1)} %get-tuple-element.69), channel_id=1, source_target_pairs={{0,4},{4,8},{8,12},{12,0},{1,5},{5,9},{9,13},{13,1},{2,6},{6,10},{... | collective-permute-start | bytes 2162696 | tf_op jit(solution)/shard_map/ppermute | solution.py:252
  73.2 19.4 %collective-permute-start.5 = (f32[4,4,88,128]{3,2,1,0:T(8,128)S(1)}, f32[4,4,88,128]{3,2,1,0:T(8,128)S(1)}, u32[]{:S(2)}, u32[]{:S(2)}) collective-permute-start(f32[4,4,88,128]{3,2,1,0:T(8,128)S(1)} %get-tuple-element.71), channel_id=1, source_target_pairs={{0,96},{32,0},{64,32},{96,64},{1,97},{33,1},{65,33},{97,65},{2,98}... | collective-permute-start | bytes 2162696 | tf_op jit(solution)/shard_map/ppermute | solution.py:252
  75.6 17.8 %collective-permute-start.6 = (f32[4,4,88,128]{3,2,1,0:T(8,128)S(1)}, f32[4,4,88,128]{3,2,1,0:T(8,128)S(1)}, u32[]{:S(2)}, u32[]{:S(2)}) collective-permute-start(f32[4,4,88,128]{3,2,1,0:T(8,128)S(1)} %get-tuple-element.74), channel_id=1, source_target_pairs={{0,1},{1,2},{2,3},{3,0},{4,5},{5,6},{6,7},{7,4},{8,9},{9,10},{10,1... | collective-permute-start | bytes 2162696 | tf_op jit(solution)/shard_map/ppermute | solution.py:252
  75.9 18.9 %collective-permute-start.8 = (f32[4,4,88,128]{3,2,1,0:T(8,128)S(1)}, f32[4,4,88,128]{3,2,1,0:T(8,128)S(1)}, u32[]{:S(2)}, u32[]{:S(2)}) collective-permute-start(f32[4,4,88,128]{3,2,1,0:T(8,128)S(1)} %get-tuple-element.76), channel_id=1, source_target_pairs={{0,12},{4,0},{8,4},{12,8},{1,13},{5,1},{9,5},{13,9},{2,14},{6,2},{... | collective-permute-start | bytes 2162696 | tf_op jit(solution)/shard_map/ppermute | solution.py:252
  80.6 16.3 %collective-permute-start.10 = (f32[4,4,88,128]{3,2,1,0:T(8,128)S(1)}, f32[4,4,88,128]{3,2,1,0:T(8,128)S(1)}, u32[]{:S(2)}, u32[]{:S(2)}) collective-permute-start(f32[4,4,88,128]{3,2,1,0:T(8,128)S(1)} %get-tuple-element.81), channel_id=1, source_target_pairs={{0,3},{1,0},{2,1},{3,2},{4,7},{5,4},{6,5},{7,6},{8,11},{9,8},{10,9... | collective-permute-start | bytes 2162696 | tf_op jit(solution)/shard_map/ppermute | solution.py:252
  90.9 17.5 %collective-permute-start.4 = (f32[4,4,88,128]{3,2,1,0:T(8,128)S(1)}, f32[4,4,88,128]{3,2,1,0:T(8,128)S(1)}, u32[]{:S(2)}, u32[]{:S(2)}) collective-permute-start(f32[4,4,88,128]{3,2,1,0:T(8,128)S(1)} %get-tuple-element.70), channel_id=1, source_target_pairs={{0,64},{32,96},{64,0},{96,32},{1,65},{33,97},{65,1},{97,33},{2,66}... | collective-permute-start | bytes 2162696 | tf_op jit(solution)/shard_map/ppermute | solution.py:252
  92.7 17.3 %collective-permute-start.9 = (f32[4,4,88,128]{3,2,1,0:T(8,128)S(1)}, f32[4,4,88,128]{3,2,1,0:T(8,128)S(1)}, u32[]{:S(2)}, u32[]{:S(2)}) collective-permute-start(f32[4,4,88,128]{3,2,1,0:T(8,128)S(1)} %get-tuple-element.79), channel_id=1, source_target_pairs={{0,2},{1,3},{2,0},{3,1},{4,6},{5,7},{6,4},{7,5},{8,10},{9,11},{10,... | collective-permute-start | bytes 2162696 | tf_op jit(solution)/shard_map/ppermute | solution.py:252
  93.5 17.0 %collective-permute-start.7 = (f32[4,4,88,128]{3,2,1,0:T(8,128)S(1)}, f32[4,4,88,128]{3,2,1,0:T(8,128)S(1)}, u32[]{:S(2)}, u32[]{:S(2)}) collective-permute-start(f32[4,4,88,128]{3,2,1,0:T(8,128)S(1)} %get-tuple-element.75), channel_id=1, source_target_pairs={{0,8},{4,12},{8,0},{12,4},{1,9},{5,13},{9,1},{13,5},{2,10},{6,14},... | collective-permute-start | bytes 2162696 | tf_op jit(solution)/shard_map/ppermute | solution.py:252
  110.9 7.0 %collective-permute-start.11 = (f32[4,88,128]{2,1,0:T(8,128)S(1)}, f32[4,88,128]{2,1,0:T(8,128)S(1)}, u32[]{:S(2)}, u32[]{:S(2)}) collective-permute-start(f32[4,88,128]{2,1,0:T(8,128)S(1)} %get-tuple-element.83), channel_id=1, source_target_pairs={{0,4},{4,8},{8,12},{12,0},{1,5},{5,9},{9,13},{13,1},{2,6},{6,10},{... | collective-permute-start | bytes 540680 | tf_op jit(solution)/shard_map/ppermute | solution.py:252
  111.0 9.6 %collective-permute-start.12 = (f32[4,88,128]{2,1,0:T(8,128)S(1)}, f32[4,88,128]{2,1,0:T(8,128)S(1)}, u32[]{:S(2)}, u32[]{:S(2)}) collective-permute-start(f32[4,88,128]{2,1,0:T(8,128)S(1)} %get-tuple-element.85), channel_id=1, source_target_pairs={{0,1},{1,2},{2,3},{3,0},{4,5},{5,6},{6,7},{7,4},{8,9},{9,10},{10,1... | collective-permute-start | bytes 540680 | tf_op jit(solution)/shard_map/ppermute | solution.py:252
  113.5 7.5 %collective-permute-start.14 = (f32[4,88,128]{2,1,0:T(8,128)S(1)}, f32[4,88,128]{2,1,0:T(8,128)S(1)}, u32[]{:S(2)}, u32[]{:S(2)}) collective-permute-start(f32[4,88,128]{2,1,0:T(8,128)S(1)} %get-tuple-element.87), channel_id=1, source_target_pairs={{0,12},{4,0},{8,4},{12,8},{1,13},{5,1},{9,5},{13,9},{2,14},{6,2},{... | collective-permute-start | bytes 540680 | tf_op jit(solution)/shard_map/ppermute | solution.py:252
  115.9 5.6 %collective-permute-start.15 = (f32[4,88,128]{2,1,0:T(8,128)S(1)}, f32[4,88,128]{2,1,0:T(8,128)S(1)}, u32[]{:S(2)}, u32[]{:S(2)}) collective-permute-start(f32[4,88,128]{2,1,0:T(8,128)S(1)} %get-tuple-element.90), channel_id=1, source_target_pairs={{0,32},{32,64},{64,96},{96,0},{1,33},{33,65},{65,97},{97,1},{2,34}... | collective-permute-start | bytes 540680 | tf_op jit(solution)/shard_map/ppermute | solution.py:252
  115.9 8.7 %collective-permute-start.17 = (f32[4,88,128]{2,1,0:T(8,128)S(1)}, f32[4,88,128]{2,1,0:T(8,128)S(1)}, u32[]{:S(2)}, u32[]{:S(2)}) collective-permute-start(f32[4,88,128]{2,1,0:T(8,128)S(1)} %get-tuple-element.92), channel_id=1, source_target_pairs={{0,3},{1,0},{2,1},{3,2},{4,7},{5,4},{6,5},{7,6},{8,11},{9,8},{10,9... | collective-permute-start | bytes 540680 | tf_op jit(solution)/shard_map/ppermute | solution.py:252
  117.9 7.0 %collective-permute-start.19 = (f32[4,88,128]{2,1,0:T(8,128)S(1)}, f32[4,88,128]{2,1,0:T(8,128)S(1)}, u32[]{:S(2)}, u32[]{:S(2)}) collective-permute-start(f32[4,88,128]{2,1,0:T(8,128)S(1)} %get-tuple-element.97), channel_id=1, source_target_pairs={{0,96},{32,0},{64,32},{96,64},{1,97},{33,1},{65,33},{97,65},{2,98}... | collective-permute-start | bytes 540680 | tf_op jit(solution)/shard_map/ppermute | solution.py:252
  120.6 5.9 %collective-permute-start.13 = (f32[4,88,128]{2,1,0:T(8,128)S(1)}, f32[4,88,128]{2,1,0:T(8,128)S(1)}, u32[]{:S(2)}, u32[]{:S(2)}) collective-permute-start(f32[4,88,128]{2,1,0:T(8,128)S(1)} %get-tuple-element.86), channel_id=1, source_target_pairs={{0,8},{4,12},{8,0},{12,4},{1,9},{5,13},{9,1},{13,5},{2,10},{6,14},... | collective-permute-start | bytes 540680 | tf_op jit(solution)/shard_map/ppermute | solution.py:252
  121.1 5.8 %collective-permute-start.18 = (f32[4,88,128]{2,1,0:T(8,128)S(1)}, f32[4,88,128]{2,1,0:T(8,128)S(1)}, u32[]{:S(2)}, u32[]{:S(2)}) collective-permute-start(f32[4,88,128]{2,1,0:T(8,128)S(1)} %get-tuple-element.95), channel_id=1, source_target_pairs={{0,64},{32,96},{64,0},{96,32},{1,65},{33,97},{65,1},{97,33},{2,66}... | collective-permute-start | bytes 540680 | tf_op jit(solution)/shard_map/ppermute | solution.py:252
  121.5 6.1 %collective-permute-start.16 = (f32[4,88,128]{2,1,0:T(8,128)S(1)}, f32[4,88,128]{2,1,0:T(8,128)S(1)}, u32[]{:S(2)}, u32[]{:S(2)}) collective-permute-start(f32[4,88,128]{2,1,0:T(8,128)S(1)} %get-tuple-element.91), channel_id=1, source_target_pairs={{0,2},{1,3},{2,0},{3,1},{4,6},{5,7},{6,4},{7,5},{8,10},{9,11},{10,... | collective-permute-start | bytes 540680 | tf_op jit(solution)/shard_map/ppermute | solution.py:252
  127.7 0.6 copy-start.2
  128.3 0.6 copy-start.3
  128.9 0.6 copy-start.4
  129.6 9.4 %collective-permute-start.20 = (f32[88,128]{1,0:T(8,128)S(1)}, f32[88,128]{1,0:T(8,128)S(1)}, u32[]{:S(2)}, u32[]{:S(2)}) collective-permute-start(f32[88,128]{1,0:T(8,128)S(1)} %get-tuple-element.99), channel_id=1, source_target_pairs={{0,1},{1,2},{2,3},{3,0},{4,5},{5,6},{6,7},{7,4},{8,9},{9,10},{10,1... | collective-permute-start | bytes 135176 | tf_op jit(solution)/shard_map/ppermute | solution.py:252
  129.8 11.3 %collective-permute-start.21 = (f32[88,128]{1,0:T(8,128)S(1)}, f32[88,128]{1,0:T(8,128)S(1)}, u32[]{:S(2)}, u32[]{:S(2)}) collective-permute-start(f32[88,128]{1,0:T(8,128)S(1)} %get-tuple-element.101), channel_id=1, source_target_pairs={{0,32},{32,64},{64,96},{96,0},{1,33},{33,65},{65,97},{97,1},{2,34}... | collective-permute-start | bytes 135176 | tf_op jit(solution)/shard_map/ppermute | solution.py:252
  135.4 7.2 %collective-permute-start.23 = (f32[88,128]{1,0:T(8,128)S(1)}, f32[88,128]{1,0:T(8,128)S(1)}, u32[]{:S(2)}, u32[]{:S(2)}) collective-permute-start(f32[88,128]{1,0:T(8,128)S(1)} %get-tuple-element.103), channel_id=1, source_target_pairs={{0,3},{1,0},{2,1},{3,2},{4,7},{5,4},{6,5},{7,6},{8,11},{9,8},{10,9... | collective-permute-start | bytes 135176 | tf_op jit(solution)/shard_map/ppermute | solution.py:252
  137.8 6.1 %collective-permute-start.24 = (f32[88,128]{1,0:T(8,128)S(1)}, f32[88,128]{1,0:T(8,128)S(1)}, u32[]{:S(2)}, u32[]{:S(2)}) collective-permute-start(f32[88,128]{1,0:T(8,128)S(1)} %get-tuple-element.106), channel_id=1, source_target_pairs={{0,4},{4,8},{8,12},{12,0},{1,5},{5,9},{9,13},{13,1},{2,6},{6,10},{... | collective-permute-start | bytes 135176 | tf_op jit(solution)/shard_map/ppermute | solution.py:252
  137.8 7.8 %collective-permute-start.26 = (f32[88,128]{1,0:T(8,128)S(1)}, f32[88,128]{1,0:T(8,128)S(1)}, u32[]{:S(2)}, u32[]{:S(2)}) collective-permute-start(f32[88,128]{1,0:T(8,128)S(1)} %get-tuple-element.108), channel_id=1, source_target_pairs={{0,96},{32,0},{64,32},{96,64},{1,97},{33,1},{65,33},{97,65},{2,98}... | collective-permute-start | bytes 135176 | tf_op jit(solution)/shard_map/ppermute | solution.py:252
  139.0 9.4 %copy-start.5 = (f32[88,128]{1,0:T(8,128)}, f32[88,128]{1,0:T(8,128)S(1)}, u32[]{:S(2)}) copy-start(f32[88,128]{1,0:T(8,128)S(1)} %collective-permute-done.20.refs_1_) | copy-start | bytes 135172
  139.0 6.7 %collective-permute-start.28 = (f32[88,128]{1,0:T(8,128)S(1)}, f32[88,128]{1,0:T(8,128)S(1)}, u32[]{:S(2)}, u32[]{:S(2)}) collective-permute-start(f32[88,128]{1,0:T(8,128)S(1)} %get-tuple-element.113), channel_id=1, source_target_pairs={{0,12},{4,0},{8,4},{12,8},{1,13},{5,1},{9,5},{13,9},{2,14},{6,2},{... | collective-permute-start | bytes 135176 | tf_op jit(solution)/shard_map/ppermute | solution.py:252
  141.0 7.3 %copy-start.6 = (f32[88,128]{1,0:T(8,128)}, f32[88,128]{1,0:T(8,128)S(1)}, u32[]{:S(2)}) copy-start(f32[88,128]{1,0:T(8,128)S(1)} %collective-permute-done.21.refs_5_) | copy-start | bytes 135172
  141.0 4.7 %collective-permute-start.22 = (f32[88,128]{1,0:T(8,128)S(1)}, f32[88,128]{1,0:T(8,128)S(1)}, u32[]{:S(2)}, u32[]{:S(2)}) collective-permute-start(f32[88,128]{1,0:T(8,128)S(1)} %get-tuple-element.102), channel_id=1, source_target_pairs={{0,2},{1,3},{2,0},{3,1},{4,6},{5,7},{6,4},{7,5},{8,10},{9,11},{10,... | collective-permute-start | bytes 135176 | tf_op jit(solution)/shard_map/ppermute | solution.py:252
  142.7 5.7 %copy-start.7 = (f32[88,128]{1,0:T(8,128)}, f32[88,128]{1,0:T(8,128)S(1)}, u32[]{:S(2)}) copy-start(f32[88,128]{1,0:T(8,128)S(1)} %collective-permute-done.23.refs_3_) | copy-start | bytes 135172
  142.7 4.4 %collective-permute-start.27 = (f32[88,128]{1,0:T(8,128)S(1)}, f32[88,128]{1,0:T(8,128)S(1)}, u32[]{:S(2)}, u32[]{:S(2)}) collective-permute-start(f32[88,128]{1,0:T(8,128)S(1)} %get-tuple-element.111), channel_id=1, source_target_pairs={{0,8},{4,12},{8,0},{12,4},{1,9},{5,13},{9,1},{13,5},{2,10},{6,14},... | collective-permute-start | bytes 135176 | tf_op jit(solution)/shard_map/ppermute | solution.py:252
  144.0 4.4 %copy-start.8 = (f32[88,128]{1,0:T(8,128)}, f32[88,128]{1,0:T(8,128)S(1)}, u32[]{:S(2)}) copy-start(f32[88,128]{1,0:T(8,128)S(1)} %collective-permute-done.24.refs_9_) | copy-start | bytes 135172
  144.0 4.4 %collective-permute-start.25 = (f32[88,128]{1,0:T(8,128)S(1)}, f32[88,128]{1,0:T(8,128)S(1)}, u32[]{:S(2)}, u32[]{:S(2)}) collective-permute-start(f32[88,128]{1,0:T(8,128)S(1)} %get-tuple-element.107), channel_id=1, source_target_pairs={{0,64},{32,96},{64,0},{96,32},{1,65},{33,97},{65,1},{97,33},{2,66}... | collective-permute-start | bytes 135176 | tf_op jit(solution)/shard_map/ppermute | solution.py:252
  145.7 2.7 copy-start.9
  145.7 2.7 copy-start.10
  145.7 2.7 copy-start.11
  147.1 1.3 copy-start.12
  148.4 0.6 copy-start.13
  246.5 1.6 copy-start.1
Sparse Core Ops, SparseCore 0:
  150.9 94.4 all-gather.2

commit v5 on v4

--- a/solution.py
+++ b/solution.py
@@ -10,15 +10,14 @@
 
 X, CORE, Z, Y = "x", "core", "z", "y"
 DP_ROWS = (X, CORE, Z, Y)
+ORDERS = ((0, 2, 3), (2, 3, 0))
 
 penalty_weight = 10.0
 step_size = 0.05
 
 LANES = 128
 BLOCK_ROWS = 264
-IN_FLIGHT = 5
-CHAINS = 8
-PART_ROWS = 88
+CHAINS = 4
 
 bf16 = jnp.bfloat16
 f32 = jnp.float32
@@ -117,173 +116,136 @@
     )(history_ids.T, positive_ids.reshape(1, users))
 
 
-def partial_kernel(rows_ref, here_ref, table_ref, codes_ref, gram_ref, *refs, half, other_core):
-    if other_core:
-        out_ref = refs[0]
-        scratch = refs[1:]
-    else:
-        from_ref = refs[0]
-        earlier = refs[1 : 1 + 8 * half]
-        outs = refs[1 + 8 * half : 11 + 8 * half]
-        scratch = refs[11 + 8 * half :]
-    picked_refs, block_refs = scratch[:4], scratch[4:]
-    dx = pl.program_id(0)
-    dz = pl.program_id(1)
-    at_x = (here_ref[0] + (dx + 2 * half)) & 3
-    at_core = here_ref[1] ^ 1 if other_core else here_ref[1]
-    at_z = (here_ref[2] + dz) & 3
+def partial_kernel(rows_ref, plane_ref, table_ref, codes_ref, gram_ref, *refs, first, first_step):
+    from_ref = refs[0] if len(refs) == 10 else None
+    out_ref = refs[-9]
+    picked_refs = refs[-8:]
     code_of = iota2((2 * LANES, LANES), 0).astype(f32)
     one = jnp.ones((2 * LANES, LANES), f32)
     zero = jnp.zeros((2 * LANES, LANES), f32)
     unroll = 32
-    for dy in range(4):
-        at_y = (here_ref[3] + dy) & 3
-        source = ((at_x * 2 + at_core) * 4 + at_z) * 4 + at_y
-        base = source * LANES
-        picked_ref = picked_refs[dy]
-        for at in range(0, LANES, unroll):
-            picked = [table_ref[pl.ds(rows_ref[base + (at + k)], 1), :] for k in range(unroll)]
-            for k in range(unroll):
-                picked_ref[at + k : at + k + 1, :] = picked[k]
-        weight = jnp.where(codes_ref[pl.ds(source, 1), :] == code_of, one, zero).astype(bf16)
-        block = dot_f32(
-            jnp.concatenate([weight, weight], axis=1),
-            jnp.concatenate(split2(picked_ref[...]), axis=0),
-        )
-        gram = jnp.broadcast_to(gram_ref[pl.ds(source, 1), :], (8, LANES))
-        if other_core:
-            out_ref[0, 0, dy, : 2 * LANES, :] = block
-            out_ref[0, 0, dy, 2 * LANES :, :] = gram
-        else:
-            block_refs[dy][: 2 * LANES, :] = block + from_ref[0, 0, dy, : 2 * LANES, :]
-            block_refs[dy][2 * LANES :, :] = gram + from_ref[0, 0, dy, 2 * LANES :, :]
-    if other_core:
-        return
-    n = PART_ROWS
-    for i in range(2):
-
-        @pl.when(dx == i)
-        def _(i=i):
-            for dy in range(4):
-                outs[i][dz, dy] = block_refs[dy][:n, :]
-
-    for j in range(4):
-
-        @pl.when(dz == j)
-        def _(j=j):
-            for dy in range(4):
-                outs[2 + j][dy, dx + 2 * half] = block_refs[dy][n : 2 * n, :]
-
-    for dy in range(4):
-        outs[6 + dy][dx + 2 * half, dz] = block_refs[dy][2 * n :, :]
-
-    if half:
-
-        @pl.when((dx == 0) & (dz == 0))
-        def _():
-            for j in range(4):
-                for k in range(4):
-                    for m in range(2):
-                        outs[2 + j][k, m] = earlier[j][k, m]
-                        outs[6 + j][m, k] = earlier[4 + j][m, k]
-
-
-def partial_sums(rows_idx, here, table, codes, gram, half, received=None, earlier=()):
+    offsets = (first + first_step * pl.program_id(0), 2 * pl.program_id(1))
+    at_first = ((plane_ref[1] + offsets[0]) & 3) * plane_ref[4]
+    for k in range(2):
+        at_second = ((plane_ref[2] + (offsets[1] + k)) & 3) * plane_ref[5]
+        for j in range(4):
+            at_third = ((plane_ref[3] + j) & 3) * plane_ref[6]
+            source = plane_ref[0] + at_first + at_second + at_third
+            base = source * LANES
+            picked_ref = picked_refs[4 * k + j]
+            for at in range(0, LANES, unroll):
+                picked = [
+                    table_ref[pl.ds(rows_ref[base + (at + i)], 1), :] for i in range(unroll)
+                ]
+                for i in range(unroll):
+                    picked_ref[at + i : at + i + 1, :] = picked[i]
+            weight = jnp.where(codes_ref[pl.ds(source, 1), :] == code_of, one, zero)
+            weight = weight.astype(bf16)
+            block = dot_f32(
+                jnp.concatenate([weight, weight], axis=1),
+                jnp.concatenate(split2(picked_ref[...]), axis=0),
+            )
+            gram = jnp.broadcast_to(gram_ref[pl.ds(source, 1), :], (8, LANES))
+            if from_ref is not None:
+                block = block + from_ref[0, k, j, : 2 * LANES, :]
+                gram = gram + from_ref[0, k, j, 2 * LANES :, :]
+            out_ref[0, k, j, : 2 * LANES, :] = block
+            out_ref[0, k, j, 2 * LANES :, :] = gram
+
+
+def partial_sums(rows_idx, plane, table, codes, gram, firsts, received=None, place=0):
     rows_dev, width = table.shape
-    other_core = received is None
-    blocks = pl.BlockSpec((1, 1, 4, BLOCK_ROWS, width), lambda dx, dz, r, h: (dx, dz, 0, 0, 0))
+    n = len(firsts)
+    block = (1, 2, 4, BLOCK_ROWS, width)
 
     def whole(shape):
-        return pl.BlockSpec(shape, lambda dx, dz, r, h: (0,) * len(shape))
+        return pl.BlockSpec(shape, lambda i, k, r, p: (0,) * len(shape))
 
     in_specs = [whole((rows_dev, width)), whole(codes.shape), whole(gram.shape)]
-    operands = (rows_idx, here, table, codes, gram)
-    scratch = [pltpu.VMEM((LANES, width), f32)] * 4
-    if other_core:
-        shapes = [(2, 4, 4, BLOCK_ROWS, width)]
-        out_specs = [blocks]
-    else:
-        in_specs += [blocks] + [whole(piece.shape) for piece in earlier]
-        operands += (received, *earlier)
-        end = (PART_ROWS, width)
-        shapes = [(4, 4) + end] * 2
-        if half:
-            shapes += [(4, 4) + end] * 8
-        else:
-            shapes += [(4, 2) + end] * 4 + [(2, 4) + end] * 4
-        out_specs = [whole(shape) for shape in shapes]
-        scratch = scratch + [pltpu.VMEM((BLOCK_ROWS, width), f32)] * 4
+    operands = (rows_idx, plane, table, codes, gram)
+    if received is not None:
+        in_specs.append(pl.BlockSpec(block, lambda i, k, r, p: (place, k, 0, 0, 0)))
+        operands += (received,)
     return pl.pallas_call(
-        functools.partial(partial_kernel, half=half, other_core=other_core),
+        functools.partial(
+            partial_kernel, first=firsts[0], first_step=firsts[-1] - firsts[0]
+        ),
         grid_spec=pltpu.PrefetchScalarGridSpec(
             num_scalar_prefetch=2,
-            grid=(2, 4),
+            grid=(n, 2),
             in_specs=in_specs,
-            out_specs=out_specs,
-            scratch_shapes=scratch,
+            out_specs=pl.BlockSpec(block, lambda i, k, r, p: (i, k, 0, 0, 0)),
+            scratch_shapes=[pltpu.VMEM((LANES, width), f32)] * 8,
         ),
-        out_shape=[jax.ShapeDtypeStruct(shape, f32) for shape in shapes],
-        compiler_params=pltpu.CompilerParams(vmem_limit_bytes=40 * 2**20),
-        name="partial_other" if other_core else "partial_own",
+        out_shape=jax.ShapeDtypeStruct((n, 4, 4, BLOCK_ROWS, width), f32),
+        compiler_params=pltpu.CompilerParams(vmem_limit_bytes=32 * 2**20),
+        name="partial_sums",
     )(*operands)
 
 
 def split_sum_kernel(*refs):
-    outs = refs[12:]
-    for part in range(3):
-        pieces = refs[4 * part : 4 * part + 4]
-        for i in range(4):
-            total = (pieces[0][i] + pieces[1][i]) + (pieces[2][i] + pieces[3][i])
-            outs[4 * part + i][...] = total
-
-
-def split_sums(parts, name):
-    operands = [piece for part in parts for piece in part]
-    outs = pl.pallas_call(
+    pieces, outs = refs[:4], refs[4:]
+    for i in range(4):
+        outs[i][...] = (pieces[0][i] + pieces[1][i]) + (pieces[2][i] + pieces[3][i])
+
+
+def split_sums(pieces, name):
+    return pl.pallas_call(
         split_sum_kernel,
-        out_shape=[jax.ShapeDtypeStruct(operands[0].shape[1:], f32)] * 12,
+        out_shape=[jax.ShapeDtypeStruct(pieces[0].shape[1:], f32)] * 4,
         compiler_params=pltpu.CompilerParams(vmem_limit_bytes=40 * 2**20),
         name=name,
-    )(*operands)
-    return [outs[4 * part : 4 * part + 4] for part in range(3)]
-
-
-def shifted(array, axis, by):
-    return lax.ppermute(array, axis, [(i, (i + by) % 4) for i in range(4)])
-
-
-def moved(parts, axes):
-    order = [(part, d) for d in (1, 3, 2) for part in range(3)]
-    results = [[part[0], None, None, None] for part in parts]
-    done = []
-    for k, (part, d) in enumerate(order):
-        piece = parts[part][d]
-        if k >= IN_FLIGHT:
-            piece, _ = lax.optimization_barrier((piece, done[k - IN_FLIGHT]))
-        done.append(shifted(piece, axes[part], d))
-        results[part][d] = done[-1]
-    return results
-
-
-def to_sources(rows_idx, here, table, codes, gram):
+    )(*pieces)
+
+
+def along(stage, by):
+    pairs = []
+    for device in range(128):
+        at = [device // 32, device // 16 % 2, device // 4 % 4, device % 4]
+        axis = ORDERS[at[1]][stage]
+        at[axis] = (at[axis] + by) % 4
+        pairs.append((device, ((at[0] * 2 + at[1]) * 4 + at[2]) * 4 + at[3]))
+    return pairs
+
+
+def shifted(array, stage, by):
+    return lax.ppermute(array, DP_ROWS, along(stage, by)) if by else array
+
+
+def plane_of(core):
+    here = jnp.stack([lax.axis_index(axis) for axis in DP_ROWS]).astype(i32)
+    strides = jnp.array([32, 16, 4, 1], i32)
+    orders = [jnp.array(order, i32) for order in ORDERS]
+    order = jnp.where(core == 0, orders[0], orders[1])
+    chosen = order[:, None] == jnp.arange(4, dtype=i32)[None, :]
+    at = jnp.sum(jnp.where(chosen, here[None, :], 0), axis=1)
+    stride = jnp.sum(jnp.where(chosen, strides[None, :], 0), axis=1)
+    return jnp.concatenate([(core * 16)[None], at, stride])
+
+
+def to_sources(rows_idx, table, codes, gram):
+    core = lax.axis_index(CORE).astype(i32)
+    other, own = plane_of(1 - core), plane_of(core)
     swap = [(0, 1), (1, 0)]
-    call = functools.partial(partial_sums, rows_idx, here, table, codes, gram)
-    received = [lax.ppermute(call(half)[0], CORE, swap) for half in range(2)]
-    early = call(0, received[0])
-    late = call(1, received[1], early[2:])
-    parts = [[early[0], early[1], late[0], late[1]], late[2:6], late[6:10]]
-    parts = split_sums(moved(parts, (X, Z, Y)), "sum_stage_1")
-    parts = split_sums(moved(parts, (Z, Y, X)), "sum_stage_2")
-    return moved(parts, (Y, X, Z))
+    received = []
+    for firsts in ((1, 3), (2, 0)):
+        mine = partial_sums(rows_idx, other, table, codes, gram, firsts)
+        received.append(lax.ppermute(mine, CORE, swap))
+    pieces = [None] * 4
+    for k, first in enumerate((1, 3, 2, 0)):
+        block = partial_sums(
+            rows_idx, own, table, codes, gram, (first,), received[k // 2], k % 2
+        )
+        pieces[first] = shifted(block.reshape(block.shape[1:]), 0, first)
+    for stage in (1, 2):
+        parts = split_sums(pieces, f"sum_stage_{stage}")
+        pieces = [shifted(part, stage, by) for by, part in enumerate(parts)]
+    return pieces
 
 
 def user_kernel(*refs, hist_len):
-    out_ref = refs[12]
-    sums = []
-    for part in range(3):
-        piece = refs[4 * part : 4 * part + 4]
-        sums.append((piece[0][...] + piece[1][...]) + (piece[2][...] + piece[3][...]))
-    sums = jnp.concatenate(sums, axis=0)
+    out_ref = refs[4]
+    sums = (refs[0][...] + refs[1][...]) + (refs[2][...] + refs[3][...])
     user = sums[:LANES] / hist_len
     positive = sums[LANES : 2 * LANES]
     gap = jnp.sum(user * positive, axis=1, keepdims=True) - 1.0
@@ -303,11 +265,10 @@
     )
 
 
-def user_block(parts, hist_len):
-    pieces = [piece for part in parts for piece in part]
+def user_block(pieces, hist_len):
     return pl.pallas_call(
         functools.partial(user_kernel, hist_len=hist_len),
-        out_shape=jax.ShapeDtypeStruct((BLOCK_ROWS, pieces[0].shape[-1]), f32),
+        out_shape=jax.ShapeDtypeStruct(pieces[0].shape, f32),
         name="user_block",
     )(*pieces)
 
@@ -344,7 +305,7 @@
     gram_ref[...] += half_gram(users)
 
     base = g * (sources * LANES)
-    unroll = 16
+    unroll = 128
 
     def body(j, carry):
         for at in range(0, unroll, CHAINS):
@@ -381,7 +342,7 @@
 def update_rows(row_idx, src_idx, blocks, item_total, table, state, coef, hist_len):
     rows_dev, width = table.shape
     devices = blocks.shape[0]
-    sources = 8
+    sources = 16
     whole = pl.BlockSpec((rows_dev, width), lambda g, r, s: (0, 0))
     return pl.pallas_call(
         functools.partial(update_kernel, sources=sources, coef=coef, hist_len=hist_len),
@@ -425,11 +386,10 @@
     asked = lax.all_to_all(lists, DP_ROWS, split_axis=0, concat_axis=0, tiled=True)
     rows = asked[:, 0, :].astype(i32).reshape(-1)
     codes = asked[:, 1, :]
-    place = jnp.arange(devices * LANES, dtype=i32) // LANES % 8 * (2 * LANES)
+    place = jnp.arange(devices * LANES, dtype=i32) // LANES % 16 * (2 * LANES)
     src_idx = place + jnp.maximum(codes.astype(i32).reshape(-1), 0)
-    here = jnp.stack([lax.axis_index(axis) for axis in DP_ROWS]).astype(i32)
-    parts = to_sources(jnp.where(rows < rows_dev, rows, 0), here, item_table, codes, item_gram)
-    block = user_block(parts, hist_len)
+    pieces = to_sources(jnp.where(rows < rows_dev, rows, 0), item_table, codes, item_gram)
+    block = user_block(pieces, hist_len)
     blocks = lax.all_gather(block, DP_ROWS)
     item_total = blocks[:, 2 * LANES + 1, :]
     return update_rows(

time: 302 us -> 273 us (0.904)
  starting transfers between devices: 51.8 us -> 20.2 us
  waiting for transfers between devices: 133 us -> 137 us
    ppermute x29 -> x11, starting transfers between devices: 40.3 us -> 8.64 us  [the longest x9 8.12 us: shifted(): return lax.ppermute(array, DP_ROWS, along(stage, by)) if by else array]
    ppermute x29 -> x11, waiting for transfers between devices: 34.2 us -> 49.8 us  [the longest x9 48.6 us: shifted(): return lax.ppermute(array, DP_ROWS, along(stage, by)) if by else array]
    all_gather x1, waiting for transfers between devices: 94.6 us -> 83 us  [shards(): blocks = lax.all_gather(block, DP_ROWS)]
    pallas_call x6 -> x8, Pallas kernels: 33.6 us -> 37.9 us  [the longest x6 37.3 us: partial_sums(): pl.pallas_call(functools.partial(partial_kernel, first=firsts[0], first_s...]
    pallas_call x1, Pallas kernels: 46.3 us -> 42.2 us  [update_rows(): pl.pallas_call(functools.partial(update_kernel, sources=sources, coef=coe...]
  transfers between devices with their start and end apart: 31 -> 13, of which waited for: 16 -> 10; matrix products, arithmetic and copies ran while one was open for 2% -> 2% of each run, Pallas kernels for 8% -> 11%
where the time goes in v5:
time: 273 us
  waiting for transfers between devices  137 us (50%)
  Pallas kernels  91.2 us (33%)
  starting transfers between devices  20.2 us (7%)
  between operations  14.2 us (5%)
  matrix products  5.81 us (2%)
  local copies, waits for them, and re-layouts  4.02 us (1%)
    all_gather x1, waiting for transfers between devices, shards(): blocks = lax.all_gather(block, DP_ROWS)  83 us
    ppermute x9, waiting for transfers between devices, shifted(): return lax.ppermute(array, DP_ROWS, along(stage, by)) if by else array  48.6 us
    pallas_call x1, Pallas kernels, update_rows(): pl.pallas_call(functools.partial(update_kernel, sources=sources, coef=coe...  42.2 us
    pallas_call x6, Pallas kernels, partial_sums(): pl.pallas_call(functools.partial(partial_kernel, first=firsts[0], first_s...  37.3 us
    all_to_all x1, starting transfers between devices, shards(): lax.all_to_all(lists, DP_ROWS, split_axis=0, concat_axis=0, tiled=True)  11.5 us
    pallas_call x1, Pallas kernels, request_lists(): pl.pallas_call(functools.partial(list_kernel, slots=hist_len + 1, rows_de...  9.3 us
    ppermute x9, starting transfers between devices, shifted(): return lax.ppermute(array, DP_ROWS, along(stage, by)) if by else array  8.12 us
    dot_general x1, matrix products, shards(): jnp.dot(item_table.T, item_table, precision=lax.Precision.HIGHEST, prefer...  5.81 us
  transfers between devices with their start and end apart: 13, of which 10 were waited for; matrix products, arithmetic and copies ran while one was open for 2% of the time, Pallas kernels for 11%

profile of v5, /device:TPU:1, one launch (start us, length us, event | category | flops | bytes accessed | tf_op | source)
XLA Modules:
  0.0 272.7 jit_solution(13593655380736726138)
XLA Ops:
  7.2 9.3 %request_lists.1 = f32[128,2,128]{2,1,0:T(2,128)} custom-call(s32[50,128]{1,0:T(8,128)} %bitcast.40, s32[1,128]{1,0:T(1,128)} %bitcast.41), custom_call_target="tpu_custom_call" | custom-call | tf_op jit(solution)/shard_map/request_lists/pallas_call | solution.py:112
  16.5 11.5 %all-to-all-start = ((f32[128,2,128]{2,1,0:T(2,128)}), f32[128,2,128]{2,1,0:T(2,128)S(1)}, u32[]{:S(2)}, u32[]{:S(2)}) async-start(f32[128,2,128]{2,1,0:T(2,128)} %request_lists.1), calls=%async_computation | async-start | bytes 262144 | tf_op jit(solution)/shard_map/all_to_all | solution.py:386
  28.0 0.0 copy-start.6
  28.0 0.0 copy-start.7
  28.0 0.0 copy-start.8
  28.0 0.0 all-gather.3.cloned.1.call-start
  28.1 0.0 copy-start
  28.1 5.8 %fusion.7.gram_ref = f32[128,128]{1,0:T(8,128)S(1)} fusion(f32[4096,128]{1,0:T(8,128)} %table_ref.13), kind=kOutput, calls=%fused_computation.27 | convolution fusion | flops 805306368 | bytes 2162688 | tf_op jit(solution)/shard_map/dot_general | solution.py:379
  33.9 0.1 pad_add_fusion
  34.0 0.0 copy-done.6
  34.0 0.0 copy-done.7
  34.0 0.0 copy-done.8
  34.0 0.2 select_reduce_fusion.1
  34.2 0.1 pad_add_fusion.2.plane_ref
  34.3 3.9 %all-to-all-done = f32[128,2,128]{2,1,0:T(2,128)S(1)} async-done(((f32[128,2,128]{2,1,0:T(2,128)}), f32[128,2,128]{2,1,0:T(2,128)S(1)}, u32[]{:S(2)}, u32[]{:S(2)}) %all-to-all-start) | async-done | bytes 131104 | tf_op jit(solution)/shard_map/all_to_all | solution.py:386
  38.2 0.1 fusion.6
  38.3 0.0 copy-done
  38.3 7.8 %partial_sums.6 = f32[2,4,4,264,128]{4,3,2,1,0:T(8,128)} custom-call(s32[16384]{0:T(1024)S(1)} %compare_select_fusion.rows_ref, s32[7]{0:T(128)S(1)} %pad_add_fusion.2.plane_ref, f32[4096,128]{1,0:T(8,128)S(1)} %copy-done, f32[128,128]{1,0:T(8,128)S(1)} %bitcast.25, f32[128,128]{1,0:T(8,128)S(1)} %fusion.7.gram_ref), custom_call_target="tpu_custom_call" | custom-call | tf_op jit(solution)/shard_map/partial_sums/pallas_call | solution.py:169
  46.1 0.5 collective-permute-start
  46.6 7.8 %partial_sums.8 = f32[2,4,4,264,128]{4,3,2,1,0:T(8,128)} custom-call(s32[16384]{0:T(1024)S(1)} %compare_select_fusion.rows_ref, s32[7]{0:T(128)S(1)} %pad_add_fusion.2.plane_ref, f32[4096,128]{1,0:T(8,128)S(1)} %copy-done, f32[128,128]{1,0:T(8,128)S(1)} %bitcast.26, f32[128,128]{1,0:T(8,128)S(1)} %fusion.7.gram_ref), custom_call_target="tpu_custom_call" | custom-call | tf_op jit(solution)/shard_map/partial_sums/pallas_call | solution.py:169
  54.3 0.1 collective-permute-start.1
  54.4 0.1 pad_add_fusion.1.plane_ref
  54.5 0.0 collective-permute-done.refs_0_
  54.5 5.4 %partial_sums.10 = f32[1,4,4,264,128]{4,3,2,1,0:T(8,128)S(1)} custom-call(s32[16384]{0:T(1024)S(1)} %compare_select_fusion.rows_ref, s32[7]{0:T(128)S(1)} %pad_add_fusion.1.plane_ref, f32[4096,128]{1,0:T(8,128)S(1)} %copy-done, f32[128,128]{1,0:T(8,128)S(1)} %bitcast.27, f32[128,128]{1,0:T(8,128)S(1)} %fusion.7.gram_ref, ...), custom_call_target="tpu_custom_call" | custom-call | tf_op jit(solution)/shard_map/partial_sums/pallas_call | solution.py:169
  59.9 0.9 collective-permute-start.3
  60.8 1.2 collective-permute-done.1.refs_0_
  62.0 5.4 %partial_sums.11 = f32[1,4,4,264,128]{4,3,2,1,0:T(8,128)S(1)} custom-call(s32[16384]{0:T(1024)S(1)} %compare_select_fusion.rows_ref, s32[7]{0:T(128)S(1)} %pad_add_fusion.1.plane_ref, f32[4096,128]{1,0:T(8,128)S(1)} %copy-done, f32[128,128]{1,0:T(8,128)S(1)} %bitcast.28, f32[128,128]{1,0:T(8,128)S(1)} %fusion.7.gram_ref, ...), custom_call_target="tpu_custom_call" | custom-call | tf_op jit(solution)/shard_map/partial_sums/pallas_call | solution.py:169
  67.5 1.0 collective-permute-start.4
  68.4 5.4 %partial_sums.9 = f32[1,4,4,264,128]{4,3,2,1,0:T(8,128)S(1)} custom-call(s32[16384]{0:T(1024)S(1)} %compare_select_fusion.rows_ref, s32[7]{0:T(128)S(1)} %pad_add_fusion.1.plane_ref, f32[4096,128]{1,0:T(8,128)S(1)} %copy-done, f32[128,128]{1,0:T(8,128)S(1)} %bitcast.29, f32[128,128]{1,0:T(8,128)S(1)} %fusion.7.gram_ref, ...), custom_call_target="tpu_custom_call" | custom-call | tf_op jit(solution)/shard_map/partial_sums/pallas_call | solution.py:169
  73.9 0.6 collective-permute-start.2
  74.5 5.4 %partial_sums.7 = f32[1,4,4,264,128]{4,3,2,1,0:T(8,128)S(1)} custom-call(s32[16384]{0:T(1024)S(1)} %compare_select_fusion.rows_ref, s32[7]{0:T(128)S(1)} %pad_add_fusion.1.plane_ref, f32[4096,128]{1,0:T(8,128)S(1)} %copy-done, f32[128,128]{1,0:T(8,128)S(1)} %bitcast.30, f32[128,128]{1,0:T(8,128)S(1)} %fusion.7.gram_ref, ...), custom_call_target="tpu_custom_call" | custom-call | tf_op jit(solution)/shard_map/partial_sums/pallas_call | solution.py:169
  80.0 7.5 %collective-permute-done.3.refs_2_ = f32[4,4,264,128]{3,2,1,0:T(8,128)S(1)} collective-permute-done((f32[4,4,264,128]{3,2,1,0:T(8,128)S(1)}, f32[4,4,264,128]{3,2,1,0:T(8,128)S(1)}, u32[]{:S(2)}, u32[]{:S(2)}) %collective-permute-start.3) | collective-permute-done | bytes 2162720 | tf_op jit(solution)/shard_map/ppermute | solution.py:212
  87.4 21.0 %collective-permute-done.4.refs_3_ = f32[4,4,264,128]{3,2,1,0:T(8,128)S(1)} collective-permute-done((f32[4,4,264,128]{3,2,1,0:T(8,128)S(1)}, f32[4,4,264,128]{3,2,1,0:T(8,128)S(1)}, u32[]{:S(2)}, u32[]{:S(2)}) %collective-permute-start.4) | collective-permute-done | bytes 2162720 | tf_op jit(solution)/shard_map/ppermute | solution.py:212
  108.5 2.1 collective-permute-done.2.refs_1_
  110.6 0.4 sum_stage_1.1
  111.0 0.4 collective-permute-start.5
  111.4 1.6 collective-permute-start.6
  113.0 1.0 collective-permute-start.7
  114.0 12.6 %collective-permute-done.5.refs_1_ = f32[4,264,128]{2,1,0:T(8,128)S(1)} collective-permute-done((f32[4,264,128]{2,1,0:T(8,128)S(1)}, f32[4,264,128]{2,1,0:T(8,128)S(1)}, u32[]{:S(2)}, u32[]{:S(2)}) %collective-permute-start.5) | collective-permute-done | bytes 540704 | tf_op jit(solution)/shard_map/ppermute | solution.py:212
  126.6 0.0 collective-permute-done.6.refs_2_
  126.6 0.6 collective-permute-done.7.refs_3_
  127.2 0.1 sum_stage_2.1
  127.3 0.0 copy-start.2
  127.3 0.6 copy-done.2
  128.0 0.0 collective-permute-start.8
  128.0 2.0 collective-permute-start.9
  130.0 0.6 collective-permute-start.10
  130.7 4.1 %collective-permute-done.8.refs_1_ = f32[264,128]{1,0:T(8,128)S(1)} collective-permute-done((f32[264,128]{1,0:T(8,128)S(1)}, f32[264,128]{1,0:T(8,128)S(1)}, u32[]{:S(2)}, u32[]{:S(2)}) %collective-permute-start.8) | collective-permute-done | bytes 135200 | tf_op jit(solution)/shard_map/ppermute | solution.py:212
  134.8 0.0 copy-start.3
  134.8 0.0 collective-permute-done.9.refs_2_
  134.8 0.0 copy-start.4
  134.8 0.6 collective-permute-done.10.refs_3_
  135.4 0.0 copy-start.5
  135.4 0.0 copy-done.3
  135.4 0.1 copy-done.4
  135.5 0.6 copy-done.5
  136.1 1.9 user_block.1
  137.9 0.0 all-gather.3.cloned.1.call-update
  138.0 83.0 %all-gather.3.cloned.1.call-done = f32[33792,128]{1,0:T(8,128)} async-done(((f32[264,128]{1,0:T(8,128)}), f32[33792,128]{1,0:T(8,128)}) %all-gather.3.cloned.1.call-update) | async-done | bytes 17301520 | tf_op jit(solution)/shard_map/all_gather | solution.py:393
  221.0 1.1 slice.14
  222.1 0.0 copy-start.1
  222.1 1.6 copy-done.1
  223.7 42.2 %update_rows.1 = (f32[4096,128]{1,0:T(8,128)}, f32[4096,128]{1,0:T(8,128)}) custom-call(s32[16384]{0:T(1024)S(1)} %bitcast.36, s32[16384]{0:T(1024)S(1)} %fusion.2.src_idx_ref, f32[128,264,128]{2,1,0:T(8,128)} %bitcast.39, f32[128,128]{1,0:T(8,128)S(1)} %bitcast.37, f32[4096,128]{1,0:T(8,128)S(1)} %copy-done, f32[4096,128]{1,0:T(8,128)S(1)} %copy-done.1), custom_call_target="tpu_custom_call" | custom-call | tf_op jit(solution)/shard_map/update_rows/pallas_call | solution.py:347
  (3 shorter events, 0.0 us)
Async XLA Ops:
  16.5 21.7 %all-to-all-start = ((f32[128,2,128]{2,1,0:T(2,128)}), f32[128,2,128]{2,1,0:T(2,128)S(1)}, u32[]{:S(2)}, u32[]{:S(2)}) async-start(f32[128,2,128]{2,1,0:T(2,128)} %request_lists.1), calls=%async_computation | async-start | bytes 262144 | tf_op jit(solution)/shard_map/all_to_all | solution.py:386
  28.0 6.0 %copy-start.6 = (s32[3]{0:T(128)S(1)}, s32[3]{0:T(128)}, u32[]{:S(2)}) copy-start(s32[3]{0:T(128)} %constant.64.clone) | copy-start | bytes 40
  28.0 6.0 %copy-start.7 = (s32[3]{0:T(128)S(1)}, s32[3]{0:T(128)}, u32[]{:S(2)}) copy-start(s32[3]{0:T(128)} %constant.63.clone) | copy-start | bytes 40
  28.0 6.0 %copy-start.8 = (s32[4]{0:T(128)S(1)}, s32[4]{0:T(128)}, u32[]{:S(2)}) copy-start(s32[4]{0:T(128)} %constant.62.clone) | copy-start | bytes 52
  28.0 193.0 %all-gather.3.cloned.1.call-start = ((), (), s32[]{:S(2)}) async-start(), calls=%async_computation.1 | async-start | bytes 17436672 | tf_op jit(solution)/shard_map/all_gather | solution.py:393
  28.1 10.2 %copy-start = (f32[4096,128]{1,0:T(8,128)S(1)}, f32[4096,128]{1,0:T(8,128)}, u32[]{:S(2)}) copy-start(f32[4096,128]{1,0:T(8,128)} %table_ref.13) | copy-start | bytes 6291460
  46.1 8.4 %collective-permute-start = (f32[2,4,4,264,128]{4,3,2,1,0:T(8,128)}, f32[2,4,4,264,128]{4,3,2,1,0:T(8,128)}, u32[]{:S(2)}, u32[]{:S(2)}) collective-permute-start(f32[2,4,4,264,128]{4,3,2,1,0:T(8,128)} %partial_sums.6), channel_id=1, source_target_pairs={{0,16},{16,0},{1,17},{17,1},{2,18},{18,2},{3,19},{19,3},{4,20},{20... | collective-permute-start | bytes 12976136 | tf_op jit(solution)/shard_map/ppermute | solution.py:233
  54.3 7.7 %collective-permute-start.1 = (f32[2,4,4,264,128]{4,3,2,1,0:T(8,128)}, f32[2,4,4,264,128]{4,3,2,1,0:T(8,128)}, u32[]{:S(2)}, u32[]{:S(2)}) collective-permute-start(f32[2,4,4,264,128]{4,3,2,1,0:T(8,128)} %partial_sums.8), channel_id=1, source_target_pairs={{0,16},{16,0},{1,17},{17,1},{2,18},{18,2},{3,19},{19,3},{4,20},{20... | collective-permute-start | bytes 12976136 | tf_op jit(solution)/shard_map/ppermute | solution.py:233
  59.9 27.5 %collective-permute-start.3 = (f32[4,4,264,128]{3,2,1,0:T(8,128)S(1)}, f32[4,4,264,128]{3,2,1,0:T(8,128)S(1)}, u32[]{:S(2)}, u32[]{:S(2)}) collective-permute-start(f32[4,4,264,128]{3,2,1,0:T(8,128)S(1)} %bitcast.32), channel_id=1, source_target_pairs={{0,64},{1,65},{2,66},{3,67},{4,68},{5,69},{6,70},{7,71},{8,72},{9,... | collective-permute-start | bytes 6488072 | tf_op jit(solution)/shard_map/ppermute | solution.py:212
  67.5 41.0 %collective-permute-start.4 = (f32[4,4,264,128]{3,2,1,0:T(8,128)S(1)}, f32[4,4,264,128]{3,2,1,0:T(8,128)S(1)}, u32[]{:S(2)}, u32[]{:S(2)}) collective-permute-start(f32[4,4,264,128]{3,2,1,0:T(8,128)S(1)} %bitcast.33), channel_id=1, source_target_pairs={{0,96},{1,97},{2,98},{3,99},{4,100},{5,101},{6,102},{7,103},{8,104... | collective-permute-start | bytes 6488072 | tf_op jit(solution)/shard_map/ppermute | solution.py:212
  73.9 36.7 %collective-permute-start.2 = (f32[4,4,264,128]{3,2,1,0:T(8,128)S(1)}, f32[4,4,264,128]{3,2,1,0:T(8,128)S(1)}, u32[]{:S(2)}, u32[]{:S(2)}) collective-permute-start(f32[4,4,264,128]{3,2,1,0:T(8,128)S(1)} %bitcast.34), channel_id=1, source_target_pairs={{0,32},{1,33},{2,34},{3,35},{4,36},{5,37},{6,38},{7,39},{8,40},{9,... | collective-permute-start | bytes 6488072 | tf_op jit(solution)/shard_map/ppermute | solution.py:212
  111.0 15.6 %collective-permute-start.5 = (f32[4,264,128]{2,1,0:T(8,128)S(1)}, f32[4,264,128]{2,1,0:T(8,128)S(1)}, u32[]{:S(2)}, u32[]{:S(2)}) collective-permute-start(f32[4,264,128]{2,1,0:T(8,128)S(1)} %get-tuple-element.11), channel_id=1, source_target_pairs={{0,4},{1,5},{2,6},{3,7},{4,8},{5,9},{6,10},{7,11},{8,12},{9,13},{1... | collective-permute-start | bytes 1622024 | tf_op jit(solution)/shard_map/ppermute | solution.py:212
  111.4 15.2 %collective-permute-start.6 = (f32[4,264,128]{2,1,0:T(8,128)S(1)}, f32[4,264,128]{2,1,0:T(8,128)S(1)}, u32[]{:S(2)}, u32[]{:S(2)}) collective-permute-start(f32[4,264,128]{2,1,0:T(8,128)S(1)} %get-tuple-element.12), channel_id=1, source_target_pairs={{0,8},{1,9},{2,10},{3,11},{4,12},{5,13},{6,14},{7,15},{8,0},{9,1},... | collective-permute-start | bytes 1622024 | tf_op jit(solution)/shard_map/ppermute | solution.py:212
  113.0 14.2 %collective-permute-start.7 = (f32[4,264,128]{2,1,0:T(8,128)S(1)}, f32[4,264,128]{2,1,0:T(8,128)S(1)}, u32[]{:S(2)}, u32[]{:S(2)}) collective-permute-start(f32[4,264,128]{2,1,0:T(8,128)S(1)} %get-tuple-element.13), channel_id=1, source_target_pairs={{0,12},{1,13},{2,14},{3,15},{4,0},{5,1},{6,2},{7,3},{8,4},{9,5},{1... | collective-permute-start | bytes 1622024 | tf_op jit(solution)/shard_map/ppermute | solution.py:212
  127.3 0.7 copy-start.2
  128.0 6.8 %collective-permute-start.8 = (f32[264,128]{1,0:T(8,128)S(1)}, f32[264,128]{1,0:T(8,128)S(1)}, u32[]{:S(2)}, u32[]{:S(2)}) collective-permute-start(f32[264,128]{1,0:T(8,128)S(1)} %get-tuple-element.15), channel_id=1, source_target_pairs={{0,1},{1,2},{2,3},{3,0},{4,5},{5,6},{6,7},{7,4},{8,9},{9,10},{10,1... | collective-permute-start | bytes 405512 | tf_op jit(solution)/shard_map/ppermute | solution.py:212
  128.0 6.8 %collective-permute-start.9 = (f32[264,128]{1,0:T(8,128)S(1)}, f32[264,128]{1,0:T(8,128)S(1)}, u32[]{:S(2)}, u32[]{:S(2)}) collective-permute-start(f32[264,128]{1,0:T(8,128)S(1)} %get-tuple-element.16), channel_id=1, source_target_pairs={{0,2},{1,3},{2,0},{3,1},{4,6},{5,7},{6,4},{7,5},{8,10},{9,11},{10,... | collective-permute-start | bytes 405512 | tf_op jit(solution)/shard_map/ppermute | solution.py:212
  130.0 5.4 %collective-permute-start.10 = (f32[264,128]{1,0:T(8,128)S(1)}, f32[264,128]{1,0:T(8,128)S(1)}, u32[]{:S(2)}, u32[]{:S(2)}) collective-permute-start(f32[264,128]{1,0:T(8,128)S(1)} %get-tuple-element.17), channel_id=1, source_target_pairs={{0,3},{1,0},{2,1},{3,2},{4,7},{5,4},{6,5},{7,6},{8,11},{9,8},{10,9... | collective-permute-start | bytes 405512 | tf_op jit(solution)/shard_map/ppermute | solution.py:212
  134.8 0.7 copy-start.3
  134.8 0.7 copy-start.4
  135.4 0.7 copy-start.5
  222.1 1.6 copy-start.1
Sparse Core Ops, SparseCore 0:
  138.1 82.9 all-gather.2

commit v6 on v5

--- a/solution.py
+++ b/solution.py
@@ -17,6 +17,7 @@
 
 LANES = 128
 BLOCK_ROWS = 264
+GROUP = 4
 CHAINS = 4
 
 bf16 = jnp.bfloat16
@@ -60,11 +61,17 @@
 
 
 def list_kernel(history_ref, positive_ref, out_ref, *, slots, rows_dev):
-    ids_r = jnp.concatenate(
-        [history_ref[...], positive_ref[...], jnp.zeros((LANES - slots, LANES), i32)], axis=0
-    )
-    ids_c = ids_r.T
+    shift = rows_dev.bit_length() - 1
     sq = (LANES, LANES)
+    ids = jnp.concatenate(
+        [history_ref[...], positive_ref[...], jnp.full((LANES - slots, LANES), -1, i32)], axis=0
+    )
+    owner_r = lax.shift_right_arithmetic(ids, shift)
+    owner_c = owner_r.T
+    local = ids & (rows_dev - 1)
+    high_r = (lax.shift_right_logical(local, 6) + 1).astype(f32)
+    low_r = (local & 63).astype(f32)
+    users = iota2((1, LANES), 1).astype(f32)
     lane = iota2(sq, 1)
     sub = iota2(sq, 0)
     lane_f = lane.astype(f32)
@@ -72,39 +79,42 @@
     zero = jnp.zeros(sq, f32)
     lower = jnp.concatenate([jnp.where(sub > lane, one, zero), one], axis=0).astype(bf16)
     ones = one.astype(bf16)
-    users = iota2((1, LANES), 1)
     carry = jnp.zeros(sq, f32)
     acc = jnp.zeros((3 * LANES, LANES), f32)
-    for h in range(slots):
-        owner_c = ids_c[:, h : h + 1] // rows_dev
-        member = owner_c == lane
-        counts = dot_f32(lower, jnp.where(member, one, zero).astype(bf16))
-        mine = jnp.where(member, counts[:LANES] + carry, zero).astype(bf16)
-        rank = dot_f32(mine, ones)
-        place = jnp.where(rank == lane_f, one, zero).astype(bf16)
-        ids = ids_r[h : h + 1, :]
-        local = ids % rows_dev
-        at_owner = ids // rows_dev == sub
-        high = (local // 64 + 1).astype(f32)
-        low = (local % 64).astype(f32)
-        code = (users + (LANES if h == slots - 1 else 0)).astype(f32)
-        vals = jnp.concatenate(
-            [
-                jnp.where(at_owner, jnp.broadcast_to(high, sq), zero),
-                jnp.where(at_owner, jnp.broadcast_to(low, sq), zero),
-                jnp.where(at_owner, jnp.broadcast_to(code, sq), zero),
-            ],
-            axis=0,
-        ).astype(bf16)
-        acc = acc + dot_f32(vals, place)
-        carry = carry + counts[LANES:]
+    for start in range(0, slots, GROUP):
+        group = range(start, start + GROUP)
+        members = [owner_c[:, h : h + 1] == lane for h in group]
+        counts = dot_f32(
+            lower,
+            jnp.concatenate([jnp.where(m, one, zero) for m in members], axis=1).astype(bf16),
+        )
+        mine = []
+        for k, member in enumerate(members):
+            block = counts[:, k * LANES : (k + 1) * LANES]
+            mine.append(jnp.where(member, block[:LANES] + carry, zero))
+            carry = carry + block[LANES:]
+        rank = dot_f32(jnp.concatenate(mine, axis=0).astype(bf16), ones)
+        place = jnp.where(rank == jnp.concatenate([lane_f] * GROUP, axis=0), 1.0, 0.0)
+        vals = []
+        for h in group:
+            at_owner = owner_r[h : h + 1, :] == sub
+            code = users + (LANES if h == slots - 1 else 0)
+            vals.append(
+                jnp.concatenate(
+                    [
+                        jnp.where(at_owner, jnp.broadcast_to(value, sq), zero)
+                        for value in (high_r[h : h + 1, :], low_r[h : h + 1, :], code)
+                    ],
+                    axis=0,
+                )
+            )
+        acc = acc + dot_f32(jnp.concatenate(vals, axis=1).astype(bf16), place.astype(bf16))
     high = acc[:LANES].astype(i32)
     low = acc[LANES : 2 * LANES].astype(i32)
     code = acc[2 * LANES :].astype(i32)
     present = high > 0
-    code = jnp.where(present, code, -1)
     out_ref[:, 0, :] = jnp.where(present, (high - 1) * 64 + low, rows_dev).astype(f32)
-    out_ref[:, 1, :] = code.astype(f32)
+    out_ref[:, 1, :] = jnp.where(present, code, -1).astype(f32)
 
 
 def request_lists(history_ids, positive_ids, rows_dev):

time: 273 us -> 269 us (0.985)
  Pallas kernels: 91.2 us -> 87.1 us
    pallas_call x1, Pallas kernels: 9.3 us -> 5.49 us  [request_lists(): pl.pallas_call(functools.partial(list_kernel, slots=hist_len + 1, rows_de...]
where the time goes in v6:
time: 269 us
  waiting for transfers between devices  137 us (51%)
  Pallas kernels  87.1 us (32%)
  starting transfers between devices  20.2 us (8%)
  between operations  14.2 us (5%)
  matrix products  5.81 us (2%)
  local copies, waits for them, and re-layouts  4.02 us (1%)
    all_gather x1, waiting for transfers between devices, shards(): blocks = lax.all_gather(block, DP_ROWS)  83 us
    ppermute x9, waiting for transfers between devices, shifted(): return lax.ppermute(array, DP_ROWS, along(stage, by)) if by else array  48.6 us
    pallas_call x1, Pallas kernels, update_rows(): pl.pallas_call(functools.partial(update_kernel, sources=sources, coef=coe...  41.8 us
    pallas_call x6, Pallas kernels, partial_sums(): pl.pallas_call(functools.partial(partial_kernel, first=firsts[0], first_s...  37.3 us
    all_to_all x1, starting transfers between devices, shards(): lax.all_to_all(lists, DP_ROWS, split_axis=0, concat_axis=0, tiled=True)  11.5 us
    ppermute x9, starting transfers between devices, shifted(): return lax.ppermute(array, DP_ROWS, along(stage, by)) if by else array  8.13 us
    dot_general x1, matrix products, shards(): jnp.dot(item_table.T, item_table, precision=lax.Precision.HIGHEST, prefer...  5.81 us
    pallas_call x1, Pallas kernels, request_lists(): pl.pallas_call(functools.partial(list_kernel, slots=hist_len + 1, rows_de...  5.49 us
  transfers between devices with their start and end apart: 13, of which 10 were waited for; matrix products, arithmetic and copies ran while one was open for 2% of the time, Pallas kernels for 11%

profile of v6, /device:TPU:1, one launch (start us, length us, event | category | flops | bytes accessed | tf_op | source)
XLA Modules:
  0.0 268.6 jit_solution(17033930876217141015)
XLA Ops:
  7.2 5.5 %request_lists.1 = f32[128,2,128]{2,1,0:T(2,128)} custom-call(s32[50,128]{1,0:T(8,128)} %bitcast.40, s32[1,128]{1,0:T(1,128)} %bitcast.41), custom_call_target="tpu_custom_call" | custom-call | tf_op jit(solution)/shard_map/request_lists/pallas_call | solution.py:122
  12.7 11.5 %all-to-all-start = ((f32[128,2,128]{2,1,0:T(2,128)}), f32[128,2,128]{2,1,0:T(2,128)S(1)}, u32[]{:S(2)}, u32[]{:S(2)}) async-start(f32[128,2,128]{2,1,0:T(2,128)} %request_lists.1), calls=%async_computation | async-start | bytes 262144 | tf_op jit(solution)/shard_map/all_to_all | solution.py:396
  24.2 0.0 copy-start.6
  24.2 0.0 copy-start.7
  24.2 0.0 copy-start.8
  24.2 0.0 all-gather.3.cloned.1.call-start
  24.3 0.0 copy-start
  24.3 5.8 %fusion.7.gram_ref = f32[128,128]{1,0:T(8,128)S(1)} fusion(f32[4096,128]{1,0:T(8,128)} %table_ref.13), kind=kOutput, calls=%fused_computation.27 | convolution fusion | flops 805306368 | bytes 2162688 | tf_op jit(solution)/shard_map/dot_general | solution.py:389
  30.1 0.1 pad_add_fusion
  30.2 0.0 copy-done.6
  30.2 0.0 copy-done.7
  30.2 0.0 copy-done.8
  30.2 0.2 select_reduce_fusion.1
  30.4 0.1 pad_add_fusion.2.plane_ref
  30.5 3.9 %all-to-all-done = f32[128,2,128]{2,1,0:T(2,128)S(1)} async-done(((f32[128,2,128]{2,1,0:T(2,128)}), f32[128,2,128]{2,1,0:T(2,128)S(1)}, u32[]{:S(2)}, u32[]{:S(2)}) %all-to-all-start) | async-done | bytes 131104 | tf_op jit(solution)/shard_map/all_to_all | solution.py:396
  34.4 0.1 fusion.6
  34.5 0.0 copy-done
  34.5 7.8 %partial_sums.6 = f32[2,4,4,264,128]{4,3,2,1,0:T(8,128)} custom-call(s32[16384]{0:T(1024)S(1)} %compare_select_fusion.rows_ref, s32[7]{0:T(128)S(1)} %pad_add_fusion.2.plane_ref, f32[4096,128]{1,0:T(8,128)S(1)} %copy-done, f32[128,128]{1,0:T(8,128)S(1)} %bitcast.25, f32[128,128]{1,0:T(8,128)S(1)} %fusion.7.gram_ref), custom_call_target="tpu_custom_call" | custom-call | tf_op jit(solution)/shard_map/partial_sums/pallas_call | solution.py:179
  42.3 0.4 collective-permute-start
  42.8 7.8 %partial_sums.8 = f32[2,4,4,264,128]{4,3,2,1,0:T(8,128)} custom-call(s32[16384]{0:T(1024)S(1)} %compare_select_fusion.rows_ref, s32[7]{0:T(128)S(1)} %pad_add_fusion.2.plane_ref, f32[4096,128]{1,0:T(8,128)S(1)} %copy-done, f32[128,128]{1,0:T(8,128)S(1)} %bitcast.26, f32[128,128]{1,0:T(8,128)S(1)} %fusion.7.gram_ref), custom_call_target="tpu_custom_call" | custom-call | tf_op jit(solution)/shard_map/partial_sums/pallas_call | solution.py:179
  50.5 0.1 collective-permute-start.1
  50.6 0.1 pad_add_fusion.1.plane_ref
  50.7 0.0 collective-permute-done.refs_0_
  50.7 5.4 %partial_sums.10 = f32[1,4,4,264,128]{4,3,2,1,0:T(8,128)S(1)} custom-call(s32[16384]{0:T(1024)S(1)} %compare_select_fusion.rows_ref, s32[7]{0:T(128)S(1)} %pad_add_fusion.1.plane_ref, f32[4096,128]{1,0:T(8,128)S(1)} %copy-done, f32[128,128]{1,0:T(8,128)S(1)} %bitcast.27, f32[128,128]{1,0:T(8,128)S(1)} %fusion.7.gram_ref, ...), custom_call_target="tpu_custom_call" | custom-call | tf_op jit(solution)/shard_map/partial_sums/pallas_call | solution.py:179
  56.1 0.9 collective-permute-start.3
  57.0 1.2 collective-permute-done.1.refs_0_
  58.2 5.4 %partial_sums.11 = f32[1,4,4,264,128]{4,3,2,1,0:T(8,128)S(1)} custom-call(s32[16384]{0:T(1024)S(1)} %compare_select_fusion.rows_ref, s32[7]{0:T(128)S(1)} %pad_add_fusion.1.plane_ref, f32[4096,128]{1,0:T(8,128)S(1)} %copy-done, f32[128,128]{1,0:T(8,128)S(1)} %bitcast.28, f32[128,128]{1,0:T(8,128)S(1)} %fusion.7.gram_ref, ...), custom_call_target="tpu_custom_call" | custom-call | tf_op jit(solution)/shard_map/partial_sums/pallas_call | solution.py:179
  63.7 1.0 collective-permute-start.4
  64.6 5.4 %partial_sums.9 = f32[1,4,4,264,128]{4,3,2,1,0:T(8,128)S(1)} custom-call(s32[16384]{0:T(1024)S(1)} %compare_select_fusion.rows_ref, s32[7]{0:T(128)S(1)} %pad_add_fusion.1.plane_ref, f32[4096,128]{1,0:T(8,128)S(1)} %copy-done, f32[128,128]{1,0:T(8,128)S(1)} %bitcast.29, f32[128,128]{1,0:T(8,128)S(1)} %fusion.7.gram_ref, ...), custom_call_target="tpu_custom_call" | custom-call | tf_op jit(solution)/shard_map/partial_sums/pallas_call | solution.py:179
  70.1 0.6 collective-permute-start.2
  70.7 5.4 %partial_sums.7 = f32[1,4,4,264,128]{4,3,2,1,0:T(8,128)S(1)} custom-call(s32[16384]{0:T(1024)S(1)} %compare_select_fusion.rows_ref, s32[7]{0:T(128)S(1)} %pad_add_fusion.1.plane_ref, f32[4096,128]{1,0:T(8,128)S(1)} %copy-done, f32[128,128]{1,0:T(8,128)S(1)} %bitcast.30, f32[128,128]{1,0:T(8,128)S(1)} %fusion.7.gram_ref, ...), custom_call_target="tpu_custom_call" | custom-call | tf_op jit(solution)/shard_map/partial_sums/pallas_call | solution.py:179
  76.1 7.5 %collective-permute-done.3.refs_2_ = f32[4,4,264,128]{3,2,1,0:T(8,128)S(1)} collective-permute-done((f32[4,4,264,128]{3,2,1,0:T(8,128)S(1)}, f32[4,4,264,128]{3,2,1,0:T(8,128)S(1)}, u32[]{:S(2)}, u32[]{:S(2)}) %collective-permute-start.3) | collective-permute-done | bytes 2162720 | tf_op jit(solution)/shard_map/ppermute | solution.py:222
  83.6 21.0 %collective-permute-done.4.refs_3_ = f32[4,4,264,128]{3,2,1,0:T(8,128)S(1)} collective-permute-done((f32[4,4,264,128]{3,2,1,0:T(8,128)S(1)}, f32[4,4,264,128]{3,2,1,0:T(8,128)S(1)}, u32[]{:S(2)}, u32[]{:S(2)}) %collective-permute-start.4) | collective-permute-done | bytes 2162720 | tf_op jit(solution)/shard_map/ppermute | solution.py:222
  104.6 2.1 collective-permute-done.2.refs_1_
  106.8 0.4 sum_stage_1.1
  107.2 0.4 collective-permute-start.5
  107.6 1.6 collective-permute-start.6
  109.2 1.0 collective-permute-start.7
  110.1 12.6 %collective-permute-done.5.refs_1_ = f32[4,264,128]{2,1,0:T(8,128)S(1)} collective-permute-done((f32[4,264,128]{2,1,0:T(8,128)S(1)}, f32[4,264,128]{2,1,0:T(8,128)S(1)}, u32[]{:S(2)}, u32[]{:S(2)}) %collective-permute-start.5) | collective-permute-done | bytes 540704 | tf_op jit(solution)/shard_map/ppermute | solution.py:222
  122.7 0.0 collective-permute-done.6.refs_2_
  122.7 0.6 collective-permute-done.7.refs_3_
  123.4 0.1 sum_stage_2.1
  123.5 0.0 copy-start.2
  123.5 0.6 copy-done.2
  124.2 0.0 collective-permute-start.8
  124.2 2.1 collective-permute-start.9
  126.2 0.6 collective-permute-start.10
  126.8 4.1 %collective-permute-done.8.refs_1_ = f32[264,128]{1,0:T(8,128)S(1)} collective-permute-done((f32[264,128]{1,0:T(8,128)S(1)}, f32[264,128]{1,0:T(8,128)S(1)}, u32[]{:S(2)}, u32[]{:S(2)}) %collective-permute-start.8) | collective-permute-done | bytes 135200 | tf_op jit(solution)/shard_map/ppermute | solution.py:222
  131.0 0.0 copy-start.3
  131.0 0.0 collective-permute-done.9.refs_2_
  131.0 0.0 copy-start.4
  131.0 0.6 collective-permute-done.10.refs_3_
  131.6 0.0 copy-start.5
  131.6 0.0 copy-done.3
  131.6 0.1 copy-done.4
  131.7 0.6 copy-done.5
  132.3 1.9 user_block.1
  134.1 0.0 all-gather.3.cloned.1.call-update
  134.2 83.0 %all-gather.3.cloned.1.call-done = f32[33792,128]{1,0:T(8,128)} async-done(((f32[264,128]{1,0:T(8,128)}), f32[33792,128]{1,0:T(8,128)}) %all-gather.3.cloned.1.call-update) | async-done | bytes 17301520 | tf_op jit(solution)/shard_map/all_gather | solution.py:403
  217.2 1.1 slice.14
  218.3 0.0 copy-start.1
  218.3 1.6 copy-done.1
  219.9 41.8 %update_rows.1 = (f32[4096,128]{1,0:T(8,128)}, f32[4096,128]{1,0:T(8,128)}) custom-call(s32[16384]{0:T(1024)S(1)} %bitcast.36, s32[16384]{0:T(1024)S(1)} %fusion.2.src_idx_ref, f32[128,264,128]{2,1,0:T(8,128)} %bitcast.39, f32[128,128]{1,0:T(8,128)S(1)} %bitcast.37, f32[4096,128]{1,0:T(8,128)S(1)} %copy-done, f32[4096,128]{1,0:T(8,128)S(1)} %copy-done.1), custom_call_target="tpu_custom_call" | custom-call | tf_op jit(solution)/shard_map/update_rows/pallas_call | solution.py:357
  (3 shorter events, 0.0 us)
Async XLA Ops:
  12.7 21.7 %all-to-all-start = ((f32[128,2,128]{2,1,0:T(2,128)}), f32[128,2,128]{2,1,0:T(2,128)S(1)}, u32[]{:S(2)}, u32[]{:S(2)}) async-start(f32[128,2,128]{2,1,0:T(2,128)} %request_lists.1), calls=%async_computation | async-start | bytes 262144 | tf_op jit(solution)/shard_map/all_to_all | solution.py:396
  24.2 6.0 %copy-start.6 = (s32[3]{0:T(128)S(1)}, s32[3]{0:T(128)}, u32[]{:S(2)}) copy-start(s32[3]{0:T(128)} %constant.64.clone) | copy-start | bytes 40
  24.2 6.0 %copy-start.7 = (s32[3]{0:T(128)S(1)}, s32[3]{0:T(128)}, u32[]{:S(2)}) copy-start(s32[3]{0:T(128)} %constant.63.clone) | copy-start | bytes 40
  24.2 6.0 %copy-start.8 = (s32[4]{0:T(128)S(1)}, s32[4]{0:T(128)}, u32[]{:S(2)}) copy-start(s32[4]{0:T(128)} %constant.62.clone) | copy-start | bytes 52
  24.2 193.0 %all-gather.3.cloned.1.call-start = ((), (), s32[]{:S(2)}) async-start(), calls=%async_computation.1 | async-start | bytes 17436672 | tf_op jit(solution)/shard_map/all_gather | solution.py:403
  24.3 10.2 %copy-start = (f32[4096,128]{1,0:T(8,128)S(1)}, f32[4096,128]{1,0:T(8,128)}, u32[]{:S(2)}) copy-start(f32[4096,128]{1,0:T(8,128)} %table_ref.13) | copy-start | bytes 6291460
  42.3 8.4 %collective-permute-start = (f32[2,4,4,264,128]{4,3,2,1,0:T(8,128)}, f32[2,4,4,264,128]{4,3,2,1,0:T(8,128)}, u32[]{:S(2)}, u32[]{:S(2)}) collective-permute-start(f32[2,4,4,264,128]{4,3,2,1,0:T(8,128)} %partial_sums.6), channel_id=1, source_target_pairs={{0,16},{16,0},{1,17},{17,1},{2,18},{18,2},{3,19},{19,3},{4,20},{20... | collective-permute-start | bytes 12976136 | tf_op jit(solution)/shard_map/ppermute | solution.py:243
  50.5 7.7 %collective-permute-start.1 = (f32[2,4,4,264,128]{4,3,2,1,0:T(8,128)}, f32[2,4,4,264,128]{4,3,2,1,0:T(8,128)}, u32[]{:S(2)}, u32[]{:S(2)}) collective-permute-start(f32[2,4,4,264,128]{4,3,2,1,0:T(8,128)} %partial_sums.8), channel_id=1, source_target_pairs={{0,16},{16,0},{1,17},{17,1},{2,18},{18,2},{3,19},{19,3},{4,20},{20... | collective-permute-start | bytes 12976136 | tf_op jit(solution)/shard_map/ppermute | solution.py:243
  56.1 27.5 %collective-permute-start.3 = (f32[4,4,264,128]{3,2,1,0:T(8,128)S(1)}, f32[4,4,264,128]{3,2,1,0:T(8,128)S(1)}, u32[]{:S(2)}, u32[]{:S(2)}) collective-permute-start(f32[4,4,264,128]{3,2,1,0:T(8,128)S(1)} %bitcast.32), channel_id=1, source_target_pairs={{0,64},{1,65},{2,66},{3,67},{4,68},{5,69},{6,70},{7,71},{8,72},{9,... | collective-permute-start | bytes 6488072 | tf_op jit(solution)/shard_map/ppermute | solution.py:222
  63.7 41.0 %collective-permute-start.4 = (f32[4,4,264,128]{3,2,1,0:T(8,128)S(1)}, f32[4,4,264,128]{3,2,1,0:T(8,128)S(1)}, u32[]{:S(2)}, u32[]{:S(2)}) collective-permute-start(f32[4,4,264,128]{3,2,1,0:T(8,128)S(1)} %bitcast.33), channel_id=1, source_target_pairs={{0,96},{1,97},{2,98},{3,99},{4,100},{5,101},{6,102},{7,103},{8,104... | collective-permute-start | bytes 6488072 | tf_op jit(solution)/shard_map/ppermute | solution.py:222
  70.1 36.7 %collective-permute-start.2 = (f32[4,4,264,128]{3,2,1,0:T(8,128)S(1)}, f32[4,4,264,128]{3,2,1,0:T(8,128)S(1)}, u32[]{:S(2)}, u32[]{:S(2)}) collective-permute-start(f32[4,4,264,128]{3,2,1,0:T(8,128)S(1)} %bitcast.34), channel_id=1, source_target_pairs={{0,32},{1,33},{2,34},{3,35},{4,36},{5,37},{6,38},{7,39},{8,40},{9,... | collective-permute-start | bytes 6488072 | tf_op jit(solution)/shard_map/ppermute | solution.py:222
  107.2 15.6 %collective-permute-start.5 = (f32[4,264,128]{2,1,0:T(8,128)S(1)}, f32[4,264,128]{2,1,0:T(8,128)S(1)}, u32[]{:S(2)}, u32[]{:S(2)}) collective-permute-start(f32[4,264,128]{2,1,0:T(8,128)S(1)} %get-tuple-element.11), channel_id=1, source_target_pairs={{0,4},{1,5},{2,6},{3,7},{4,8},{5,9},{6,10},{7,11},{8,12},{9,13},{1... | collective-permute-start | bytes 1622024 | tf_op jit(solution)/shard_map/ppermute | solution.py:222
  107.6 15.2 %collective-permute-start.6 = (f32[4,264,128]{2,1,0:T(8,128)S(1)}, f32[4,264,128]{2,1,0:T(8,128)S(1)}, u32[]{:S(2)}, u32[]{:S(2)}) collective-permute-start(f32[4,264,128]{2,1,0:T(8,128)S(1)} %get-tuple-element.12), channel_id=1, source_target_pairs={{0,8},{1,9},{2,10},{3,11},{4,12},{5,13},{6,14},{7,15},{8,0},{9,1},... | collective-permute-start | bytes 1622024 | tf_op jit(solution)/shard_map/ppermute | solution.py:222
  109.2 14.2 %collective-permute-start.7 = (f32[4,264,128]{2,1,0:T(8,128)S(1)}, f32[4,264,128]{2,1,0:T(8,128)S(1)}, u32[]{:S(2)}, u32[]{:S(2)}) collective-permute-start(f32[4,264,128]{2,1,0:T(8,128)S(1)} %get-tuple-element.13), channel_id=1, source_target_pairs={{0,12},{1,13},{2,14},{3,15},{4,0},{5,1},{6,2},{7,3},{8,4},{9,5},{1... | collective-permute-start | bytes 1622024 | tf_op jit(solution)/shard_map/ppermute | solution.py:222
  123.5 0.7 copy-start.2
  124.2 6.8 %collective-permute-start.8 = (f32[264,128]{1,0:T(8,128)S(1)}, f32[264,128]{1,0:T(8,128)S(1)}, u32[]{:S(2)}, u32[]{:S(2)}) collective-permute-start(f32[264,128]{1,0:T(8,128)S(1)} %get-tuple-element.15), channel_id=1, source_target_pairs={{0,1},{1,2},{2,3},{3,0},{4,5},{5,6},{6,7},{7,4},{8,9},{9,10},{10,1... | collective-permute-start | bytes 405512 | tf_op jit(solution)/shard_map/ppermute | solution.py:222
  124.2 6.8 %collective-permute-start.9 = (f32[264,128]{1,0:T(8,128)S(1)}, f32[264,128]{1,0:T(8,128)S(1)}, u32[]{:S(2)}, u32[]{:S(2)}) collective-permute-start(f32[264,128]{1,0:T(8,128)S(1)} %get-tuple-element.16), channel_id=1, source_target_pairs={{0,2},{1,3},{2,0},{3,1},{4,6},{5,7},{6,4},{7,5},{8,10},{9,11},{10,... | collective-permute-start | bytes 405512 | tf_op jit(solution)/shard_map/ppermute | solution.py:222
  126.2 5.4 %collective-permute-start.10 = (f32[264,128]{1,0:T(8,128)S(1)}, f32[264,128]{1,0:T(8,128)S(1)}, u32[]{:S(2)}, u32[]{:S(2)}) collective-permute-start(f32[264,128]{1,0:T(8,128)S(1)} %get-tuple-element.17), channel_id=1, source_target_pairs={{0,3},{1,0},{2,1},{3,2},{4,7},{5,4},{6,5},{7,6},{8,11},{9,8},{10,9... | collective-permute-start | bytes 405512 | tf_op jit(solution)/shard_map/ppermute | solution.py:222
  131.0 0.7 copy-start.3
  131.0 0.7 copy-start.4
  131.6 0.7 copy-start.5
  218.3 1.6 copy-start.1
Sparse Core Ops, SparseCore 0:
  134.3 82.8 all-gather.2

commit v7 on v6

--- a/solution.py
+++ b/solution.py
@@ -16,7 +16,9 @@
 step_size = 0.05
 
 LANES = 128
+SUM_ROWS = 256
 BLOCK_ROWS = 264
+TOTAL_COPIES = 16
 GROUP = 4
 CHAINS = 4
 
@@ -60,7 +62,7 @@
     return halves[:, :LANES] + (cross + cross.T)
 
 
-def list_kernel(history_ref, positive_ref, out_ref, *, slots, rows_dev):
+def list_kernel(history_ref, positive_ref, gram_ref, out_ref, *, slots, rows_dev):
     shift = rows_dev.bit_length() - 1
     sq = (LANES, LANES)
     ids = jnp.concatenate(
@@ -115,18 +117,20 @@
     present = high > 0
     out_ref[:, 0, :] = jnp.where(present, (high - 1) * 64 + low, rows_dev).astype(f32)
     out_ref[:, 1, :] = jnp.where(present, code, -1).astype(f32)
-
-
-def request_lists(history_ids, positive_ids, rows_dev):
+    out_ref[:, 2, :] = gram_ref[...]
+    out_ref[:, 3, :] = zero
+
+
+def request_lists(history_ids, positive_ids, gram, rows_dev):
     users, hist_len = history_ids.shape
     return pl.pallas_call(
         functools.partial(list_kernel, slots=hist_len + 1, rows_dev=rows_dev),
-        out_shape=jax.ShapeDtypeStruct((LANES, 2, LANES), f32),
+        out_shape=jax.ShapeDtypeStruct((LANES, 4, LANES), f32),
         name="request_lists",
-    )(history_ids.T, positive_ids.reshape(1, users))
-
-
-def partial_kernel(rows_ref, plane_ref, table_ref, codes_ref, gram_ref, *refs, first, first_step):
+    )(history_ids.T, positive_ids.reshape(1, users), gram)
+
+
+def partial_kernel(rows_ref, plane_ref, table_ref, codes_ref, *refs, first, first_step):
     from_ref = refs[0] if len(refs) == 10 else None
     out_ref = refs[-9]
     picked_refs = refs[-8:]
@@ -155,24 +159,21 @@
                 jnp.concatenate([weight, weight], axis=1),
                 jnp.concatenate(split2(picked_ref[...]), axis=0),
             )
-            gram = jnp.broadcast_to(gram_ref[pl.ds(source, 1), :], (8, LANES))
             if from_ref is not None:
-                block = block + from_ref[0, k, j, : 2 * LANES, :]
-                gram = gram + from_ref[0, k, j, 2 * LANES :, :]
-            out_ref[0, k, j, : 2 * LANES, :] = block
-            out_ref[0, k, j, 2 * LANES :, :] = gram
-
-
-def partial_sums(rows_idx, plane, table, codes, gram, firsts, received=None, place=0):
+                block = block + from_ref[0, k, j]
+            out_ref[0, k, j] = block
+
+
+def partial_sums(rows_idx, plane, table, codes, firsts, received=None, place=0):
     rows_dev, width = table.shape
     n = len(firsts)
-    block = (1, 2, 4, BLOCK_ROWS, width)
+    block = (1, 2, 4, SUM_ROWS, width)
 
     def whole(shape):
         return pl.BlockSpec(shape, lambda i, k, r, p: (0,) * len(shape))
 
-    in_specs = [whole((rows_dev, width)), whole(codes.shape), whole(gram.shape)]
-    operands = (rows_idx, plane, table, codes, gram)
+    in_specs = [whole((rows_dev, width)), whole(codes.shape)]
+    operands = (rows_idx, plane, table, codes)
     if received is not None:
         in_specs.append(pl.BlockSpec(block, lambda i, k, r, p: (place, k, 0, 0, 0)))
         operands += (received,)
@@ -187,7 +188,7 @@
             out_specs=pl.BlockSpec(block, lambda i, k, r, p: (i, k, 0, 0, 0)),
             scratch_shapes=[pltpu.VMEM((LANES, width), f32)] * 8,
         ),
-        out_shape=jax.ShapeDtypeStruct((n, 4, 4, BLOCK_ROWS, width), f32),
+        out_shape=jax.ShapeDtypeStruct((n, 4, 4, SUM_ROWS, width), f32),
         compiler_params=pltpu.CompilerParams(vmem_limit_bytes=32 * 2**20),
         name="partial_sums",
     )(*operands)
@@ -233,18 +234,19 @@
     return jnp.concatenate([(core * 16)[None], at, stride])
 
 
-def to_sources(rows_idx, table, codes, gram):
-    core = lax.axis_index(CORE).astype(i32)
-    other, own = plane_of(1 - core), plane_of(core)
-    swap = [(0, 1), (1, 0)]
+def swapped(array):
+    return lax.ppermute(array, CORE, [(0, 1), (1, 0)])
+
+
+def to_sources(rows_idx, own, other, table, codes):
     received = []
     for firsts in ((1, 3), (2, 0)):
-        mine = partial_sums(rows_idx, other, table, codes, gram, firsts)
-        received.append(lax.ppermute(mine, CORE, swap))
+        mine = partial_sums(rows_idx, other, table, codes, firsts)
+        received.append(swapped(mine))
     pieces = [None] * 4
     for k, first in enumerate((1, 3, 2, 0)):
         block = partial_sums(
-            rows_idx, own, table, codes, gram, (first,), received[k // 2], k % 2
+            rows_idx, own, table, codes, (first,), received[k // 2], k % 2
         )
         pieces[first] = shifted(block.reshape(block.shape[1:]), 0, first)
     for stage in (1, 2):
@@ -253,85 +255,115 @@
     return pieces
 
 
-def user_kernel(*refs, hist_len):
-    out_ref = refs[4]
+def user_kernel(*refs, hist_len, coef):
+    item_ref, out_ref = refs[4:]
     sums = (refs[0][...] + refs[1][...]) + (refs[2][...] + refs[3][...])
     user = sums[:LANES] / hist_len
-    positive = sums[LANES : 2 * LANES]
+    positive = sums[LANES:]
     gap = jnp.sum(user * positive, axis=1, keepdims=True) - 1.0
+    grad = 2.0 * gap * positive + 2.0 * coef * dot_split(user, item_ref[...])
     sq = (LANES, LANES)
     gap_row = jnp.sum(
         jnp.where(iota2(sq, 0) == iota2(sq, 1), jnp.broadcast_to(gap, sq), 0.0),
         axis=0,
         keepdims=True,
     )
-    out_ref[:LANES, :] = positive
+    out_ref[:LANES, :] = grad / hist_len
     out_ref[LANES : 2 * LANES, :] = user
-    tail = (8, LANES)
-    out_ref[2 * LANES :, :] = jnp.where(
-        iota2(tail, 0) == 0,
-        jnp.broadcast_to(gap_row, tail),
-        sums[2 * LANES :],
-    )
-
-
-def user_block(pieces, hist_len):
-    return pl.pallas_call(
-        functools.partial(user_kernel, hist_len=hist_len),
-        out_shape=jax.ShapeDtypeStruct(pieces[0].shape, f32),
+    out_ref[2 * LANES :, :] = jnp.broadcast_to(gap_row, (8, LANES))
+
+
+def user_block(pieces, item_total, hist_len, coef):
+    return pl.pallas_call(
+        functools.partial(user_kernel, hist_len=hist_len, coef=coef),
+        out_shape=jax.ShapeDtypeStruct((BLOCK_ROWS, pieces[0].shape[-1]), f32),
         name="user_block",
+    )(*pieces, item_total)
+
+
+def stack_kernel(*refs):
+    for k in range(4):
+        refs[4][k] = refs[k][...]
+
+
+def stacked(pieces):
+    return pl.pallas_call(
+        stack_kernel,
+        out_shape=jax.ShapeDtypeStruct((4,) + pieces[0].shape, f32),
+        compiler_params=pltpu.CompilerParams(vmem_limit_bytes=24 * 2**20),
+        name="stack_blocks",
     )(*pieces)
 
 
 def update_kernel(
-    row_idx_ref, src_idx_ref, blocks_ref, item_ref, table_ref, state_ref, new_table_ref, new_state_ref,
-    stage_ref, gram_ref, *acc_refs, sources, coef, hist_len,
+    row_idx_ref, code_idx_ref, planes_ref, *refs, sides, first, last, coef
 ):
+    n = len(sides)
+    blocks, refs = refs[:n], refs[n:]
+    if not first:
+        (carry_ref, carry_gram_ref), refs = refs[:2], refs[2:]
+    if last:
+        (table_ref, state_ref), refs = refs[:2], refs[2:]
+    outs, refs = refs[:2], refs[2:]
+    stage_ref, gram_ref, acc_refs = refs[0], refs[1], refs[2:]
     g = pl.program_id(0)
-    rows_dev = table_ref.shape[0]
     sq = (LANES, LANES)
+    rows_all = acc_refs[0].shape[0]
 
     @pl.when(g == 0)
     def _():
-        gram_ref[...] = jnp.zeros_like(gram_ref)
-        for acc in acc_refs:
-            acc[...] = jnp.zeros_like(acc)
+        for k, acc in enumerate(acc_refs):
+            if k or first:
+                acc[...] = jnp.zeros_like(acc)
+            else:
+                acc[...] = carry_ref[...]
+        gram_ref[...] = jnp.zeros_like(gram_ref) if first else carry_gram_ref[...]
 
     diagonal = iota2(sq, 0) == iota2(sq, 1)
-    users = jnp.concatenate(
-        [blocks_ref[s, LANES : 2 * LANES, :] for s in range(sources)], axis=0
-    )
-    pulls = dot_split(users, item_ref[...])
-    for s in range(sources):
-        user = blocks_ref[s, LANES : 2 * LANES, :]
-        gap_row = blocks_ref[s, 2 * LANES : 2 * LANES + 1, :]
-        gap = 2.0 * jnp.sum(
-            jnp.where(diagonal, jnp.broadcast_to(gap_row, sq), 0.0), axis=1, keepdims=True
-        )
-        pull = pulls[LANES * s : LANES * (s + 1)]
-        grad = gap * blocks_ref[s, :LANES, :] + 2.0 * coef * pull
-        stage_ref[2 * LANES * s : 2 * LANES * s + LANES, :] = grad / hist_len
-        stage_ref[2 * LANES * s + LANES : 2 * LANES * (s + 1), :] = gap * user
-    gram_ref[...] += half_gram(users)
-
-    base = g * (sources * LANES)
-    unroll = 128
-
-    def body(j, carry):
-        for at in range(0, unroll, CHAINS):
-            first = base + j * unroll + at
-            rows = [row_idx_ref[first + k] for k in range(CHAINS)]
-            srcs = [src_idx_ref[first + k] for k in range(CHAINS)]
-            grads = [stage_ref[pl.ds(srcs[k], 1), :] for k in range(CHAINS)]
-            sums = [acc_refs[k][pl.ds(rows[k], 1), :] + grads[k] for k in range(CHAINS)]
-            for k in range(CHAINS):
-                acc_refs[k][pl.ds(rows[k], 1), :] = sums[k]
-        return carry
-
-    lax.fori_loop(0, sources * LANES // unroll, body, 0)
+    for a in range(n):
+        users = []
+        for k in range(8):
+            at = (8 * a + k) * 2 * LANES
+            spot = (k // 4, k % 4)
+            user = blocks[a][(*spot, slice(LANES, 2 * LANES))]
+            gap_row = blocks[a][(*spot, slice(2 * LANES, 2 * LANES + 1))]
+            gap = 2.0 * jnp.sum(
+                jnp.where(diagonal, jnp.broadcast_to(gap_row, sq), 0.0), axis=1, keepdims=True
+            )
+            stage_ref[at : at + LANES, :] = blocks[a][(*spot, slice(0, LANES))]
+            stage_ref[at + LANES : at + 2 * LANES, :] = gap * user
+            users.append(user)
+        gram_ref[...] += half_gram(jnp.concatenate(users, axis=0))
+
+    for a, (side, offset) in enumerate(sides):
+        here = [planes_ref[7 * side + k] for k in range(7)]
+        base = here[0] + ((here[1] - offset) & 3) * here[4]
+
+        def body(k, carry, a=a, here=here, base=base):
+            at_second = ((here[2] - (2 * g + lax.shift_right_logical(k, 2))) & 3) * here[5]
+            at_third = ((here[3] - (k & 3)) & 3) * here[6]
+            source = (base + at_second + at_third) * LANES
+            stage = (8 * a + k) * (2 * LANES)
+            for at in range(0, LANES, CHAINS):
+                rows = [row_idx_ref[source + (at + c)] for c in range(CHAINS)]
+                srcs = [stage + code_idx_ref[source + (at + c)] for c in range(CHAINS)]
+                grads = [stage_ref[pl.ds(srcs[c], 1), :] for c in range(CHAINS)]
+                sums = [acc_refs[c][pl.ds(rows[c], 1), :] + grads[c] for c in range(CHAINS)]
+                for c in range(CHAINS):
+                    acc_refs[c][pl.ds(rows[c], 1), :] = sums[c]
+            return carry
+
+        lax.fori_loop(0, 8, body, 0)
 
     @pl.when(g == pl.num_programs(0) - 1)
     def _():
+        if not last:
+            total = acc_refs[0][...]
+            for acc in acc_refs[1:]:
+                total = total + acc[...]
+            outs[0][...] = total
+            outs[1][...] = gram_ref[...]
+            return
         step = 512
         gram = whole_gram(gram_ref[...])
 
@@ -342,48 +374,49 @@
             for acc in acc_refs:
                 grad = grad + acc[at, :]
             new_state = state_ref[at, :] + grad * grad
-            new_state_ref[at, :] = new_state
-            new_table_ref[at, :] = table - step_size * grad / jnp.sqrt(new_state)
+            outs[1][at, :] = new_state
+            outs[0][at, :] = table - step_size * grad / jnp.sqrt(new_state)
             return carry
 
-        lax.fori_loop(0, rows_dev // step, finish, 0)
-
-
-def update_rows(row_idx, src_idx, blocks, item_total, table, state, coef, hist_len):
-    rows_dev, width = table.shape
-    devices = blocks.shape[0]
-    sources = 16
-    whole = pl.BlockSpec((rows_dev, width), lambda g, r, s: (0, 0))
-    return pl.pallas_call(
-        functools.partial(update_kernel, sources=sources, coef=coef, hist_len=hist_len),
+        lax.fori_loop(0, (rows_all - 8) // step, finish, 0)
+
+
+def update_rows(row_idx, code_idx, planes, blocks, sides, rows_dev, carry, final, coef):
+    width = blocks[0].shape[-1]
+
+    def whole(shape):
+        return pl.BlockSpec(shape, lambda g, r, c, p: (0,) * len(shape))
+
+    part = pl.BlockSpec((2, 4, BLOCK_ROWS, width), lambda g, r, c, p: (g, 0, 0, 0))
+    extra = (*carry, *final)
+    if final:
+        out_shapes = [(rows_dev, width)] * 2
+    else:
+        out_shapes = [(rows_dev + 8, width), (width, 2 * width)]
+    return pl.pallas_call(
+        functools.partial(
+            update_kernel, sides=sides, first=not carry, last=bool(final), coef=coef
+        ),
         grid_spec=pltpu.PrefetchScalarGridSpec(
-            num_scalar_prefetch=2,
-            grid=(devices // sources,),
-            in_specs=[
-                pl.BlockSpec((sources, BLOCK_ROWS, width), lambda g, r, s: (g, 0, 0)),
-                pl.BlockSpec((width, width), lambda g, r, s: (0, 0)),
-                whole,
-                whole,
-            ],
-            out_specs=[whole, whole],
+            num_scalar_prefetch=3,
+            grid=(2,),
+            in_specs=[part] * len(blocks) + [whole(array.shape) for array in extra],
+            out_specs=[whole(shape) for shape in out_shapes],
             scratch_shapes=[
-                pltpu.VMEM((sources * 2 * LANES, width), f32),
+                pltpu.VMEM((len(blocks) * 8 * 2 * LANES, width), f32),
                 pltpu.VMEM((width, 2 * width), f32),
             ]
             + [pltpu.VMEM((rows_dev + 8, width), f32)] * CHAINS,
         ),
-        out_shape=(
-            jax.ShapeDtypeStruct((rows_dev, width), f32),
-            jax.ShapeDtypeStruct((rows_dev, width), f32),
-        ),
+        out_shape=[jax.ShapeDtypeStruct(shape, f32) for shape in out_shapes],
         compiler_params=pltpu.CompilerParams(vmem_limit_bytes=48 * 2**20),
-        name="update_rows",
-    )(row_idx, src_idx, blocks, item_total, table, state)
+        name="update_rows" if final else "add_rows",
+    )(row_idx, code_idx, planes, *blocks, *extra)
 
 
 def shards(item_table, adagrad_state, history_ids, positive_ids):
     rows_dev, width = item_table.shape
-    users_dev, hist_len = history_ids.shape
+    _, hist_len = history_ids.shape
     devices = lax.axis_size(DP_ROWS)
     coef = penalty_weight / (rows_dev * devices)
     item_gram = jnp.dot(
@@ -392,18 +425,40 @@
         precision=lax.Precision.HIGHEST,
         preferred_element_type=f32,
     )
-    lists = request_lists(history_ids, positive_ids, rows_dev)
+    lists = request_lists(history_ids, positive_ids, item_gram, rows_dev)
     asked = lax.all_to_all(lists, DP_ROWS, split_axis=0, concat_axis=0, tiled=True)
     rows = asked[:, 0, :].astype(i32).reshape(-1)
     codes = asked[:, 1, :]
-    place = jnp.arange(devices * LANES, dtype=i32) // LANES % 16 * (2 * LANES)
-    src_idx = place + jnp.maximum(codes.astype(i32).reshape(-1), 0)
-    pieces = to_sources(jnp.where(rows < rows_dev, rows, 0), item_table, codes, item_gram)
-    block = user_block(pieces, hist_len)
-    blocks = lax.all_gather(block, DP_ROWS)
-    item_total = blocks[:, 2 * LANES + 1, :]
-    return update_rows(
-        rows, src_idx, blocks, item_total, item_table, adagrad_state, coef, hist_len
+    code_idx = jnp.maximum(codes.astype(i32).reshape(-1), 0)
+    total_row = jnp.broadcast_to(asked[:, 2, :].sum(axis=0), (TOTAL_COPIES, width))
+    total_row = lax.optimization_barrier(total_row)
+    totals = lax.optimization_barrier(lax.all_gather(total_row, DP_ROWS))
+    item_total = totals[:, 0, :]
+    core = lax.axis_index(CORE).astype(i32)
+    own, other = plane_of(core), plane_of(1 - core)
+    planes = jnp.concatenate([own, other])
+    pieces = to_sources(jnp.where(rows < rows_dev, rows, 0), own, other, item_table, codes)
+    block = user_block(pieces, item_total, hist_len, coef)
+    line = stacked([shifted(block, 2, by) for by in range(4)])
+    plane = stacked([shifted(line, 1, by) for by in range(4)])
+    update = functools.partial(update_rows, rows, code_idx, planes)
+    near = (shifted(plane, 0, 1), shifted(plane, 0, 3))
+    carry = update([plane, swapped(plane)], ((0, 0), (1, 0)), rows_dev, (), (), coef)
+    plane, *near, carry = lax.optimization_barrier((plane, *near, carry))
+    across = shifted(plane, 0, 2)
+    carry = update(
+        [*near, *map(swapped, near)], ((0, 1), (0, 3), (1, 1), (1, 3)), rows_dev, carry, (), coef
+    )
+    across, carry = lax.optimization_barrier((across, carry))
+    return tuple(
+        update(
+            [across, swapped(across)],
+            ((0, 2), (1, 2)),
+            rows_dev,
+            carry,
+            (item_table, adagrad_state),
+            coef,
+        )
     )
 
 

time: 269 us -> 276 us (1.026)
  waiting for transfers between devices: 137 us -> 103 us
  Pallas kernels: 87.1 us -> 110 us
  starting transfers between devices: 20.2 us -> 33 us
  local copies, waits for them, and re-layouts: 4.02 us -> 8.65 us
    all_gather x1, waiting for transfers between devices: 83 us -> 5.98 us  [shards(): totals = lax.optimization_barrier(lax.all_gather(total_row, DP_ROWS))]
    ppermute x9 -> x18, waiting for transfers between devices: 48.6 us -> 72.1 us  [shifted(): return lax.ppermute(array, DP_ROWS, along(stage, by)) if by else array]
    pallas_call x2 -> x6, Pallas kernels: 43.7 us -> 60.9 us  [the longest x3 57.4 us: update_rows(): pl.pallas_call(functools.partial(update_kernel, sides=sides, first=not ca...]
    ppermute x2 -> x6, waiting for transfers between devices: 1.23 us -> 13.8 us  [swapped(): return lax.ppermute(array, CORE, [(0, 1), (1, 0)])]
    all_to_all x1, waiting for transfers between devices: 3.87 us -> 11 us  [shards(): lax.all_to_all(lists, DP_ROWS, split_axis=0, concat_axis=0, tiled=True)]
    ppermute x9 -> x18, starting transfers between devices: 8.13 us -> 15.2 us  [shifted(): return lax.ppermute(array, DP_ROWS, along(stage, by)) if by else array]
    ppermute x2 -> x6, starting transfers between devices: 0.5 us -> 6.25 us  [swapped(): return lax.ppermute(array, CORE, [(0, 1), (1, 0)])]
    unnamed x18 -> x28, local copies, waits for them, and re-layouts: 2.92 us -> 6.26 us
  transfers between devices with their start and end apart: 13 -> 26, of which waited for: 10 -> 19; matrix products, arithmetic and copies ran while one was open for 2% -> 1% of each run, Pallas kernels for 11% -> 27%
where the time goes in v7:
time: 276 us
  Pallas kernels  110 us (40%)
  waiting for transfers between devices  103 us (37%)
  starting transfers between devices  33 us (12%)
  between operations  14.2 us (5%)
  local copies, waits for them, and re-layouts  8.65 us (3%)
  matrix products  6.45 us (2%)
    ppermute x18, waiting for transfers between devices, shifted(): return lax.ppermute(array, DP_ROWS, along(stage, by)) if by else array  72.1 us
    pallas_call x3, Pallas kernels, update_rows(): pl.pallas_call(functools.partial(update_kernel, sides=sides, first=not ca...  57.4 us
    pallas_call x6, Pallas kernels, partial_sums(): pl.pallas_call(functools.partial(partial_kernel, first=firsts[0], first_s...  40.1 us
    ppermute x18, starting transfers between devices, shifted(): return lax.ppermute(array, DP_ROWS, along(stage, by)) if by else array  15.2 us
    ppermute x6, waiting for transfers between devices, swapped(): return lax.ppermute(array, CORE, [(0, 1), (1, 0)])  13.8 us
    all_to_all x1, starting transfers between devices, shards(): lax.all_to_all(lists, DP_ROWS, split_axis=0, concat_axis=0, tiled=True)  11.5 us
    all_to_all x1, waiting for transfers between devices, shards(): lax.all_to_all(lists, DP_ROWS, split_axis=0, concat_axis=0, tiled=True)  11 us
    dot_general x1, matrix products, shards(): jnp.dot(item_table.T, item_table, precision=lax.Precision.HIGHEST, prefer...  6.45 us
  transfers between devices with their start and end apart: 26, of which 19 were waited for; matrix products, arithmetic and copies ran while one was open for 1% of the time, Pallas kernels for 27%

profile of v7, /device:TPU:1, one launch (start us, length us, event | category | flops | bytes accessed | tf_op | source)
XLA Modules:
  0.0 275.9 jit_solution(17519818439830309511)
XLA Ops:
  7.2 6.4 %fusion.gram_ref = f32[128,128]{1,0:T(8,128)} fusion(f32[4096,128]{1,0:T(8,128)} %refs_4_.1), kind=kOutput, calls=%fused_computation.15 | convolution fusion | flops 805306368 | bytes 2162688 | tf_op jit(solution)/shard_map/dot_general | solution.py:422
  13.7 5.7 %request_lists.1 = f32[128,4,128]{2,1,0:T(4,128)} custom-call(s32[50,128]{1,0:T(8,128)} %bitcast.37, s32[1,128]{1,0:T(1,128)} %bitcast.39, f32[128,128]{1,0:T(8,128)} %fusion.gram_ref), custom_call_target="tpu_custom_call" | custom-call | tf_op jit(solution)/shard_map/request_lists/pallas_call | solution.py:126
  19.4 11.5 %all-to-all-start = ((f32[128,4,128]{2,1,0:T(4,128)}), f32[128,4,128]{2,1,0:T(4,128)S(1)}, u32[]{:S(2)}, u32[]{:S(2)}) async-start(f32[128,4,128]{2,1,0:T(4,128)} %request_lists.1), calls=%async_computation | async-start | bytes 524288 | tf_op jit(solution)/shard_map/all_to_all | solution.py:429
  31.1 0.2 select_reduce_fusion
  31.4 11.0 %all-to-all-done = f32[128,4,128]{2,1,0:T(4,128)S(1)} async-done(((f32[128,4,128]{2,1,0:T(4,128)}), f32[128,4,128]{2,1,0:T(4,128)S(1)}, u32[]{:S(2)}, u32[]{:S(2)}) %all-to-all-start) | async-done | bytes 262176 | tf_op jit(solution)/shard_map/all_to_all | solution.py:429
  42.3 0.2 slice_reduce_fusion
  42.5 7.8 %partial_sums.6 = f32[2,4,4,256,128]{4,3,2,1,0:T(8,128)} custom-call(s32[16384]{0:T(1024)S(1)} %compare_select_fusion.rows_ref, s32[7]{0:T(128)S(1)} %pad_add_fusion.2.plane_ref, f32[4096,128]{1,0:T(8,128)S(1)} %copy-done, f32[128,128]{1,0:T(8,128)S(1)} %bitcast.25), custom_call_target="tpu_custom_call" | custom-call | tf_op jit(solution)/shard_map/partial_sums/pallas_call | solution.py:180
  50.3 0.5 collective-permute-start
  50.8 7.7 %partial_sums.8 = f32[2,4,4,256,128]{4,3,2,1,0:T(8,128)} custom-call(s32[16384]{0:T(1024)S(1)} %compare_select_fusion.rows_ref, s32[7]{0:T(128)S(1)} %pad_add_fusion.2.plane_ref, f32[4096,128]{1,0:T(8,128)S(1)} %copy-done, f32[128,128]{1,0:T(8,128)S(1)} %bitcast.26), custom_call_target="tpu_custom_call" | custom-call | tf_op jit(solution)/shard_map/partial_sums/pallas_call | solution.py:180
  58.6 6.4 %partial_sums.10 = f32[1,4,4,256,128]{4,3,2,1,0:T(8,128)} custom-call(s32[16384]{0:T(1024)S(1)} %compare_select_fusion.rows_ref, s32[7]{0:T(128)S(1)} %pad_add_fusion.1.plane_ref, f32[4096,128]{1,0:T(8,128)S(1)} %copy-done, f32[128,128]{1,0:T(8,128)S(1)} %bitcast.27, f32[2,4,4,256,128]{4,3,2,1,0:T(8,128)} %collective-permute-done.refs_0_), custom_call_target="tpu_custom_call" | custom-call | tf_op jit(solution)/shard_map/partial_sums/pallas_call | solution.py:180
  65.0 0.7 collective-permute-start.3
  65.7 0.3 collective-permute-done.1.refs_0_
  66.0 6.4 %partial_sums.11 = f32[1,4,4,256,128]{4,3,2,1,0:T(8,128)} custom-call(s32[16384]{0:T(1024)S(1)} %compare_select_fusion.rows_ref, s32[7]{0:T(128)S(1)} %pad_add_fusion.1.plane_ref, f32[4096,128]{1,0:T(8,128)S(1)} %copy-done, f32[128,128]{1,0:T(8,128)S(1)} %bitcast.28, f32[2,4,4,256,128]{4,3,2,1,0:T(8,128)} %collective-permute-done.1.refs_0_), custom_call_target="tpu_custom_call" | custom-call | tf_op jit(solution)/shard_map/partial_sums/pallas_call | solution.py:180
  72.4 1.9 collective-permute-start.4
  74.3 6.4 %partial_sums.9 = f32[1,4,4,256,128]{4,3,2,1,0:T(8,128)} custom-call(s32[16384]{0:T(1024)S(1)} %compare_select_fusion.rows_ref, s32[7]{0:T(128)S(1)} %pad_add_fusion.1.plane_ref, f32[4096,128]{1,0:T(8,128)S(1)} %copy-done, f32[128,128]{1,0:T(8,128)S(1)} %bitcast.29, f32[2,4,4,256,128]{4,3,2,1,0:T(8,128)} %collective-permute-done.1.refs_0_), custom_call_target="tpu_custom_call" | custom-call | tf_op jit(solution)/shard_map/partial_sums/pallas_call | solution.py:180
  80.7 0.6 broadcast_in_dim.53
  81.4 5.4 %partial_sums.7 = f32[1,4,4,256,128]{4,3,2,1,0:T(8,128)S(1)} custom-call(s32[16384]{0:T(1024)S(1)} %compare_select_fusion.rows_ref, s32[7]{0:T(128)S(1)} %pad_add_fusion.1.plane_ref, f32[4096,128]{1,0:T(8,128)S(1)} %copy-done, f32[128,128]{1,0:T(8,128)S(1)} %bitcast.30, f32[2,4,4,256,128]{4,3,2,1,0:T(8,128)} %collective-permute-done.refs_0_), custom_call_target="tpu_custom_call" | custom-call | tf_op jit(solution)/shard_map/partial_sums/pallas_call | solution.py:180
  86.8 5.3 %collective-permute-done.3.refs_2_ = f32[4,4,256,128]{3,2,1,0:T(8,128)} collective-permute-done((f32[4,4,256,128]{3,2,1,0:T(8,128)}, f32[4,4,256,128]{3,2,1,0:T(8,128)}, u32[]{:S(2)}, u32[]{:S(2)}) %collective-permute-start.3) | collective-permute-done | bytes 2097184 | tf_op jit(solution)/shard_map/ppermute | solution.py:223
  92.0 20.5 %collective-permute-done.4.refs_3_ = f32[4,4,256,128]{3,2,1,0:T(8,128)} collective-permute-done((f32[4,4,256,128]{3,2,1,0:T(8,128)}, f32[4,4,256,128]{3,2,1,0:T(8,128)}, u32[]{:S(2)}, u32[]{:S(2)}) %collective-permute-start.4) | collective-permute-done | bytes 2097184 | tf_op jit(solution)/shard_map/ppermute | solution.py:223
  112.5 2.1 collective-permute-done.2.refs_1_
  114.7 3.3 %sum_stage_1.1 = (f32[4,256,128]{2,1,0:T(8,128)S(1)}, f32[4,256,128]{2,1,0:T(8,128)S(1)}, f32[4,256,128]{2,1,0:T(8,128)S(1)}, f32[4,256,128]{2,1,0:T(8,128)S(1)}) custom-call(f32[4,4,256,128]{3,2,1,0:T(8,128)S(1)} %bitcast.24, f32[4,4,256,128]{3,2,1,0:T(8,128)} %collective-permute-done.2.refs_1_, f32[4,4,256,128]{3,2,1,0:T(8,128)} %collective-permute-done.3.refs_2_, ...), custom_call_target="tpu_custom_call" | custom-call | tf_op jit(solution)/shard_map/sum_stage_1/pallas_call | solution.py:204
  117.9 0.4 collective-permute-start.5
  118.3 1.6 collective-permute-start.6
  120.0 0.9 collective-permute-start.7
  120.8 12.8 %collective-permute-done.5.refs_1_ = f32[4,256,128]{2,1,0:T(8,128)S(1)} collective-permute-done((f32[4,256,128]{2,1,0:T(8,128)S(1)}, f32[4,256,128]{2,1,0:T(8,128)S(1)}, u32[]{:S(2)}, u32[]{:S(2)}) %collective-permute-start.5) | collective-permute-done | bytes 524320 | tf_op jit(solution)/shard_map/ppermute | solution.py:223
  133.6 0.6 collective-permute-done.7.refs_3_
  134.2 0.1 sum_stage_2.1
  134.4 0.6 copy-done.4
  135.0 2.1 collective-permute-start.9
  137.1 0.6 collective-permute-start.10
  137.7 6.0 %all-gather.3.cloned.1.call-done = f32[2048,128]{1,0:T(8,128)} async-done(((f32[16,128]{1,0:T(8,128)}), f32[2048,128]{1,0:T(8,128)}) %all-gather.3.cloned.1.call-update) | async-done | bytes 1048592 | tf_op jit(solution)/shard_map/all_gather | solution.py:435
  143.7 1.7 slice.19
  145.4 0.6 copy-done.8
  146.1 1.9 user_block.1.refs_0_
  148.1 2.2 collective-permute-start.13
  150.3 0.6 collective-permute-start.11
  150.9 3.2 %collective-permute-done.13.refs_3_ = f32[264,128]{1,0:T(8,128)S(1)} collective-permute-done((f32[264,128]{1,0:T(8,128)}, f32[264,128]{1,0:T(8,128)S(1)}, u32[]{:S(2)}, u32[]{:S(2)}) %collective-permute-start.13) | collective-permute-done | bytes 135200 | tf_op jit(solution)/shard_map/ppermute | solution.py:223
  154.0 1.9 collective-permute-done.12.refs_2_
  156.0 1.3 collective-permute-done.11.refs_1_
  157.3 0.9 copy-done.3
  158.3 1.7 collective-permute-start.16
  159.9 0.2 collective-permute-start.15
  160.1 0.5 collective-permute-start.14
  160.6 11.4 %collective-permute-done.16.refs_3_ = f32[4,264,128]{2,1,0:T(8,128)S(1)} collective-permute-done((f32[4,264,128]{2,1,0:T(8,128)S(1)}, f32[4,264,128]{2,1,0:T(8,128)S(1)}, u32[]{:S(2)}, u32[]{:S(2)}) %collective-permute-start.16) | collective-permute-done | bytes 540704 | tf_op jit(solution)/shard_map/ppermute | solution.py:223
  172.0 3.6 %collective-permute-done.14.refs_1_ = f32[4,264,128]{2,1,0:T(8,128)S(1)} collective-permute-done((f32[4,264,128]{2,1,0:T(8,128)S(1)}, f32[4,264,128]{2,1,0:T(8,128)S(1)}, u32[]{:S(2)}, u32[]{:S(2)}) %collective-permute-start.14) | collective-permute-done | bytes 540704 | tf_op jit(solution)/shard_map/ppermute | solution.py:223
  175.6 1.5 stack_blocks.3.refs_0_
  177.2 3.6 %collective-permute-start.19 = (f32[4,4,264,128]{3,2,1,0:T(8,128)}, f32[4,4,264,128]{3,2,1,0:T(8,128)}, u32[]{:S(2)}, u32[]{:S(2)}) collective-permute-start(f32[4,4,264,128]{3,2,1,0:T(8,128)} %stack_blocks.3.refs_0_), channel_id=1, source_target_pairs={{0,16},{16,0},{1,17},{17,1},{2,18},{18,2},{3,19},{19,3},{4,20},{20... | collective-permute-start | bytes 6488072 | tf_op jit(solution)/shard_map/ppermute | solution.py:238
  180.8 0.5 collective-permute-start.18
  181.3 1.0 collective-permute-start.17
  182.3 2.7 collective-permute-done.19.refs_1_
  185.0 14.3 %add_rows.2 = (f32[4104,128]{1,0:T(8,128)S(1)}, f32[128,256]{1,0:T(8,128)S(1)}) custom-call(s32[16384]{0:T(1024)S(1)} %bitcast.33, s32[16384]{0:T(1024)S(1)} %maximum_bitcast_fusion.code_idx_ref, s32[14]{0:T(128)S(1)} %concatenate.10.planes_ref, f32[4,4,264,128]{3,2,1,0:T(8,128)} %stack_blocks.3.refs_0_, f32[4,4,264,128]{3,2,1,0:T(8,128)} %collective-permute-done.19.refs_1_), custom_call_target="tpu_custom_call" | custom-call | tf_op jit(solution)/shard_map/add_rows/pallas_call | solution.py:396
  199.3 7.7 %collective-permute-done.18.refs_1_ = f32[4,4,264,128]{3,2,1,0:T(8,128)} collective-permute-done((f32[4,4,264,128]{3,2,1,0:T(8,128)}, f32[4,4,264,128]{3,2,1,0:T(8,128)}, u32[]{:S(2)}, u32[]{:S(2)}) %collective-permute-start.18) | collective-permute-done | bytes 2162720 | tf_op jit(solution)/shard_map/ppermute | solution.py:223
  207.0 1.7 collective-permute-done.17.refs_0_
  208.7 1.7 collective-permute-start.21
  210.4 0.4 collective-permute-start.20
  210.8 6.8 %collective-permute-done.21.refs_2_ = f32[4,4,264,128]{3,2,1,0:T(8,128)S(1)} collective-permute-done((f32[4,4,264,128]{3,2,1,0:T(8,128)}, f32[4,4,264,128]{3,2,1,0:T(8,128)S(1)}, u32[]{:S(2)}, u32[]{:S(2)}) %collective-permute-start.21) | collective-permute-done | bytes 2162720 | tf_op jit(solution)/shard_map/ppermute | solution.py:238
  217.5 0.2 collective-permute-done.22.refs_3_
  217.7 1.2 copy-done.6
  218.9 23.4 %add_rows.3 = (f32[4104,128]{1,0:T(8,128)S(1)}, f32[128,256]{1,0:T(8,128)S(1)}) custom-call(s32[16384]{0:T(1024)S(1)} %bitcast.34, s32[16384]{0:T(1024)S(1)} %maximum_bitcast_fusion.code_idx_ref, s32[14]{0:T(128)S(1)} %concatenate.10.planes_ref, f32[4,4,264,128]{3,2,1,0:T(8,128)} %collective-permute-done.17.refs_0_, ...), custom_call_target="tpu_custom_call" | custom-call | tf_op jit(solution)/shard_map/add_rows/pallas_call | solution.py:396
  242.3 1.4 copy-done.1
  243.7 0.4 collective-permute-start.23
  244.1 3.9 %collective-permute-done.23.refs_1_ = f32[4,4,264,128]{3,2,1,0:T(8,128)S(1)} collective-permute-done((f32[4,4,264,128]{3,2,1,0:T(8,128)S(1)}, f32[4,4,264,128]{3,2,1,0:T(8,128)S(1)}, u32[]{:S(2)}, u32[]{:S(2)}) %collective-permute-start.23) | collective-permute-done | bytes 2162720 | tf_op jit(solution)/shard_map/ppermute | solution.py:238
  248.0 1.3 copy-done.7
  249.4 19.7 %update_rows.1 = (f32[4096,128]{1,0:T(8,128)}, f32[4096,128]{1,0:T(8,128)}) custom-call(s32[16384]{0:T(1024)S(1)} %bitcast.35, s32[16384]{0:T(1024)S(1)} %maximum_bitcast_fusion.code_idx_ref, s32[14]{0:T(128)S(1)} %concatenate.10.planes_ref, f32[4,4,264,128]{3,2,1,0:T(8,128)} %copy-done.5, f32[4,4,264,128]{3,2,1,0:T(8,128)} %copy-done.7, ...), custom_call_target="tpu_custom_call" | custom-call | tf_op jit(solution)/shard_map/update_rows/pallas_call | solution.py:396
  (44 shorter events, 0.6 us)
Async XLA Ops:
  7.2 23.8 %copy-start.11 = (s32[3]{0:T(128)S(1)}, s32[3]{0:T(128)}, u32[]{:S(2)}) copy-start(s32[3]{0:T(128)} %constant.36.clone) | copy-start | bytes 40
  7.2 23.8 %copy-start.12 = (s32[3]{0:T(128)S(1)}, s32[3]{0:T(128)}, u32[]{:S(2)}) copy-start(s32[3]{0:T(128)} %constant.35.clone) | copy-start | bytes 40
  7.2 23.9 %copy-start.13 = (s32[4]{0:T(128)S(1)}, s32[4]{0:T(128)}, u32[]{:S(2)}) copy-start(s32[4]{0:T(128)} %constant.34.clone) | copy-start | bytes 52
  7.2 35.3 %copy-start = (f32[4096,128]{1,0:T(8,128)S(1)}, f32[4096,128]{1,0:T(8,128)}, u32[]{:S(2)}) copy-start(f32[4096,128]{1,0:T(8,128)} %refs_4_.1) | copy-start | bytes 6291460
  19.4 22.9 %all-to-all-start = ((f32[128,4,128]{2,1,0:T(4,128)}), f32[128,4,128]{2,1,0:T(4,128)S(1)}, u32[]{:S(2)}, u32[]{:S(2)}) async-start(f32[128,4,128]{2,1,0:T(4,128)} %request_lists.1), calls=%async_computation | async-start | bytes 524288 | tf_op jit(solution)/shard_map/all_to_all | solution.py:429
  30.9 112.8 %all-gather.3.cloned.1.call-start = ((), (), s32[]{:S(2)}) async-start(), calls=%async_computation.1 | async-start | bytes 1056768 | tf_op jit(solution)/shard_map/all_gather | solution.py:435
  50.3 8.3 %collective-permute-start = (f32[2,4,4,256,128]{4,3,2,1,0:T(8,128)}, f32[2,4,4,256,128]{4,3,2,1,0:T(8,128)}, u32[]{:S(2)}, u32[]{:S(2)}) collective-permute-start(f32[2,4,4,256,128]{4,3,2,1,0:T(8,128)} %partial_sums.6), channel_id=1, source_target_pairs={{0,16},{16,0},{1,17},{17,1},{2,18},{18,2},{3,19},{19,3},{4,20},{20... | collective-permute-start | bytes 12582920 | tf_op jit(solution)/shard_map/ppermute | solution.py:238
  58.5 7.5 %collective-permute-start.1 = (f32[2,4,4,256,128]{4,3,2,1,0:T(8,128)}, f32[2,4,4,256,128]{4,3,2,1,0:T(8,128)}, u32[]{:S(2)}, u32[]{:S(2)}) collective-permute-start(f32[2,4,4,256,128]{4,3,2,1,0:T(8,128)} %partial_sums.8), channel_id=1, source_target_pairs={{0,16},{16,0},{1,17},{17,1},{2,18},{18,2},{3,19},{19,3},{4,20},{20... | collective-permute-start | bytes 12582920 | tf_op jit(solution)/shard_map/ppermute | solution.py:238
  65.0 27.0 %collective-permute-start.3 = (f32[4,4,256,128]{3,2,1,0:T(8,128)}, f32[4,4,256,128]{3,2,1,0:T(8,128)}, u32[]{:S(2)}, u32[]{:S(2)}) collective-permute-start(f32[4,4,256,128]{3,2,1,0:T(8,128)} %bitcast.13), channel_id=1, source_target_pairs={{0,64},{1,65},{2,66},{3,67},{4,68},{5,69},{6,70},{7,71},{8,72},{9,... | collective-permute-start | bytes 6291464 | tf_op jit(solution)/shard_map/ppermute | solution.py:223
  72.4 40.1 %collective-permute-start.4 = (f32[4,4,256,128]{3,2,1,0:T(8,128)}, f32[4,4,256,128]{3,2,1,0:T(8,128)}, u32[]{:S(2)}, u32[]{:S(2)}) collective-permute-start(f32[4,4,256,128]{3,2,1,0:T(8,128)} %bitcast.14), channel_id=1, source_target_pairs={{0,96},{1,97},{2,98},{3,99},{4,100},{5,101},{6,102},{7,103},{8,104... | collective-permute-start | bytes 6291464 | tf_op jit(solution)/shard_map/ppermute | solution.py:223
  80.7 33.9 %collective-permute-start.2 = (f32[4,4,256,128]{3,2,1,0:T(8,128)}, f32[4,4,256,128]{3,2,1,0:T(8,128)}, u32[]{:S(2)}, u32[]{:S(2)}) collective-permute-start(f32[4,4,256,128]{3,2,1,0:T(8,128)} %bitcast.12), channel_id=1, source_target_pairs={{0,32},{1,33},{2,34},{3,35},{4,36},{5,37},{6,38},{7,39},{8,40},{9,... | collective-permute-start | bytes 6291464 | tf_op jit(solution)/shard_map/ppermute | solution.py:223
  117.9 15.7 %collective-permute-start.5 = (f32[4,256,128]{2,1,0:T(8,128)S(1)}, f32[4,256,128]{2,1,0:T(8,128)S(1)}, u32[]{:S(2)}, u32[]{:S(2)}) collective-permute-start(f32[4,256,128]{2,1,0:T(8,128)S(1)} %get-tuple-element.23), channel_id=1, source_target_pairs={{0,4},{1,5},{2,6},{3,7},{4,8},{5,9},{6,10},{7,11},{8,12},{9,13},{1... | collective-permute-start | bytes 1572872 | tf_op jit(solution)/shard_map/ppermute | solution.py:223
  118.3 15.3 %collective-permute-start.6 = (f32[4,256,128]{2,1,0:T(8,128)S(1)}, f32[4,256,128]{2,1,0:T(8,128)S(1)}, u32[]{:S(2)}, u32[]{:S(2)}) collective-permute-start(f32[4,256,128]{2,1,0:T(8,128)S(1)} %get-tuple-element.24), channel_id=1, source_target_pairs={{0,8},{1,9},{2,10},{3,11},{4,12},{5,13},{6,14},{7,15},{8,0},{9,1},... | collective-permute-start | bytes 1572872 | tf_op jit(solution)/shard_map/ppermute | solution.py:223
  120.0 14.3 %collective-permute-start.7 = (f32[4,256,128]{2,1,0:T(8,128)S(1)}, f32[4,256,128]{2,1,0:T(8,128)S(1)}, u32[]{:S(2)}, u32[]{:S(2)}) collective-permute-start(f32[4,256,128]{2,1,0:T(8,128)S(1)} %get-tuple-element.25), channel_id=1, source_target_pairs={{0,12},{1,13},{2,14},{3,15},{4,0},{5,1},{6,2},{7,3},{8,4},{9,5},{1... | collective-permute-start | bytes 1572872 | tf_op jit(solution)/shard_map/ppermute | solution.py:223
  134.3 0.7 copy-start.4
  135.0 10.4 %collective-permute-start.8 = (f32[256,128]{1,0:T(8,128)S(1)}, f32[256,128]{1,0:T(8,128)S(1)}, u32[]{:S(2)}, u32[]{:S(2)}) collective-permute-start(f32[256,128]{1,0:T(8,128)S(1)} %get-tuple-element.27), channel_id=1, source_target_pairs={{0,1},{1,2},{2,3},{3,0},{4,5},{5,6},{6,7},{7,4},{8,9},{9,10},{10,1... | collective-permute-start | bytes 393224 | tf_op jit(solution)/shard_map/ppermute | solution.py:223
  135.0 10.4 %collective-permute-start.9 = (f32[256,128]{1,0:T(8,128)S(1)}, f32[256,128]{1,0:T(8,128)S(1)}, u32[]{:S(2)}, u32[]{:S(2)}) collective-permute-start(f32[256,128]{1,0:T(8,128)S(1)} %get-tuple-element.28), channel_id=1, source_target_pairs={{0,2},{1,3},{2,0},{3,1},{4,6},{5,7},{6,4},{7,5},{8,10},{9,11},{10,... | collective-permute-start | bytes 393224 | tf_op jit(solution)/shard_map/ppermute | solution.py:223
  137.1 8.3 %collective-permute-start.10 = (f32[256,128]{1,0:T(8,128)S(1)}, f32[256,128]{1,0:T(8,128)S(1)}, u32[]{:S(2)}, u32[]{:S(2)}) collective-permute-start(f32[256,128]{1,0:T(8,128)S(1)} %get-tuple-element.29), channel_id=1, source_target_pairs={{0,3},{1,0},{2,1},{3,2},{4,7},{5,4},{6,5},{7,6},{8,11},{9,8},{10,9... | collective-permute-start | bytes 393224 | tf_op jit(solution)/shard_map/ppermute | solution.py:223
  145.4 0.6 copy-start.8
  145.4 0.7 copy-start.9
  145.4 0.7 copy-start.10
  148.1 6.0 %collective-permute-start.13 = (f32[264,128]{1,0:T(8,128)}, f32[264,128]{1,0:T(8,128)S(1)}, u32[]{:S(2)}, u32[]{:S(2)}) collective-permute-start(f32[264,128]{1,0:T(8,128)} %user_block.1.refs_0_), channel_id=1, source_target_pairs={{0,3},{1,0},{2,1},{3,2},{4,7},{5,4},{6,5},{7,6},{8,11},{9,8},{10,9... | collective-permute-start | bytes 405512 | tf_op jit(solution)/shard_map/ppermute | solution.py:223
  150.3 5.7 %collective-permute-start.12 = (f32[264,128]{1,0:T(8,128)}, f32[264,128]{1,0:T(8,128)S(1)}, u32[]{:S(2)}, u32[]{:S(2)}) collective-permute-start(f32[264,128]{1,0:T(8,128)} %user_block.1.refs_0_), channel_id=1, source_target_pairs={{0,2},{1,3},{2,0},{3,1},{4,6},{5,7},{6,4},{7,5},{8,10},{9,11},{10,... | collective-permute-start | bytes 405512 | tf_op jit(solution)/shard_map/ppermute | solution.py:223
  150.3 7.0 %collective-permute-start.11 = (f32[264,128]{1,0:T(8,128)}, f32[264,128]{1,0:T(8,128)S(1)}, u32[]{:S(2)}, u32[]{:S(2)}) collective-permute-start(f32[264,128]{1,0:T(8,128)} %user_block.1.refs_0_), channel_id=1, source_target_pairs={{0,1},{1,2},{2,3},{3,0},{4,5},{5,6},{6,7},{7,4},{8,9},{9,10},{10,1... | collective-permute-start | bytes 405512 | tf_op jit(solution)/shard_map/ppermute | solution.py:223
  157.3 0.9 copy-start.3
  158.3 13.8 %collective-permute-start.16 = (f32[4,264,128]{2,1,0:T(8,128)S(1)}, f32[4,264,128]{2,1,0:T(8,128)S(1)}, u32[]{:S(2)}, u32[]{:S(2)}) collective-permute-start(f32[4,264,128]{2,1,0:T(8,128)S(1)} %stack_blocks.2.refs_0_), channel_id=1, source_target_pairs={{0,12},{1,13},{2,14},{3,15},{4,0},{5,1},{6,2},{7,3},{8,4},{9,5},{1... | collective-permute-start | bytes 1622024 | tf_op jit(solution)/shard_map/ppermute | solution.py:223
  159.9 12.1 %collective-permute-start.15 = (f32[4,264,128]{2,1,0:T(8,128)S(1)}, f32[4,264,128]{2,1,0:T(8,128)S(1)}, u32[]{:S(2)}, u32[]{:S(2)}) collective-permute-start(f32[4,264,128]{2,1,0:T(8,128)S(1)} %stack_blocks.2.refs_0_), channel_id=1, source_target_pairs={{0,8},{1,9},{2,10},{3,11},{4,12},{5,13},{6,14},{7,15},{8,0},{9,1},... | collective-permute-start | bytes 1622024 | tf_op jit(solution)/shard_map/ppermute | solution.py:223
  160.1 15.5 %collective-permute-start.14 = (f32[4,264,128]{2,1,0:T(8,128)S(1)}, f32[4,264,128]{2,1,0:T(8,128)S(1)}, u32[]{:S(2)}, u32[]{:S(2)}) collective-permute-start(f32[4,264,128]{2,1,0:T(8,128)S(1)} %stack_blocks.2.refs_0_), channel_id=1, source_target_pairs={{0,4},{1,5},{2,6},{3,7},{4,8},{5,9},{6,10},{7,11},{8,12},{9,13},{1... | collective-permute-start | bytes 1622024 | tf_op jit(solution)/shard_map/ppermute | solution.py:223
  177.2 7.8 %collective-permute-start.19 = (f32[4,4,264,128]{3,2,1,0:T(8,128)}, f32[4,4,264,128]{3,2,1,0:T(8,128)}, u32[]{:S(2)}, u32[]{:S(2)}) collective-permute-start(f32[4,4,264,128]{3,2,1,0:T(8,128)} %stack_blocks.3.refs_0_), channel_id=1, source_target_pairs={{0,16},{16,0},{1,17},{17,1},{2,18},{18,2},{3,19},{19,3},{4,20},{20... | collective-permute-start | bytes 6488072 | tf_op jit(solution)/shard_map/ppermute | solution.py:238
  180.8 26.2 %collective-permute-start.18 = (f32[4,4,264,128]{3,2,1,0:T(8,128)}, f32[4,4,264,128]{3,2,1,0:T(8,128)}, u32[]{:S(2)}, u32[]{:S(2)}) collective-permute-start(f32[4,4,264,128]{3,2,1,0:T(8,128)} %stack_blocks.3.refs_0_), channel_id=1, source_target_pairs={{0,96},{1,97},{2,98},{3,99},{4,100},{5,101},{6,102},{7,103},{8,104... | collective-permute-start | bytes 6488072 | tf_op jit(solution)/shard_map/ppermute | solution.py:223
  181.3 27.4 %collective-permute-start.17 = (f32[4,4,264,128]{3,2,1,0:T(8,128)}, f32[4,4,264,128]{3,2,1,0:T(8,128)}, u32[]{:S(2)}, u32[]{:S(2)}) collective-permute-start(f32[4,4,264,128]{3,2,1,0:T(8,128)} %stack_blocks.3.refs_0_), channel_id=1, source_target_pairs={{0,32},{1,33},{2,34},{3,35},{4,36},{5,37},{6,38},{7,39},{8,40},{9,... | collective-permute-start | bytes 6488072 | tf_op jit(solution)/shard_map/ppermute | solution.py:223
  208.7 40.7 %copy-start.2 = (f32[4096,128]{1,0:T(8,128)S(1)}, f32[4096,128]{1,0:T(8,128)}, u32[]{:S(2)}) copy-start(f32[4096,128]{1,0:T(8,128)} %refs_5_.1) | copy-start | bytes 6291460
  208.7 8.8 %collective-permute-start.21 = (f32[4,4,264,128]{3,2,1,0:T(8,128)}, f32[4,4,264,128]{3,2,1,0:T(8,128)S(1)}, u32[]{:S(2)}, u32[]{:S(2)}) collective-permute-start(f32[4,4,264,128]{3,2,1,0:T(8,128)} %collective-permute-done.17.refs_0_), channel_id=1, source_target_pairs={{0,16},{16,0},{1,17},{17,1},{2,18},{18,2},{3,19},{19,3},{4,20},{20... | collective-permute-start | bytes 6488072 | tf_op jit(solution)/shard_map/ppermute | solution.py:238
  210.4 7.3 %collective-permute-start.22 = (f32[4,4,264,128]{3,2,1,0:T(8,128)}, f32[4,4,264,128]{3,2,1,0:T(8,128)}, u32[]{:S(2)}, u32[]{:S(2)}) collective-permute-start(f32[4,4,264,128]{3,2,1,0:T(8,128)} %collective-permute-done.18.refs_1_), channel_id=1, source_target_pairs={{0,16},{16,0},{1,17},{17,1},{2,18},{18,2},{3,19},{19,3},{4,20},{20... | collective-permute-start | bytes 6488072 | tf_op jit(solution)/shard_map/ppermute | solution.py:238
  210.4 33.3 %collective-permute-start.20 = (f32[4,4,264,128]{3,2,1,0:T(8,128)}, f32[4,4,264,128]{3,2,1,0:T(8,128)S(1)}, u32[]{:S(2)}, u32[]{:S(2)}) collective-permute-start(f32[4,4,264,128]{3,2,1,0:T(8,128)} %stack_blocks.3.refs_0_), channel_id=1, source_target_pairs={{0,64},{1,65},{2,66},{3,67},{4,68},{5,69},{6,70},{7,71},{8,72},{9,... | collective-permute-start | bytes 6488072 | tf_op jit(solution)/shard_map/ppermute | solution.py:223
  217.5 1.4 copy-start.6
  242.3 1.4 copy-start.1
  243.7 4.3 %copy-start.5 = (f32[4,4,264,128]{3,2,1,0:T(8,128)}, f32[4,4,264,128]{3,2,1,0:T(8,128)S(1)}, u32[]{:S(2)}) copy-start(f32[4,4,264,128]{3,2,1,0:T(8,128)S(1)} %collective-permute-done.20.refs_0_) | copy-start | bytes 6488068
  243.7 4.3 %collective-permute-start.23 = (f32[4,4,264,128]{3,2,1,0:T(8,128)S(1)}, f32[4,4,264,128]{3,2,1,0:T(8,128)S(1)}, u32[]{:S(2)}, u32[]{:S(2)}) collective-permute-start(f32[4,4,264,128]{3,2,1,0:T(8,128)S(1)} %collective-permute-done.20.refs_0_), channel_id=1, source_target_pairs={{0,16},{16,0},{1,17},{17,1},{2,18},{18,2},{3,19},{19,3},{4,20},{20... | collective-permute-start | bytes 6488072 | tf_op jit(solution)/shard_map/ppermute | solution.py:238
  248.0 1.3 copy-start.7
Sparse Core Ops, SparseCore 0:
  81.5 62.1 all-gather.2

commit v8 on v7

--- a/solution.py
+++ b/solution.py
@@ -62,7 +62,7 @@
     return halves[:, :LANES] + (cross + cross.T)
 
 
-def list_kernel(history_ref, positive_ref, gram_ref, out_ref, *, slots, rows_dev):
+def list_kernel(history_ref, positive_ref, table_ref, out_ref, *, slots, rows_dev):
     shift = rows_dev.bit_length() - 1
     sq = (LANES, LANES)
     ids = jnp.concatenate(
@@ -83,6 +83,9 @@
     ones = one.astype(bf16)
     carry = jnp.zeros(sq, f32)
     acc = jnp.zeros((3 * LANES, LANES), f32)
+    halves = jnp.zeros((LANES, 2 * LANES), f32)
+    for at in range(0, rows_dev, 1024):
+        halves = halves + half_gram(table_ref[at : at + 1024, :])
     for start in range(0, slots, GROUP):
         group = range(start, start + GROUP)
         members = [owner_c[:, h : h + 1] == lane for h in group]
@@ -117,17 +120,19 @@
     present = high > 0
     out_ref[:, 0, :] = jnp.where(present, (high - 1) * 64 + low, rows_dev).astype(f32)
     out_ref[:, 1, :] = jnp.where(present, code, -1).astype(f32)
-    out_ref[:, 2, :] = gram_ref[...]
+    out_ref[:, 2, :] = whole_gram(halves)
     out_ref[:, 3, :] = zero
 
 
-def request_lists(history_ids, positive_ids, gram, rows_dev):
+def request_lists(history_ids, positive_ids, table):
+    rows_dev = table.shape[0]
     users, hist_len = history_ids.shape
     return pl.pallas_call(
         functools.partial(list_kernel, slots=hist_len + 1, rows_dev=rows_dev),
         out_shape=jax.ShapeDtypeStruct((LANES, 4, LANES), f32),
+        compiler_params=pltpu.CompilerParams(vmem_limit_bytes=16 * 2**20),
         name="request_lists",
-    )(history_ids.T, positive_ids.reshape(1, users), gram)
+    )(history_ids.T, positive_ids.reshape(1, users), table)
 
 
 def partial_kernel(rows_ref, plane_ref, table_ref, codes_ref, *refs, first, first_step):
@@ -189,7 +194,7 @@
             scratch_shapes=[pltpu.VMEM((LANES, width), f32)] * 8,
         ),
         out_shape=jax.ShapeDtypeStruct((n, 4, 4, SUM_ROWS, width), f32),
-        compiler_params=pltpu.CompilerParams(vmem_limit_bytes=32 * 2**20),
+        compiler_params=pltpu.CompilerParams(vmem_limit_bytes=24 * 2**20),
         name="partial_sums",
     )(*operands)
 
@@ -204,7 +209,7 @@
     return pl.pallas_call(
         split_sum_kernel,
         out_shape=[jax.ShapeDtypeStruct(pieces[0].shape[1:], f32)] * 4,
-        compiler_params=pltpu.CompilerParams(vmem_limit_bytes=40 * 2**20),
+        compiler_params=pltpu.CompilerParams(vmem_limit_bytes=24 * 2**20),
         name=name,
     )(*pieces)
 
@@ -419,13 +424,7 @@
     _, hist_len = history_ids.shape
     devices = lax.axis_size(DP_ROWS)
     coef = penalty_weight / (rows_dev * devices)
-    item_gram = jnp.dot(
-        item_table.T,
-        item_table,
-        precision=lax.Precision.HIGHEST,
-        preferred_element_type=f32,
-    )
-    lists = request_lists(history_ids, positive_ids, item_gram, rows_dev)
+    lists = request_lists(history_ids, positive_ids, item_table)
     asked = lax.all_to_all(lists, DP_ROWS, split_axis=0, concat_axis=0, tiled=True)
     rows = asked[:, 0, :].astype(i32).reshape(-1)
     codes = asked[:, 1, :]
@@ -446,9 +445,10 @@
     carry = update([plane, swapped(plane)], ((0, 0), (1, 0)), rows_dev, (), (), coef)
     plane, *near, carry = lax.optimization_barrier((plane, *near, carry))
     across = shifted(plane, 0, 2)
-    carry = update(
-        [*near, *map(swapped, near)], ((0, 1), (0, 3), (1, 1), (1, 3)), rows_dev, carry, (), coef
-    )
+    far = [swapped(piece) for piece in near]
+    carry = update(near, ((0, 1), (0, 3)), rows_dev, carry, (), coef)
+    *far, carry = lax.optimization_barrier((*far, carry))
+    carry = update(far, ((1, 1), (1, 3)), rows_dev, carry, (), coef)
     across, carry = lax.optimization_barrier((across, carry))
     return tuple(
         update(

time: 276 us -> 293 us (1.062)
  waiting for transfers between devices: 103 us -> 116 us
  matrix products: 6.45 us -> 0 us
  Pallas kernels: 110 us -> 115 us
  local copies, waits for them, and re-layouts: 8.65 us -> 12.4 us
    all_gather x1, waiting for transfers between devices: 5.98 us -> 26.8 us  [shards(): totals = lax.optimization_barrier(lax.all_gather(total_row, DP_ROWS))]
    ppermute x6, waiting for transfers between devices: 13.8 us -> 5.59 us  [swapped(): return lax.ppermute(array, CORE, [(0, 1), (1, 0)])]
    dot_general x1 -> x0, matrix products: 6.45 us -> none  [shards(): jnp.dot(item_table.T, item_table, precision=lax.Precision.HIGHEST, prefer...]
    pallas_call x3 -> x4, Pallas kernels: 57.4 us -> 62.6 us  [update_rows(): pl.pallas_call(functools.partial(update_kernel, sides=sides, first=not ca...]
    unnamed x28 -> x36, local copies, waits for them, and re-layouts: 6.26 us -> 10.1 us
    ppermute x18, starting transfers between devices: 15.2 us -> 18.6 us  [shifted(): return lax.ppermute(array, DP_ROWS, along(stage, by)) if by else array]
  transfers between devices with their start and end apart: 26 -> 26, of which waited for: 19 -> 13; matrix products, arithmetic and copies ran while one was open for 1% -> 1% of each run, Pallas kernels for 27% -> 27%
where the time goes in v8:
time: 293 us; the launch traced here: 292 us
  waiting for transfers between devices  116 us (40%)
  Pallas kernels  115 us (39%)
  starting transfers between devices  34.1 us (12%)
  between operations  14.3 us (5%)
  local copies, waits for them, and re-layouts  12.4 us (4%)
    ppermute x18, waiting for transfers between devices, shifted(): return lax.ppermute(array, DP_ROWS, along(stage, by)) if by else array  72.9 us
    pallas_call x4, Pallas kernels, update_rows(): pl.pallas_call(functools.partial(update_kernel, sides=sides, first=not ca...  62.6 us
    pallas_call x6, Pallas kernels, partial_sums(): pl.pallas_call(functools.partial(partial_kernel, first=firsts[0], first_s...  40.2 us
    all_gather x1, waiting for transfers between devices, shards(): totals = lax.optimization_barrier(lax.all_gather(total_row, DP_ROWS))  26.8 us
    ppermute x18, starting transfers between devices, shifted(): return lax.ppermute(array, DP_ROWS, along(stage, by)) if by else array  18.6 us
    all_to_all x1, starting transfers between devices, shards(): lax.all_to_all(lists, DP_ROWS, split_axis=0, concat_axis=0, tiled=True)  11.5 us
    all_to_all x1, waiting for transfers between devices, shards(): lax.all_to_all(lists, DP_ROWS, split_axis=0, concat_axis=0, tiled=True)  11 us
    unnamed x36, local copies, waits for them, and re-layouts  10.1 us
  transfers between devices with their start and end apart: 26, of which 13 were waited for; matrix products, arithmetic and copies ran while one was open for 1% of the time, Pallas kernels for 27%

profile of v8, /device:TPU:1, one launch (start us, length us, event | category | flops | bytes accessed | tf_op | source)
XLA Modules:
  0.0 292.2 jit_solution(75246894677847791)
XLA Ops:
  7.2 1.6 copy-done
  8.8 0.7 copy-done.6
  9.6 0.7 copy-done.7
  10.2 4.9 %request_lists.1 = f32[128,4,128]{2,1,0:T(4,128)} custom-call(s32[50,128]{1,0:T(8,128)S(1)} %bitcast.35, s32[1,128]{1,0:T(1,128)S(1)} %bitcast.36, f32[4096,128]{1,0:T(8,128)S(1)} %copy-done), custom_call_target="tpu_custom_call" | custom-call | tf_op jit(solution)/shard_map/request_lists/pallas_call | solution.py:130
  15.1 11.5 %all-to-all-start = ((f32[128,4,128]{2,1,0:T(4,128)}), f32[128,4,128]{2,1,0:T(4,128)S(1)}, u32[]{:S(2)}, u32[]{:S(2)}) async-start(f32[128,4,128]{2,1,0:T(4,128)} %request_lists.1), calls=%async_computation | async-start | bytes 524288 | tf_op jit(solution)/shard_map/all_to_all | solution.py:428
  26.7 0.1 pad_add_fusion
  26.8 0.2 select_reduce_fusion
  27.1 11.0 %all-to-all-done = f32[128,4,128]{2,1,0:T(4,128)S(1)} async-done(((f32[128,4,128]{2,1,0:T(4,128)}), f32[128,4,128]{2,1,0:T(4,128)S(1)}, u32[]{:S(2)}, u32[]{:S(2)}) %all-to-all-start) | async-done | bytes 262176 | tf_op jit(solution)/shard_map/all_to_all | solution.py:428
  38.1 0.2 slice_reduce_fusion
  38.3 7.7 %partial_sums.8 = f32[2,4,4,256,128]{4,3,2,1,0:T(8,128)} custom-call(s32[16384]{0:T(1024)S(1)} %compare_select_fusion.rows_ref, s32[7]{0:T(128)S(1)} %pad_add_fusion.2.plane_ref, f32[4096,128]{1,0:T(8,128)S(1)} %copy-done.1, f32[128,128]{1,0:T(8,128)S(1)} %bitcast.23), custom_call_target="tpu_custom_call" | custom-call | tf_op jit(solution)/shard_map/partial_sums/pallas_call | solution.py:185
  46.0 0.5 collective-permute-start.1
  46.5 7.8 %partial_sums.6 = f32[2,4,4,256,128]{4,3,2,1,0:T(8,128)} custom-call(s32[16384]{0:T(1024)S(1)} %compare_select_fusion.rows_ref, s32[7]{0:T(128)S(1)} %pad_add_fusion.2.plane_ref, f32[4096,128]{1,0:T(8,128)S(1)} %copy-done.1, f32[128,128]{1,0:T(8,128)S(1)} %bitcast.24), custom_call_target="tpu_custom_call" | custom-call | tf_op jit(solution)/shard_map/partial_sums/pallas_call | solution.py:185
  54.4 6.4 %partial_sums.9 = f32[1,4,4,256,128]{4,3,2,1,0:T(8,128)} custom-call(s32[16384]{0:T(1024)S(1)} %compare_select_fusion.rows_ref, s32[7]{0:T(128)S(1)} %pad_add_fusion.1.plane_ref, f32[4096,128]{1,0:T(8,128)S(1)} %copy-done.1, f32[128,128]{1,0:T(8,128)S(1)} %bitcast.25, f32[2,4,4,256,128]{4,3,2,1,0:T(8,128)} %collective-permute-done.1.refs_0_), custom_call_target="tpu_custom_call" | custom-call | tf_op jit(solution)/shard_map/partial_sums/pallas_call | solution.py:185
  60.8 0.6 collective-permute-start.2
  61.4 6.4 %partial_sums.11 = f32[1,4,4,256,128]{4,3,2,1,0:T(8,128)} custom-call(s32[16384]{0:T(1024)S(1)} %compare_select_fusion.rows_ref, s32[7]{0:T(128)S(1)} %pad_add_fusion.1.plane_ref, f32[4096,128]{1,0:T(8,128)S(1)} %copy-done.1, f32[128,128]{1,0:T(8,128)S(1)} %bitcast.26, f32[2,4,4,256,128]{4,3,2,1,0:T(8,128)} %collective-permute-done.1.refs_0_), custom_call_target="tpu_custom_call" | custom-call | tf_op jit(solution)/shard_map/partial_sums/pallas_call | solution.py:185
  67.8 2.1 collective-permute-start.4
  69.9 6.4 %partial_sums.10 = f32[1,4,4,256,128]{4,3,2,1,0:T(8,128)} custom-call(s32[16384]{0:T(1024)S(1)} %compare_select_fusion.rows_ref, s32[7]{0:T(128)S(1)} %pad_add_fusion.1.plane_ref, f32[4096,128]{1,0:T(8,128)S(1)} %copy-done.1, f32[128,128]{1,0:T(8,128)S(1)} %bitcast.27, f32[2,4,4,256,128]{4,3,2,1,0:T(8,128)} %collective-permute-done.refs_0_), custom_call_target="tpu_custom_call" | custom-call | tf_op jit(solution)/shard_map/partial_sums/pallas_call | solution.py:185
  76.3 0.6 broadcast_in_dim.53
  76.9 5.4 %partial_sums.7 = f32[1,4,4,256,128]{4,3,2,1,0:T(8,128)S(1)} custom-call(s32[16384]{0:T(1024)S(1)} %compare_select_fusion.rows_ref, s32[7]{0:T(128)S(1)} %pad_add_fusion.1.plane_ref, f32[4096,128]{1,0:T(8,128)S(1)} %copy-done.1, f32[128,128]{1,0:T(8,128)S(1)} %bitcast.28, f32[2,4,4,256,128]{4,3,2,1,0:T(8,128)} %collective-permute-done.refs_0_), custom_call_target="tpu_custom_call" | custom-call | tf_op jit(solution)/shard_map/partial_sums/pallas_call | solution.py:185
  82.3 27.7 %collective-permute-done.2.refs_1_ = f32[4,4,256,128]{3,2,1,0:T(8,128)} collective-permute-done((f32[4,4,256,128]{3,2,1,0:T(8,128)}, f32[4,4,256,128]{3,2,1,0:T(8,128)}, u32[]{:S(2)}, u32[]{:S(2)}) %collective-permute-start.2) | collective-permute-done | bytes 2097184 | tf_op jit(solution)/shard_map/ppermute | solution.py:228
  110.0 5.7 %collective-permute-done.4.refs_3_ = f32[4,4,256,128]{3,2,1,0:T(8,128)} collective-permute-done((f32[4,4,256,128]{3,2,1,0:T(8,128)}, f32[4,4,256,128]{3,2,1,0:T(8,128)}, u32[]{:S(2)}, u32[]{:S(2)}) %collective-permute-start.4) | collective-permute-done | bytes 2097184 | tf_op jit(solution)/shard_map/ppermute | solution.py:228
  115.8 3.3 %sum_stage_1.1 = (f32[4,256,128]{2,1,0:T(8,128)S(1)}, f32[4,256,128]{2,1,0:T(8,128)S(1)}, f32[4,256,128]{2,1,0:T(8,128)S(1)}, f32[4,256,128]{2,1,0:T(8,128)S(1)}) custom-call(f32[4,4,256,128]{3,2,1,0:T(8,128)S(1)} %bitcast.22, f32[4,4,256,128]{3,2,1,0:T(8,128)} %collective-permute-done.2.refs_1_, f32[4,4,256,128]{3,2,1,0:T(8,128)} %collective-permute-done.3.refs_2_, ...), custom_call_target="tpu_custom_call" | custom-call | tf_op jit(solution)/shard_map/sum_stage_1/pallas_call | solution.py:209
  119.0 0.4 collective-permute-start.5
  119.4 1.6 collective-permute-start.6
  121.0 0.9 collective-permute-start.7
  121.9 12.5 %collective-permute-done.5.refs_1_ = f32[4,256,128]{2,1,0:T(8,128)S(1)} collective-permute-done((f32[4,256,128]{2,1,0:T(8,128)S(1)}, f32[4,256,128]{2,1,0:T(8,128)S(1)}, u32[]{:S(2)}, u32[]{:S(2)}) %collective-permute-start.5) | collective-permute-done | bytes 524320 | tf_op jit(solution)/shard_map/ppermute | solution.py:228
  134.5 0.8 collective-permute-done.7.refs_3_
  135.2 0.1 sum_stage_2.1
  135.3 0.6 copy-done.5
  136.0 0.8 collective-permute-start.10
  136.7 0.7 collective-permute-start.8
  137.5 0.6 collective-permute-start.9
  138.1 26.8 %all-gather.3.cloned.1.call-done = f32[2048,128]{1,0:T(8,128)} async-done(((f32[16,128]{1,0:T(8,128)}), f32[2048,128]{1,0:T(8,128)}) %all-gather.3.cloned.1.call-update) | async-done | bytes 1048592 | tf_op jit(solution)/shard_map/all_gather | solution.py:434
  164.8 1.7 slice.19
  166.6 0.6 copy-done.12
  167.3 1.9 user_block.1.refs_0_
  169.2 1.8 collective-permute-start.12
  171.0 1.5 collective-permute-start.13
  172.5 3.8 %collective-permute-done.11.refs_1_ = f32[264,128]{1,0:T(8,128)S(1)} collective-permute-done((f32[264,128]{1,0:T(8,128)}, f32[264,128]{1,0:T(8,128)S(1)}, u32[]{:S(2)}, u32[]{:S(2)}) %collective-permute-start.11) | collective-permute-done | bytes 135200 | tf_op jit(solution)/shard_map/ppermute | solution.py:228
  176.3 0.6 collective-permute-done.13.refs_3_
  176.8 0.9 copy-done.4
  177.9 1.9 collective-permute-start.15
  179.8 1.3 collective-permute-start.16
  181.1 12.3 %collective-permute-done.14.refs_1_ = f32[4,264,128]{2,1,0:T(8,128)S(1)} collective-permute-done((f32[4,264,128]{2,1,0:T(8,128)S(1)}, f32[4,264,128]{2,1,0:T(8,128)S(1)}, u32[]{:S(2)}, u32[]{:S(2)}) %collective-permute-start.14) | collective-permute-done | bytes 540704 | tf_op jit(solution)/shard_map/ppermute | solution.py:228
  193.4 0.6 collective-permute-done.16.refs_3_
  194.0 1.5 stack_blocks.3.refs_0_
  195.5 2.5 collective-permute-start.19
  198.0 0.6 collective-permute-start.17
  198.6 2.1 collective-permute-start.18
  200.7 0.1 concatenate.10.planes_ref
  200.8 1.4 collective-permute-done.19.refs_1_
  202.2 14.3 %add_rows.3 = (f32[4104,128]{1,0:T(8,128)S(1)}, f32[128,256]{1,0:T(8,128)S(1)}) custom-call(s32[16384]{0:T(1024)S(1)} %bitcast.31, s32[16384]{0:T(1024)S(1)} %maximum_bitcast_fusion.code_idx_ref, s32[14]{0:T(128)S(1)} %concatenate.10.planes_ref, f32[4,4,264,128]{3,2,1,0:T(8,128)} %stack_blocks.3.refs_0_, f32[4,4,264,128]{3,2,1,0:T(8,128)} %collective-permute-done.19.refs_1_), custom_call_target="tpu_custom_call" | custom-call | tf_op jit(solution)/shard_map/add_rows/pallas_call | solution.py:401
  216.5 8.9 %collective-permute-done.17.refs_0_ = f32[4,4,264,128]{3,2,1,0:T(8,128)} collective-permute-done((f32[4,4,264,128]{3,2,1,0:T(8,128)}, f32[4,4,264,128]{3,2,1,0:T(8,128)}, u32[]{:S(2)}, u32[]{:S(2)}) %collective-permute-start.17) | collective-permute-done | bytes 2162720 | tf_op jit(solution)/shard_map/ppermute | solution.py:228
  225.4 0.9 collective-permute-start.21
  226.3 1.7 collective-permute-start.20
  228.0 14.2 %add_rows.4 = (f32[4104,128]{1,0:T(8,128)S(1)}, f32[128,256]{1,0:T(8,128)S(1)}) custom-call(s32[16384]{0:T(1024)S(1)} %bitcast.32, s32[16384]{0:T(1024)S(1)} %maximum_bitcast_fusion.code_idx_ref, s32[14]{0:T(128)S(1)} %concatenate.10.planes_ref, f32[4,4,264,128]{3,2,1,0:T(8,128)} %collective-permute-done.17.refs_0_, ...), custom_call_target="tpu_custom_call" | custom-call | tf_op jit(solution)/shard_map/add_rows/pallas_call | solution.py:401
  242.2 1.4 copy-done.10
  243.6 0.7 copy-done.11
  244.3 14.4 %add_rows.5 = (f32[4104,128]{1,0:T(8,128)S(1)}, f32[128,256]{1,0:T(8,128)S(1)}) custom-call(s32[16384]{0:T(1024)S(1)} %bitcast.33, s32[16384]{0:T(1024)S(1)} %maximum_bitcast_fusion.code_idx_ref, s32[14]{0:T(128)S(1)} %concatenate.10.planes_ref, f32[4,4,264,128]{3,2,1,0:T(8,128)} %copy-done.10, f32[4,4,264,128]{3,2,1,0:T(8,128)} %copy-done.11, ...), custom_call_target="tpu_custom_call" | custom-call | tf_op jit(solution)/shard_map/add_rows/pallas_call | solution.py:401
  258.7 1.4 copy-done.2
  260.0 0.1 collective-permute-start.23
  260.1 4.1 %collective-permute-done.23.refs_1_ = f32[4,4,264,128]{3,2,1,0:T(8,128)S(1)} collective-permute-done((f32[4,4,264,128]{3,2,1,0:T(8,128)S(1)}, f32[4,4,264,128]{3,2,1,0:T(8,128)S(1)}, u32[]{:S(2)}, u32[]{:S(2)}) %collective-permute-start.23) | collective-permute-done | bytes 2162720 | tf_op jit(solution)/shard_map/ppermute | solution.py:243
  264.3 1.4 copy-done.9
  265.6 19.8 %update_rows.1 = (f32[4096,128]{1,0:T(8,128)}, f32[4096,128]{1,0:T(8,128)}) custom-call(s32[16384]{0:T(1024)S(1)} %bitcast.34, s32[16384]{0:T(1024)S(1)} %maximum_bitcast_fusion.code_idx_ref, s32[14]{0:T(128)S(1)} %concatenate.10.planes_ref, f32[4,4,264,128]{3,2,1,0:T(8,128)} %copy-done.8, f32[4,4,264,128]{3,2,1,0:T(8,128)} %copy-done.9, ...), custom_call_target="tpu_custom_call" | custom-call | tf_op jit(solution)/shard_map/update_rows/pallas_call | solution.py:401
  (52 shorter events, 0.6 us)
Async XLA Ops:
  7.2 19.5 %copy-start.15 = (s32[3]{0:T(128)S(1)}, s32[3]{0:T(128)}, u32[]{:S(2)}) copy-start(s32[3]{0:T(128)} %constant.35.clone) | copy-start | bytes 40
  7.2 19.5 %copy-start.16 = (s32[3]{0:T(128)S(1)}, s32[3]{0:T(128)}, u32[]{:S(2)}) copy-start(s32[3]{0:T(128)} %constant.36.clone) | copy-start | bytes 40
  7.2 19.6 %copy-start.17 = (s32[4]{0:T(128)S(1)}, s32[4]{0:T(128)}, u32[]{:S(2)}) copy-start(s32[4]{0:T(128)} %constant.34.clone) | copy-start | bytes 52
  7.2 1.6 copy-start
  8.8 0.7 copy-start.6
  9.6 0.7 copy-start.7
  10.2 28.0 %copy-start.1 = (f32[4096,128]{1,0:T(8,128)S(1)}, f32[4096,128]{1,0:T(8,128)}, u32[]{:S(2)}) copy-start(f32[4096,128]{1,0:T(8,128)} %refs_4_.1) | copy-start | bytes 6291460
  15.1 22.9 %all-to-all-start = ((f32[128,4,128]{2,1,0:T(4,128)}), f32[128,4,128]{2,1,0:T(4,128)S(1)}, u32[]{:S(2)}, u32[]{:S(2)}) async-start(f32[128,4,128]{2,1,0:T(4,128)} %request_lists.1), calls=%async_computation | async-start | bytes 524288 | tf_op jit(solution)/shard_map/all_to_all | solution.py:428
  26.6 138.2 %all-gather.3.cloned.1.call-start = ((), (), s32[]{:S(2)}) async-start(), calls=%async_computation.1 | async-start | bytes 1056768 | tf_op jit(solution)/shard_map/all_gather | solution.py:434
  46.0 8.4 %collective-permute-start.1 = (f32[2,4,4,256,128]{4,3,2,1,0:T(8,128)}, f32[2,4,4,256,128]{4,3,2,1,0:T(8,128)}, u32[]{:S(2)}, u32[]{:S(2)}) collective-permute-start(f32[2,4,4,256,128]{4,3,2,1,0:T(8,128)} %partial_sums.8), channel_id=1, source_target_pairs={{0,16},{16,0},{1,17},{17,1},{2,18},{18,2},{3,19},{19,3},{4,20},{20... | collective-permute-start | bytes 12582920 | tf_op jit(solution)/shard_map/ppermute | solution.py:243
  54.3 15.5 %collective-permute-start = (f32[2,4,4,256,128]{4,3,2,1,0:T(8,128)}, f32[2,4,4,256,128]{4,3,2,1,0:T(8,128)}, u32[]{:S(2)}, u32[]{:S(2)}) collective-permute-start(f32[2,4,4,256,128]{4,3,2,1,0:T(8,128)} %partial_sums.6), channel_id=1, source_target_pairs={{0,16},{16,0},{1,17},{17,1},{2,18},{18,2},{3,19},{19,3},{4,20},{20... | collective-permute-start | bytes 12582920 | tf_op jit(solution)/shard_map/ppermute | solution.py:243
  60.8 49.2 %collective-permute-start.2 = (f32[4,4,256,128]{3,2,1,0:T(8,128)}, f32[4,4,256,128]{3,2,1,0:T(8,128)}, u32[]{:S(2)}, u32[]{:S(2)}) collective-permute-start(f32[4,4,256,128]{3,2,1,0:T(8,128)} %bitcast.12), channel_id=1, source_target_pairs={{0,32},{1,33},{2,34},{3,35},{4,36},{5,37},{6,38},{7,39},{8,40},{9,... | collective-permute-start | bytes 6291464 | tf_op jit(solution)/shard_map/ppermute | solution.py:228
  67.8 48.0 %collective-permute-start.4 = (f32[4,4,256,128]{3,2,1,0:T(8,128)}, f32[4,4,256,128]{3,2,1,0:T(8,128)}, u32[]{:S(2)}, u32[]{:S(2)}) collective-permute-start(f32[4,4,256,128]{3,2,1,0:T(8,128)} %bitcast.14), channel_id=1, source_target_pairs={{0,96},{1,97},{2,98},{3,99},{4,100},{5,101},{6,102},{7,103},{8,104... | collective-permute-start | bytes 6291464 | tf_op jit(solution)/shard_map/ppermute | solution.py:228
  76.3 39.5 %collective-permute-start.3 = (f32[4,4,256,128]{3,2,1,0:T(8,128)}, f32[4,4,256,128]{3,2,1,0:T(8,128)}, u32[]{:S(2)}, u32[]{:S(2)}) collective-permute-start(f32[4,4,256,128]{3,2,1,0:T(8,128)} %bitcast.13), channel_id=1, source_target_pairs={{0,64},{1,65},{2,66},{3,67},{4,68},{5,69},{6,70},{7,71},{8,72},{9,... | collective-permute-start | bytes 6291464 | tf_op jit(solution)/shard_map/ppermute | solution.py:228
  119.0 15.5 %collective-permute-start.5 = (f32[4,256,128]{2,1,0:T(8,128)S(1)}, f32[4,256,128]{2,1,0:T(8,128)S(1)}, u32[]{:S(2)}, u32[]{:S(2)}) collective-permute-start(f32[4,256,128]{2,1,0:T(8,128)S(1)} %get-tuple-element.29), channel_id=1, source_target_pairs={{0,4},{1,5},{2,6},{3,7},{4,8},{5,9},{6,10},{7,11},{8,12},{9,13},{1... | collective-permute-start | bytes 1572872 | tf_op jit(solution)/shard_map/ppermute | solution.py:228
  119.4 15.0 %collective-permute-start.6 = (f32[4,256,128]{2,1,0:T(8,128)S(1)}, f32[4,256,128]{2,1,0:T(8,128)S(1)}, u32[]{:S(2)}, u32[]{:S(2)}) collective-permute-start(f32[4,256,128]{2,1,0:T(8,128)S(1)} %get-tuple-element.30), channel_id=1, source_target_pairs={{0,8},{1,9},{2,10},{3,11},{4,12},{5,13},{6,14},{7,15},{8,0},{9,1},... | collective-permute-start | bytes 1572872 | tf_op jit(solution)/shard_map/ppermute | solution.py:228
  121.0 14.2 %collective-permute-start.7 = (f32[4,256,128]{2,1,0:T(8,128)S(1)}, f32[4,256,128]{2,1,0:T(8,128)S(1)}, u32[]{:S(2)}, u32[]{:S(2)}) collective-permute-start(f32[4,256,128]{2,1,0:T(8,128)S(1)} %get-tuple-element.31), channel_id=1, source_target_pairs={{0,12},{1,13},{2,14},{3,15},{4,0},{5,1},{6,2},{7,3},{8,4},{9,5},{1... | collective-permute-start | bytes 1572872 | tf_op jit(solution)/shard_map/ppermute | solution.py:228
  135.3 0.7 copy-start.5
  136.0 30.5 %collective-permute-start.10 = (f32[256,128]{1,0:T(8,128)S(1)}, f32[256,128]{1,0:T(8,128)S(1)}, u32[]{:S(2)}, u32[]{:S(2)}) collective-permute-start(f32[256,128]{1,0:T(8,128)S(1)} %get-tuple-element.35), channel_id=1, source_target_pairs={{0,3},{1,0},{2,1},{3,2},{4,7},{5,4},{6,5},{7,6},{8,11},{9,8},{10,9... | collective-permute-start | bytes 393224 | tf_op jit(solution)/shard_map/ppermute | solution.py:228
  136.7 29.8 %collective-permute-start.8 = (f32[256,128]{1,0:T(8,128)S(1)}, f32[256,128]{1,0:T(8,128)S(1)}, u32[]{:S(2)}, u32[]{:S(2)}) collective-permute-start(f32[256,128]{1,0:T(8,128)S(1)} %get-tuple-element.33), channel_id=1, source_target_pairs={{0,1},{1,2},{2,3},{3,0},{4,5},{5,6},{6,7},{7,4},{8,9},{9,10},{10,1... | collective-permute-start | bytes 393224 | tf_op jit(solution)/shard_map/ppermute | solution.py:228
  137.5 29.1 %collective-permute-start.9 = (f32[256,128]{1,0:T(8,128)S(1)}, f32[256,128]{1,0:T(8,128)S(1)}, u32[]{:S(2)}, u32[]{:S(2)}) collective-permute-start(f32[256,128]{1,0:T(8,128)S(1)} %get-tuple-element.34), channel_id=1, source_target_pairs={{0,2},{1,3},{2,0},{3,1},{4,6},{5,7},{6,4},{7,5},{8,10},{9,11},{10,... | collective-permute-start | bytes 393224 | tf_op jit(solution)/shard_map/ppermute | solution.py:228
  166.5 0.7 copy-start.12
  166.5 0.7 copy-start.13
  166.6 0.7 copy-start.14
  169.2 7.0 %collective-permute-start.11 = (f32[264,128]{1,0:T(8,128)}, f32[264,128]{1,0:T(8,128)S(1)}, u32[]{:S(2)}, u32[]{:S(2)}) collective-permute-start(f32[264,128]{1,0:T(8,128)} %user_block.1.refs_0_), channel_id=1, source_target_pairs={{0,1},{1,2},{2,3},{3,0},{4,5},{5,6},{6,7},{7,4},{8,9},{9,10},{10,1... | collective-permute-start | bytes 405512 | tf_op jit(solution)/shard_map/ppermute | solution.py:228
  169.2 7.0 %collective-permute-start.12 = (f32[264,128]{1,0:T(8,128)}, f32[264,128]{1,0:T(8,128)S(1)}, u32[]{:S(2)}, u32[]{:S(2)}) collective-permute-start(f32[264,128]{1,0:T(8,128)} %user_block.1.refs_0_), channel_id=1, source_target_pairs={{0,2},{1,3},{2,0},{3,1},{4,6},{5,7},{6,4},{7,5},{8,10},{9,11},{10,... | collective-permute-start | bytes 405512 | tf_op jit(solution)/shard_map/ppermute | solution.py:228
  171.0 5.8 %collective-permute-start.13 = (f32[264,128]{1,0:T(8,128)}, f32[264,128]{1,0:T(8,128)S(1)}, u32[]{:S(2)}, u32[]{:S(2)}) collective-permute-start(f32[264,128]{1,0:T(8,128)} %user_block.1.refs_0_), channel_id=1, source_target_pairs={{0,3},{1,0},{2,1},{3,2},{4,7},{5,4},{6,5},{7,6},{8,11},{9,8},{10,9... | collective-permute-start | bytes 405512 | tf_op jit(solution)/shard_map/ppermute | solution.py:228
  176.8 0.9 copy-start.4
  177.8 15.6 %collective-permute-start.14 = (f32[4,264,128]{2,1,0:T(8,128)S(1)}, f32[4,264,128]{2,1,0:T(8,128)S(1)}, u32[]{:S(2)}, u32[]{:S(2)}) collective-permute-start(f32[4,264,128]{2,1,0:T(8,128)S(1)} %stack_blocks.2.refs_0_), channel_id=1, source_target_pairs={{0,4},{1,5},{2,6},{3,7},{4,8},{5,9},{6,10},{7,11},{8,12},{9,13},{1... | collective-permute-start | bytes 1622024 | tf_op jit(solution)/shard_map/ppermute | solution.py:228
  177.9 15.5 %collective-permute-start.15 = (f32[4,264,128]{2,1,0:T(8,128)S(1)}, f32[4,264,128]{2,1,0:T(8,128)S(1)}, u32[]{:S(2)}, u32[]{:S(2)}) collective-permute-start(f32[4,264,128]{2,1,0:T(8,128)S(1)} %stack_blocks.2.refs_0_), channel_id=1, source_target_pairs={{0,8},{1,9},{2,10},{3,11},{4,12},{5,13},{6,14},{7,15},{8,0},{9,1},... | collective-permute-start | bytes 1622024 | tf_op jit(solution)/shard_map/ppermute | solution.py:228
  179.8 14.2 %collective-permute-start.16 = (f32[4,264,128]{2,1,0:T(8,128)S(1)}, f32[4,264,128]{2,1,0:T(8,128)S(1)}, u32[]{:S(2)}, u32[]{:S(2)}) collective-permute-start(f32[4,264,128]{2,1,0:T(8,128)S(1)} %stack_blocks.2.refs_0_), channel_id=1, source_target_pairs={{0,12},{1,13},{2,14},{3,15},{4,0},{5,1},{6,2},{7,3},{8,4},{9,5},{1... | collective-permute-start | bytes 1622024 | tf_op jit(solution)/shard_map/ppermute | solution.py:228
  195.5 6.7 %collective-permute-start.19 = (f32[4,4,264,128]{3,2,1,0:T(8,128)}, f32[4,4,264,128]{3,2,1,0:T(8,128)}, u32[]{:S(2)}, u32[]{:S(2)}) collective-permute-start(f32[4,4,264,128]{3,2,1,0:T(8,128)} %stack_blocks.3.refs_0_), channel_id=1, source_target_pairs={{0,16},{16,0},{1,17},{17,1},{2,18},{18,2},{3,19},{19,3},{4,20},{20... | collective-permute-start | bytes 6488072 | tf_op jit(solution)/shard_map/ppermute | solution.py:243
  198.0 27.4 %collective-permute-start.17 = (f32[4,4,264,128]{3,2,1,0:T(8,128)}, f32[4,4,264,128]{3,2,1,0:T(8,128)}, u32[]{:S(2)}, u32[]{:S(2)}) collective-permute-start(f32[4,4,264,128]{3,2,1,0:T(8,128)} %stack_blocks.3.refs_0_), channel_id=1, source_target_pairs={{0,32},{1,33},{2,34},{3,35},{4,36},{5,37},{6,38},{7,39},{8,40},{9,... | collective-permute-start | bytes 6488072 | tf_op jit(solution)/shard_map/ppermute | solution.py:228
  198.6 26.9 %collective-permute-start.18 = (f32[4,4,264,128]{3,2,1,0:T(8,128)}, f32[4,4,264,128]{3,2,1,0:T(8,128)}, u32[]{:S(2)}, u32[]{:S(2)}) collective-permute-start(f32[4,4,264,128]{3,2,1,0:T(8,128)} %stack_blocks.3.refs_0_), channel_id=1, source_target_pairs={{0,96},{1,97},{2,98},{3,99},{4,100},{5,101},{6,102},{7,103},{8,104... | collective-permute-start | bytes 6488072 | tf_op jit(solution)/shard_map/ppermute | solution.py:228
  225.4 16.8 %collective-permute-start.21 = (f32[4,4,264,128]{3,2,1,0:T(8,128)}, f32[4,4,264,128]{3,2,1,0:T(8,128)S(1)}, u32[]{:S(2)}, u32[]{:S(2)}) collective-permute-start(f32[4,4,264,128]{3,2,1,0:T(8,128)} %collective-permute-done.17.refs_0_), channel_id=1, source_target_pairs={{0,16},{16,0},{1,17},{17,1},{2,18},{18,2},{3,19},{19,3},{4,20},{20... | collective-permute-start | bytes 6488072 | tf_op jit(solution)/shard_map/ppermute | solution.py:243
  226.3 15.9 %collective-permute-start.22 = (f32[4,4,264,128]{3,2,1,0:T(8,128)}, f32[4,4,264,128]{3,2,1,0:T(8,128)S(1)}, u32[]{:S(2)}, u32[]{:S(2)}) collective-permute-start(f32[4,4,264,128]{3,2,1,0:T(8,128)} %collective-permute-done.18.refs_1_), channel_id=1, source_target_pairs={{0,16},{16,0},{1,17},{17,1},{2,18},{18,2},{3,19},{19,3},{4,20},{20... | collective-permute-start | bytes 6488072 | tf_op jit(solution)/shard_map/ppermute | solution.py:243
  226.3 33.7 %collective-permute-start.20 = (f32[4,4,264,128]{3,2,1,0:T(8,128)}, f32[4,4,264,128]{3,2,1,0:T(8,128)S(1)}, u32[]{:S(2)}, u32[]{:S(2)}) collective-permute-start(f32[4,4,264,128]{3,2,1,0:T(8,128)} %stack_blocks.3.refs_0_), channel_id=1, source_target_pairs={{0,64},{1,65},{2,66},{3,67},{4,68},{5,69},{6,70},{7,71},{8,72},{9,... | collective-permute-start | bytes 6488072 | tf_op jit(solution)/shard_map/ppermute | solution.py:228
  242.2 1.4 copy-start.10
  242.2 2.0 copy-start.11
  244.3 21.4 %copy-start.3 = (f32[4096,128]{1,0:T(8,128)S(1)}, f32[4096,128]{1,0:T(8,128)}, u32[]{:S(2)}) copy-start(f32[4096,128]{1,0:T(8,128)} %refs_5_.1) | copy-start | bytes 6291460
  258.7 1.4 copy-start.2
  260.0 4.3 %copy-start.8 = (f32[4,4,264,128]{3,2,1,0:T(8,128)}, f32[4,4,264,128]{3,2,1,0:T(8,128)S(1)}, u32[]{:S(2)}) copy-start(f32[4,4,264,128]{3,2,1,0:T(8,128)S(1)} %collective-permute-done.20.refs_0_) | copy-start | bytes 6488068
  260.0 4.3 %collective-permute-start.23 = (f32[4,4,264,128]{3,2,1,0:T(8,128)S(1)}, f32[4,4,264,128]{3,2,1,0:T(8,128)S(1)}, u32[]{:S(2)}, u32[]{:S(2)}) collective-permute-start(f32[4,4,264,128]{3,2,1,0:T(8,128)S(1)} %collective-permute-done.20.refs_0_), channel_id=1, source_target_pairs={{0,16},{16,0},{1,17},{17,1},{2,18},{18,2},{3,19},{19,3},{4,20},{20... | collective-permute-start | bytes 6488072 | tf_op jit(solution)/shard_map/ppermute | solution.py:243
  264.3 1.4 copy-start.9
Sparse Core Ops, SparseCore 0:
  77.0 87.7 all-gather.2

commit v9 on v6

--- a/solution.py
+++ b/solution.py
@@ -126,9 +126,9 @@
     )(history_ids.T, positive_ids.reshape(1, users))
 
 
-def partial_kernel(rows_ref, plane_ref, table_ref, codes_ref, gram_ref, *refs, first, first_step):
-    from_ref = refs[0] if len(refs) == 10 else None
-    out_ref = refs[-9]
+def partial_kernel(rows_ref, plane_ref, table_ref, codes_ref, gram_ref, *refs, first, first_step, takes):
+    from_ref = refs[0] if takes else None
+    out_refs = refs[int(takes) : -8]
     picked_refs = refs[-8:]
     code_of = iota2((2 * LANES, LANES), 0).astype(f32)
     one = jnp.ones((2 * LANES, LANES), f32)
@@ -159,14 +159,20 @@
             if from_ref is not None:
                 block = block + from_ref[0, k, j, : 2 * LANES, :]
                 gram = gram + from_ref[0, k, j, 2 * LANES :, :]
-            out_ref[0, k, j, : 2 * LANES, :] = block
-            out_ref[0, k, j, 2 * LANES :, :] = gram
-
-
-def partial_sums(rows_idx, plane, table, codes, gram, firsts, received=None, place=0):
+            if len(out_refs) == 2:
+                out_refs[0][0, k, j] = block[:LANES]
+                out_refs[1][0, k, j, :LANES, :] = block[LANES:]
+                out_refs[1][0, k, j, LANES:, :] = gram
+            else:
+                out_refs[0][0, k, j, : 2 * LANES, :] = block
+                out_refs[0][0, k, j, 2 * LANES :, :] = gram
+
+
+def partial_sums(rows_idx, plane, table, codes, gram, firsts, received=None, place=0, split=False):
     rows_dev, width = table.shape
     n = len(firsts)
     block = (1, 2, 4, BLOCK_ROWS, width)
+    sizes = (LANES, BLOCK_ROWS - LANES) if split else (BLOCK_ROWS,)
 
     def whole(shape):
         return pl.BlockSpec(shape, lambda i, k, r, p: (0,) * len(shape))
@@ -178,25 +184,34 @@
         operands += (received,)
     return pl.pallas_call(
         functools.partial(
-            partial_kernel, first=firsts[0], first_step=firsts[-1] - firsts[0]
+            partial_kernel,
+            first=firsts[0],
+            first_step=firsts[-1] - firsts[0],
+            takes=received is not None,
         ),
         grid_spec=pltpu.PrefetchScalarGridSpec(
             num_scalar_prefetch=2,
             grid=(n, 2),
             in_specs=in_specs,
-            out_specs=pl.BlockSpec(block, lambda i, k, r, p: (i, k, 0, 0, 0)),
+            out_specs=[
+                pl.BlockSpec((1, 2, 4, size, width), lambda i, k, r, p: (i, k, 0, 0, 0))
+                for size in sizes
+            ],
             scratch_shapes=[pltpu.VMEM((LANES, width), f32)] * 8,
         ),
-        out_shape=jax.ShapeDtypeStruct((n, 4, 4, BLOCK_ROWS, width), f32),
+        out_shape=[jax.ShapeDtypeStruct((n, 4, 4, size, width), f32) for size in sizes],
         compiler_params=pltpu.CompilerParams(vmem_limit_bytes=32 * 2**20),
         name="partial_sums",
     )(*operands)
 
 
 def split_sum_kernel(*refs):
-    pieces, outs = refs[:4], refs[4:]
+    pieces, outs = refs[:-4], refs[-4:]
     for i in range(4):
-        outs[i][...] = (pieces[0][i] + pieces[1][i]) + (pieces[2][i] + pieces[3][i])
+        total = pieces[0][i]
+        for piece in pieces[1:]:
+            total = total + piece[i]
+        outs[i][...] = total
 
 
 def split_sums(pieces, name):
@@ -206,6 +221,22 @@
         compiler_params=pltpu.CompilerParams(vmem_limit_bytes=40 * 2**20),
         name=name,
     )(*pieces)
+
+
+def add_rows_kernel(block_ref, part_ref, out_ref, *, start):
+    end = start + part_ref.shape[2]
+    for k in range(4):
+        out_ref[k] = block_ref[k]
+        out_ref[k, :, start:end, :] = block_ref[k, :, start:end, :] + part_ref[k]
+
+
+def with_rows(block, part, start):
+    return pl.pallas_call(
+        functools.partial(add_rows_kernel, start=start),
+        out_shape=jax.ShapeDtypeStruct(block.shape, f32),
+        compiler_params=pltpu.CompilerParams(vmem_limit_bytes=24 * 2**20),
+        name="add_relayed",
+    )(block, part)
 
 
 def along(stage, by):
@@ -239,14 +270,21 @@
     swap = [(0, 1), (1, 0)]
     received = []
     for firsts in ((1, 3), (2, 0)):
-        mine = partial_sums(rows_idx, other, table, codes, gram, firsts)
+        (mine,) = partial_sums(rows_idx, other, table, codes, gram, firsts)
         received.append(lax.ppermute(mine, CORE, swap))
-    pieces = [None] * 4
-    for k, first in enumerate((1, 3, 2, 0)):
-        block = partial_sums(
-            rows_idx, own, table, codes, gram, (first,), received[k // 2], k % 2
+
+    def blocks(first, k, split=False):
+        outs = partial_sums(
+            rows_idx, own, table, codes, gram, (first,), received[k // 2], k % 2, split
         )
-        pieces[first] = shifted(block.reshape(block.shape[1:]), 0, first)
+        return [out.reshape(out.shape[1:]) for out in outs]
+
+    upper, lower = blocks(2, 2, True)
+    upper, lower = shifted(upper, 0, 1), shifted(lower, 0, 3)
+    (ahead,), (behind,), (here,) = blocks(1, 0), blocks(3, 1), blocks(0, 3)
+    ahead = shifted(with_rows(ahead, upper, 0), 0, 1)
+    behind = shifted(with_rows(behind, lower, LANES), 0, 3)
+    pieces = [here, ahead, behind]
     for stage in (1, 2):
         parts = split_sums(pieces, f"sum_stage_{stage}")
         pieces = [shifted(part, stage, by) for by, part in enumerate(parts)]

time: 269 us -> 266 us (0.989)
  waiting for transfers between devices: 137 us -> 128 us
  starting transfers between devices: 20.2 us -> 24.3 us
    ppermute x9 -> x10, waiting for transfers between devices: 48.6 us -> 36.5 us  [shifted(): return lax.ppermute(array, DP_ROWS, along(stage, by)) if by else array]
    all_gather x1, waiting for transfers between devices: 83 us -> 87.4 us  [shards(): blocks = lax.all_gather(block, DP_ROWS)]
    ppermute x9 -> x10, starting transfers between devices: 8.13 us -> 12.3 us  [shifted(): return lax.ppermute(array, DP_ROWS, along(stage, by)) if by else array]
  transfers between devices with their start and end apart: 13 -> 14, of which waited for: 10 -> 11; matrix products, arithmetic and copies ran while one was open for 2% -> 2% of each run, Pallas kernels for 11% -> 11%
where the time goes in v9:
time: 266 us; the launch traced here: 265 us
  waiting for transfers between devices  128 us (48%)
  Pallas kernels  87.7 us (33%)
  starting transfers between devices  24.3 us (9%)
  between operations  14.2 us (5%)
  matrix products  5.81 us (2%)
  local copies, waits for them, and re-layouts  4.01 us (2%)
    all_gather x1, waiting for transfers between devices, shards(): blocks = lax.all_gather(block, DP_ROWS)  87.4 us
    pallas_call x1, Pallas kernels, update_rows(): pl.pallas_call(functools.partial(update_kernel, sources=sources, coef=coe...  42.2 us
    pallas_call x6, Pallas kernels, partial_sums(): pl.pallas_call(functools.partial(partial_kernel, first=firsts[0], first_s...  37.3 us
    ppermute x10, waiting for transfers between devices, shifted(): return lax.ppermute(array, DP_ROWS, along(stage, by)) if by else array  36.5 us
    ppermute x10, starting transfers between devices, shifted(): return lax.ppermute(array, DP_ROWS, along(stage, by)) if by else array  12.3 us
    all_to_all x1, starting transfers between devices, shards(): lax.all_to_all(lists, DP_ROWS, split_axis=0, concat_axis=0, tiled=True)  11.5 us
    dot_general x1, matrix products, shards(): jnp.dot(item_table.T, item_table, precision=lax.Precision.HIGHEST, prefer...  5.81 us
    pallas_call x1, Pallas kernels, request_lists(): pl.pallas_call(functools.partial(list_kernel, slots=hist_len + 1, rows_de...  5.49 us
  transfers between devices with their start and end apart: 14, of which 11 were waited for; matrix products, arithmetic and copies ran while one was open for 2% of the time, Pallas kernels for 11%

profile of v9, /device:TPU:1, one launch (start us, length us, event | category | flops | bytes accessed | tf_op | source)
XLA Modules:
  0.0 265.1 jit_solution(10855718073774042176)
XLA Ops:
  7.2 5.5 %request_lists.1 = f32[128,2,128]{2,1,0:T(2,128)} custom-call(s32[50,128]{1,0:T(8,128)} %bitcast.42, s32[1,128]{1,0:T(1,128)} %bitcast.43), custom_call_target="tpu_custom_call" | custom-call | tf_op jit(solution)/shard_map/request_lists/pallas_call | solution.py:122
  12.7 11.5 %all-to-all-start = ((f32[128,2,128]{2,1,0:T(2,128)}), f32[128,2,128]{2,1,0:T(2,128)S(1)}, u32[]{:S(2)}, u32[]{:S(2)}) async-start(f32[128,2,128]{2,1,0:T(2,128)} %request_lists.1), calls=%async_computation | async-start | bytes 262144 | tf_op jit(solution)/shard_map/all_to_all | solution.py:434
  24.2 0.0 copy-start.6
  24.2 0.0 copy-start.7
  24.2 0.0 copy-start.8
  24.2 0.0 all-gather.3.cloned.1.call-start
  24.3 0.0 copy-start
  24.3 5.8 %fusion.7.gram_ref = f32[128,128]{1,0:T(8,128)S(1)} fusion(f32[4096,128]{1,0:T(8,128)} %table_ref.13), kind=kOutput, calls=%fused_computation.27 | convolution fusion | flops 805306368 | bytes 2162688 | tf_op jit(solution)/shard_map/dot_general | solution.py:427
  30.1 0.1 pad_add_fusion
  30.2 0.0 copy-done.6
  30.2 0.0 copy-done.7
  30.2 0.0 copy-done.8
  30.2 0.2 select_reduce_fusion.1
  30.4 0.1 pad_add_fusion.2.plane_ref
  30.5 3.9 %all-to-all-done = f32[128,2,128]{2,1,0:T(2,128)S(1)} async-done(((f32[128,2,128]{2,1,0:T(2,128)}), f32[128,2,128]{2,1,0:T(2,128)S(1)}, u32[]{:S(2)}, u32[]{:S(2)}) %all-to-all-start) | async-done | bytes 131104 | tf_op jit(solution)/shard_map/all_to_all | solution.py:434
  34.4 0.1 fusion.6
  34.5 0.0 copy-done
  34.5 7.8 %partial_sums.6 = f32[2,4,4,264,128]{4,3,2,1,0:T(8,128)} custom-call(s32[16384]{0:T(1024)S(1)} %compare_select_fusion.rows_ref, s32[7]{0:T(128)S(1)} %pad_add_fusion.2.plane_ref, f32[4096,128]{1,0:T(8,128)S(1)} %copy-done, f32[128,128]{1,0:T(8,128)S(1)} %bitcast.28, f32[128,128]{1,0:T(8,128)S(1)} %fusion.7.gram_ref), custom_call_target="tpu_custom_call" | custom-call | tf_op jit(solution)/shard_map/partial_sums/pallas_call | solution.py:185
  42.3 0.5 collective-permute-start
  42.8 7.8 %partial_sums.8 = f32[2,4,4,264,128]{4,3,2,1,0:T(8,128)} custom-call(s32[16384]{0:T(1024)S(1)} %compare_select_fusion.rows_ref, s32[7]{0:T(128)S(1)} %pad_add_fusion.2.plane_ref, f32[4096,128]{1,0:T(8,128)S(1)} %copy-done, f32[128,128]{1,0:T(8,128)S(1)} %bitcast.29, f32[128,128]{1,0:T(8,128)S(1)} %fusion.7.gram_ref), custom_call_target="tpu_custom_call" | custom-call | tf_op jit(solution)/shard_map/partial_sums/pallas_call | solution.py:185
  50.6 0.0 collective-permute-start.1
  50.6 0.1 pad_add_fusion.1.plane_ref
  50.7 0.0 collective-permute-done.refs_0_
  50.7 5.4 %partial_sums.10 = (f32[1,4,4,128,128]{4,3,2,1,0:T(8,128)S(1)}, f32[1,4,4,136,128]{4,3,2,1,0:T(8,128)S(1)}) custom-call(s32[16384]{0:T(1024)S(1)} %compare_select_fusion.rows_ref, s32[7]{0:T(128)S(1)} %pad_add_fusion.1.plane_ref, f32[4096,128]{1,0:T(8,128)S(1)} %copy-done, f32[128,128]{1,0:T(8,128)S(1)} %bitcast.30, f32[128,128]{1,0:T(8,128)S(1)} %fusion.7.gram_ref, ...), custom_call_target="tpu_custom_call" | custom-call | tf_op jit(solution)/shard_map/partial_sums/pallas_call | solution.py:185
  56.1 0.3 collective-permute-start.4
  56.4 1.2 collective-permute-start.2
  57.6 0.6 collective-permute-done.1.refs_0_
  58.2 5.4 %partial_sums.11 = f32[1,4,4,264,128]{4,3,2,1,0:T(8,128)S(1)} custom-call(s32[16384]{0:T(1024)S(1)} %compare_select_fusion.rows_ref, s32[7]{0:T(128)S(1)} %pad_add_fusion.1.plane_ref, f32[4096,128]{1,0:T(8,128)S(1)} %copy-done, f32[128,128]{1,0:T(8,128)S(1)} %bitcast.31, f32[128,128]{1,0:T(8,128)S(1)} %fusion.7.gram_ref, ...), custom_call_target="tpu_custom_call" | custom-call | tf_op jit(solution)/shard_map/partial_sums/pallas_call | solution.py:185
  63.7 5.4 %partial_sums.9 = f32[1,4,4,264,128]{4,3,2,1,0:T(8,128)S(1)} custom-call(s32[16384]{0:T(1024)S(1)} %compare_select_fusion.rows_ref, s32[7]{0:T(128)S(1)} %pad_add_fusion.1.plane_ref, f32[4096,128]{1,0:T(8,128)S(1)} %copy-done, f32[128,128]{1,0:T(8,128)S(1)} %bitcast.32, f32[128,128]{1,0:T(8,128)S(1)} %fusion.7.gram_ref, ...), custom_call_target="tpu_custom_call" | custom-call | tf_op jit(solution)/shard_map/partial_sums/pallas_call | solution.py:185
  69.1 2.5 collective-permute-done.2.part_ref
  71.6 0.2 add_relayed.2
  71.8 0.1 collective-permute-start.3
  71.9 0.0 collective-permute-done.4.part_ref
  71.9 0.2 add_relayed.3
  72.1 2.7 %collective-permute-start.5 = (f32[4,4,264,128]{3,2,1,0:T(8,128)S(1)}, f32[4,4,264,128]{3,2,1,0:T(8,128)S(1)}, u32[]{:S(2)}, u32[]{:S(2)}) collective-permute-start(f32[4,4,264,128]{3,2,1,0:T(8,128)S(1)} %add_relayed.3), channel_id=1, source_target_pairs={{0,96},{1,97},{2,98},{3,99},{4,100},{5,101},{6,102},{7,103},{8,104... | collective-permute-start | bytes 6488072 | tf_op jit(solution)/shard_map/ppermute | solution.py:253
  74.8 5.4 %partial_sums.7 = f32[1,4,4,264,128]{4,3,2,1,0:T(8,128)S(1)} custom-call(s32[16384]{0:T(1024)S(1)} %compare_select_fusion.rows_ref, s32[7]{0:T(128)S(1)} %pad_add_fusion.1.plane_ref, f32[4096,128]{1,0:T(8,128)S(1)} %copy-done, f32[128,128]{1,0:T(8,128)S(1)} %bitcast.33, f32[128,128]{1,0:T(8,128)S(1)} %fusion.7.gram_ref, ...), custom_call_target="tpu_custom_call" | custom-call | tf_op jit(solution)/shard_map/partial_sums/pallas_call | solution.py:185
  80.2 18.7 %collective-permute-done.3.refs_1_ = f32[4,4,264,128]{3,2,1,0:T(8,128)S(1)} collective-permute-done((f32[4,4,264,128]{3,2,1,0:T(8,128)S(1)}, f32[4,4,264,128]{3,2,1,0:T(8,128)S(1)}, u32[]{:S(2)}, u32[]{:S(2)}) %collective-permute-start.3) | collective-permute-done | bytes 2162720 | tf_op jit(solution)/shard_map/ppermute | solution.py:253
  98.9 0.0 collective-permute-done.5.refs_2_
  98.9 0.3 sum_stage_1.1
  99.3 0.5 collective-permute-start.6
  99.7 2.5 collective-permute-start.7
  102.3 1.1 collective-permute-start.8
  103.4 5.7 %collective-permute-done.6.refs_1_ = f32[4,264,128]{2,1,0:T(8,128)S(1)} collective-permute-done((f32[4,264,128]{2,1,0:T(8,128)S(1)}, f32[4,264,128]{2,1,0:T(8,128)S(1)}, u32[]{:S(2)}, u32[]{:S(2)}) %collective-permute-start.6) | collective-permute-done | bytes 540704 | tf_op jit(solution)/shard_map/ppermute | solution.py:253
  109.0 6.0 %collective-permute-done.7.refs_2_ = f32[4,264,128]{2,1,0:T(8,128)S(1)} collective-permute-done((f32[4,264,128]{2,1,0:T(8,128)S(1)}, f32[4,264,128]{2,1,0:T(8,128)S(1)}, u32[]{:S(2)}, u32[]{:S(2)}) %collective-permute-start.7) | collective-permute-done | bytes 540704 | tf_op jit(solution)/shard_map/ppermute | solution.py:253
  115.1 0.4 collective-permute-done.8.refs_3_
  115.5 0.2 sum_stage_2.1
  115.6 0.0 copy-start.2
  115.6 0.6 copy-done.2
  116.3 0.3 collective-permute-start.9
  116.5 2.7 %collective-permute-start.10 = (f32[264,128]{1,0:T(8,128)S(1)}, f32[264,128]{1,0:T(8,128)S(1)}, u32[]{:S(2)}, u32[]{:S(2)}) collective-permute-start(f32[264,128]{1,0:T(8,128)S(1)} %get-tuple-element.20), channel_id=1, source_target_pairs={{0,2},{1,3},{2,0},{3,1},{4,6},{5,7},{6,4},{7,5},{8,10},{9,11},{10,... | collective-permute-start | bytes 405512 | tf_op jit(solution)/shard_map/ppermute | solution.py:253
  119.2 0.9 collective-permute-start.11
  120.1 1.2 collective-permute-done.9.refs_1_
  121.4 1.7 collective-permute-done.10.refs_2_
  123.1 0.3 collective-permute-done.11.refs_3_
  123.4 0.0 copy-done.3
  123.4 0.4 copy-done.4
  123.7 0.3 copy-done.5
  124.0 1.9 user_block.1
  125.9 0.0 all-gather.3.cloned.1.call-update
  126.0 87.4 %all-gather.3.cloned.1.call-done = f32[33792,128]{1,0:T(8,128)} async-done(((f32[264,128]{1,0:T(8,128)}), f32[33792,128]{1,0:T(8,128)}) %all-gather.3.cloned.1.call-update) | async-done | bytes 17301520 | tf_op jit(solution)/shard_map/all_gather | solution.py:441
  213.3 1.1 slice.14
  214.4 0.0 copy-start.1
  214.5 1.6 copy-done.1
  216.0 42.2 %update_rows.1 = (f32[4096,128]{1,0:T(8,128)}, f32[4096,128]{1,0:T(8,128)}) custom-call(s32[16384]{0:T(1024)S(1)} %bitcast.36, s32[16384]{0:T(1024)S(1)} %fusion.2.src_idx_ref, f32[128,264,128]{2,1,0:T(8,128)} %bitcast.41, f32[128,128]{1,0:T(8,128)S(1)} %bitcast.37, f32[4096,128]{1,0:T(8,128)S(1)} %copy-done, f32[4096,128]{1,0:T(8,128)S(1)} %copy-done.1), custom_call_target="tpu_custom_call" | custom-call | tf_op jit(solution)/shard_map/update_rows/pallas_call | solution.py:395
  (6 shorter events, 0.0 us)
Async XLA Ops:
  12.7 21.7 %all-to-all-start = ((f32[128,2,128]{2,1,0:T(2,128)}), f32[128,2,128]{2,1,0:T(2,128)S(1)}, u32[]{:S(2)}, u32[]{:S(2)}) async-start(f32[128,2,128]{2,1,0:T(2,128)} %request_lists.1), calls=%async_computation | async-start | bytes 262144 | tf_op jit(solution)/shard_map/all_to_all | solution.py:434
  24.2 6.0 %copy-start.6 = (s32[3]{0:T(128)S(1)}, s32[3]{0:T(128)}, u32[]{:S(2)}) copy-start(s32[3]{0:T(128)} %constant.64.clone) | copy-start | bytes 40
  24.2 6.0 %copy-start.7 = (s32[3]{0:T(128)S(1)}, s32[3]{0:T(128)}, u32[]{:S(2)}) copy-start(s32[3]{0:T(128)} %constant.63.clone) | copy-start | bytes 40
  24.2 6.0 %copy-start.8 = (s32[4]{0:T(128)S(1)}, s32[4]{0:T(128)}, u32[]{:S(2)}) copy-start(s32[4]{0:T(128)} %constant.62.clone) | copy-start | bytes 52
  24.2 189.1 %all-gather.3.cloned.1.call-start = ((), (), s32[]{:S(2)}) async-start(), calls=%async_computation.1 | async-start | bytes 17436672 | tf_op jit(solution)/shard_map/all_gather | solution.py:441
  24.3 10.2 %copy-start = (f32[4096,128]{1,0:T(8,128)S(1)}, f32[4096,128]{1,0:T(8,128)}, u32[]{:S(2)}) copy-start(f32[4096,128]{1,0:T(8,128)} %table_ref.13) | copy-start | bytes 6291460
  42.3 8.4 %collective-permute-start = (f32[2,4,4,264,128]{4,3,2,1,0:T(8,128)}, f32[2,4,4,264,128]{4,3,2,1,0:T(8,128)}, u32[]{:S(2)}, u32[]{:S(2)}) collective-permute-start(f32[2,4,4,264,128]{4,3,2,1,0:T(8,128)} %partial_sums.6), channel_id=1, source_target_pairs={{0,16},{16,0},{1,17},{17,1},{2,18},{18,2},{3,19},{19,3},{4,20},{20... | collective-permute-start | bytes 12976136 | tf_op jit(solution)/shard_map/ppermute | solution.py:274
  50.6 7.7 %collective-permute-start.1 = (f32[2,4,4,264,128]{4,3,2,1,0:T(8,128)}, f32[2,4,4,264,128]{4,3,2,1,0:T(8,128)}, u32[]{:S(2)}, u32[]{:S(2)}) collective-permute-start(f32[2,4,4,264,128]{4,3,2,1,0:T(8,128)} %partial_sums.8), channel_id=1, source_target_pairs={{0,16},{16,0},{1,17},{17,1},{2,18},{18,2},{3,19},{19,3},{4,20},{20... | collective-permute-start | bytes 12976136 | tf_op jit(solution)/shard_map/ppermute | solution.py:274
  56.1 15.8 %collective-permute-start.4 = (f32[4,4,136,128]{3,2,1,0:T(8,128)S(1)}, f32[4,4,136,128]{3,2,1,0:T(8,128)S(1)}, u32[]{:S(2)}, u32[]{:S(2)}) collective-permute-start(f32[4,4,136,128]{3,2,1,0:T(8,128)S(1)} %bitcast.38), channel_id=1, source_target_pairs={{0,96},{1,97},{2,98},{3,99},{4,100},{5,101},{6,102},{7,103},{8,104... | collective-permute-start | bytes 3342344 | tf_op jit(solution)/shard_map/ppermute | solution.py:253
  56.4 15.2 %collective-permute-start.2 = (f32[4,4,128,128]{3,2,1,0:T(8,128)S(1)}, f32[4,4,128,128]{3,2,1,0:T(8,128)S(1)}, u32[]{:S(2)}, u32[]{:S(2)}) collective-permute-start(f32[4,4,128,128]{3,2,1,0:T(8,128)S(1)} %bitcast.39), channel_id=1, source_target_pairs={{0,32},{1,33},{2,34},{3,35},{4,36},{5,37},{6,38},{7,39},{8,40},{9,... | collective-permute-start | bytes 3145736 | tf_op jit(solution)/shard_map/ppermute | solution.py:253
  71.8 27.2 %collective-permute-start.3 = (f32[4,4,264,128]{3,2,1,0:T(8,128)S(1)}, f32[4,4,264,128]{3,2,1,0:T(8,128)S(1)}, u32[]{:S(2)}, u32[]{:S(2)}) collective-permute-start(f32[4,4,264,128]{3,2,1,0:T(8,128)S(1)} %add_relayed.2), channel_id=1, source_target_pairs={{0,32},{1,33},{2,34},{3,35},{4,36},{5,37},{6,38},{7,39},{8,40},{9,... | collective-permute-start | bytes 6488072 | tf_op jit(solution)/shard_map/ppermute | solution.py:253
  72.1 26.9 %collective-permute-start.5 = (f32[4,4,264,128]{3,2,1,0:T(8,128)S(1)}, f32[4,4,264,128]{3,2,1,0:T(8,128)S(1)}, u32[]{:S(2)}, u32[]{:S(2)}) collective-permute-start(f32[4,4,264,128]{3,2,1,0:T(8,128)S(1)} %add_relayed.3), channel_id=1, source_target_pairs={{0,96},{1,97},{2,98},{3,99},{4,100},{5,101},{6,102},{7,103},{8,104... | collective-permute-start | bytes 6488072 | tf_op jit(solution)/shard_map/ppermute | solution.py:253
  99.3 9.8 %collective-permute-start.6 = (f32[4,264,128]{2,1,0:T(8,128)S(1)}, f32[4,264,128]{2,1,0:T(8,128)S(1)}, u32[]{:S(2)}, u32[]{:S(2)}) collective-permute-start(f32[4,264,128]{2,1,0:T(8,128)S(1)} %get-tuple-element.15), channel_id=1, source_target_pairs={{0,4},{1,5},{2,6},{3,7},{4,8},{5,9},{6,10},{7,11},{8,12},{9,13},{1... | collective-permute-start | bytes 1622024 | tf_op jit(solution)/shard_map/ppermute | solution.py:253
  99.7 15.4 %collective-permute-start.7 = (f32[4,264,128]{2,1,0:T(8,128)S(1)}, f32[4,264,128]{2,1,0:T(8,128)S(1)}, u32[]{:S(2)}, u32[]{:S(2)}) collective-permute-start(f32[4,264,128]{2,1,0:T(8,128)S(1)} %get-tuple-element.16), channel_id=1, source_target_pairs={{0,8},{1,9},{2,10},{3,11},{4,12},{5,13},{6,14},{7,15},{8,0},{9,1},... | collective-permute-start | bytes 1622024 | tf_op jit(solution)/shard_map/ppermute | solution.py:253
  102.3 13.2 %collective-permute-start.8 = (f32[4,264,128]{2,1,0:T(8,128)S(1)}, f32[4,264,128]{2,1,0:T(8,128)S(1)}, u32[]{:S(2)}, u32[]{:S(2)}) collective-permute-start(f32[4,264,128]{2,1,0:T(8,128)S(1)} %get-tuple-element.17), channel_id=1, source_target_pairs={{0,12},{1,13},{2,14},{3,15},{4,0},{5,1},{6,2},{7,3},{8,4},{9,5},{1... | collective-permute-start | bytes 1622024 | tf_op jit(solution)/shard_map/ppermute | solution.py:253
  115.6 0.7 copy-start.2
  116.3 5.1 %collective-permute-start.9 = (f32[264,128]{1,0:T(8,128)S(1)}, f32[264,128]{1,0:T(8,128)S(1)}, u32[]{:S(2)}, u32[]{:S(2)}) collective-permute-start(f32[264,128]{1,0:T(8,128)S(1)} %get-tuple-element.19), channel_id=1, source_target_pairs={{0,1},{1,2},{2,3},{3,0},{4,5},{5,6},{6,7},{7,4},{8,9},{9,10},{10,1... | collective-permute-start | bytes 405512 | tf_op jit(solution)/shard_map/ppermute | solution.py:253
  116.5 6.6 %collective-permute-start.10 = (f32[264,128]{1,0:T(8,128)S(1)}, f32[264,128]{1,0:T(8,128)S(1)}, u32[]{:S(2)}, u32[]{:S(2)}) collective-permute-start(f32[264,128]{1,0:T(8,128)S(1)} %get-tuple-element.20), channel_id=1, source_target_pairs={{0,2},{1,3},{2,0},{3,1},{4,6},{5,7},{6,4},{7,5},{8,10},{9,11},{10,... | collective-permute-start | bytes 405512 | tf_op jit(solution)/shard_map/ppermute | solution.py:253
  119.2 4.1 %collective-permute-start.11 = (f32[264,128]{1,0:T(8,128)S(1)}, f32[264,128]{1,0:T(8,128)S(1)}, u32[]{:S(2)}, u32[]{:S(2)}) collective-permute-start(f32[264,128]{1,0:T(8,128)S(1)} %get-tuple-element.21), channel_id=1, source_target_pairs={{0,3},{1,0},{2,1},{3,2},{4,7},{5,4},{6,5},{7,6},{8,11},{9,8},{10,9... | collective-permute-start | bytes 405512 | tf_op jit(solution)/shard_map/ppermute | solution.py:253
  121.4 2.0 copy-start.3
  123.1 0.6 copy-start.4
  123.4 0.7 copy-start.5
  214.4 1.6 copy-start.1
Sparse Core Ops, SparseCore 0:
  126.0 87.2 all-gather.2

commit v10 on v9

--- a/solution.py
+++ b/solution.py
@@ -322,24 +322,27 @@
 
 
 def update_kernel(
-    row_idx_ref, src_idx_ref, blocks_ref, item_ref, table_ref, state_ref, new_table_ref, new_state_ref,
-    stage_ref, gram_ref, *acc_refs, sources, coef, hist_len,
+    row_idx_ref, src_idx_ref, blocks_ref, item_ref, table_ref, state_hbm, new_table_ref, new_state_ref,
+    stage_ref, gram_ref, total_ref, state_ref, state_sem, *acc_refs, sources, coef, hist_len,
 ):
+    fetch_state = pltpu.make_async_copy(state_hbm, state_ref, state_sem)
     g = pl.program_id(0)
     rows_dev = table_ref.shape[0]
     sq = (LANES, LANES)
 
     @pl.when(g == 0)
     def _():
+        fetch_state.start()
         gram_ref[...] = jnp.zeros_like(gram_ref)
         for acc in acc_refs:
             acc[...] = jnp.zeros_like(acc)
+        total_ref[...] = item_ref[:, 0, 1, :]
 
     diagonal = iota2(sq, 0) == iota2(sq, 1)
     users = jnp.concatenate(
         [blocks_ref[s, LANES : 2 * LANES, :] for s in range(sources)], axis=0
     )
-    pulls = dot_split(users, item_ref[...])
+    pulls = dot_split(users, total_ref[...])
     for s in range(sources):
         user = blocks_ref[s, LANES : 2 * LANES, :]
         gap_row = blocks_ref[s, 2 * LANES : 2 * LANES + 1, :]
@@ -370,6 +373,7 @@
 
     @pl.when(g == pl.num_programs(0) - 1)
     def _():
+        fetch_state.wait()
         step = 512
         gram = whole_gram(gram_ref[...])
 
@@ -387,7 +391,7 @@
         lax.fori_loop(0, rows_dev // step, finish, 0)
 
 
-def update_rows(row_idx, src_idx, blocks, item_total, table, state, coef, hist_len):
+def update_rows(row_idx, src_idx, blocks, table, state, coef, hist_len):
     rows_dev, width = table.shape
     devices = blocks.shape[0]
     sources = 16
@@ -399,14 +403,17 @@
             grid=(devices // sources,),
             in_specs=[
                 pl.BlockSpec((sources, BLOCK_ROWS, width), lambda g, r, s: (g, 0, 0)),
-                pl.BlockSpec((width, width), lambda g, r, s: (0, 0)),
+                pl.BlockSpec((devices, 1, 8, width), lambda g, r, s: (0, 2 * LANES // 8, 0, 0)),
                 whole,
-                whole,
+                pl.BlockSpec(memory_space=pltpu.HBM),
             ],
             out_specs=[whole, whole],
             scratch_shapes=[
                 pltpu.VMEM((sources * 2 * LANES, width), f32),
                 pltpu.VMEM((width, 2 * width), f32),
+                pltpu.VMEM((width, width), f32),
+                pltpu.VMEM((rows_dev, width), f32),
+                pltpu.SemaphoreType.DMA,
             ]
             + [pltpu.VMEM((rows_dev + 8, width), f32)] * CHAINS,
         ),
@@ -416,7 +423,7 @@
         ),
         compiler_params=pltpu.CompilerParams(vmem_limit_bytes=48 * 2**20),
         name="update_rows",
-    )(row_idx, src_idx, blocks, item_total, table, state)
+    )(row_idx, src_idx, blocks, blocks.reshape(devices, BLOCK_ROWS // 8, 8, width), table, pltpu.with_memory_space_constraint(state, pltpu.HBM))
 
 
 def shards(item_table, adagrad_state, history_ids, positive_ids):
@@ -439,10 +446,7 @@
     pieces = to_sources(jnp.where(rows < rows_dev, rows, 0), item_table, codes, item_gram)
     block = user_block(pieces, hist_len)
     blocks = lax.all_gather(block, DP_ROWS)
-    item_total = blocks[:, 2 * LANES + 1, :]
-    return update_rows(
-        rows, src_idx, blocks, item_total, item_table, adagrad_state, coef, hist_len
-    )
+    return update_rows(rows, src_idx, blocks, item_table, adagrad_state, coef, hist_len)
 
 
 def solution(mesh):

time: 266 us -> 263 us (0.989)
  local copies, waits for them, and re-layouts: 4.01 us -> 1.34 us
where the time goes in v10:
time: 263 us
  waiting for transfers between devices  128 us (49%)
  Pallas kernels  88.1 us (33%)
  starting transfers between devices  24.3 us (9%)
  between operations  14.2 us (5%)
  matrix products  5.81 us (2%)
    all_gather x1, waiting for transfers between devices, shards(): blocks = lax.all_gather(block, DP_ROWS)  87.4 us
    pallas_call x1, Pallas kernels, update_rows(): pl.pallas_call(functools.partial(update_kernel, sources=sources, coef=coe...  42.6 us
    pallas_call x6, Pallas kernels, partial_sums(): pl.pallas_call(functools.partial(partial_kernel, first=firsts[0], first_s...  37.3 us
    ppermute x10, waiting for transfers between devices, shifted(): return lax.ppermute(array, DP_ROWS, along(stage, by)) if by else array  36.6 us
    ppermute x10, starting transfers between devices, shifted(): return lax.ppermute(array, DP_ROWS, along(stage, by)) if by else array  12.3 us
    all_to_all x1, starting transfers between devices, shards(): lax.all_to_all(lists, DP_ROWS, split_axis=0, concat_axis=0, tiled=True)  11.5 us
    dot_general x1, matrix products, shards(): jnp.dot(item_table.T, item_table, precision=lax.Precision.HIGHEST, prefer...  5.81 us
    pallas_call x1, Pallas kernels, request_lists(): pl.pallas_call(functools.partial(list_kernel, slots=hist_len + 1, rows_de...  5.49 us
  transfers between devices with their start and end apart: 14, of which 11 were waited for; matrix products, arithmetic and copies ran while one was open for 2% of the time, Pallas kernels for 11%

profile of v10, /device:TPU:1, one launch (start us, length us, event | category | flops | bytes accessed | tf_op | source)
XLA Modules:
  0.0 262.8 jit_solution(17709021997371979107)
XLA Ops:
  7.2 5.5 %request_lists.1 = f32[128,2,128]{2,1,0:T(2,128)} custom-call(s32[50,128]{1,0:T(8,128)} %bitcast.39, s32[1,128]{1,0:T(1,128)} %bitcast.40), custom_call_target="tpu_custom_call" | custom-call | tf_op jit(solution)/shard_map/request_lists/pallas_call | solution.py:122
  12.7 11.5 %all-to-all-start = ((f32[128,2,128]{2,1,0:T(2,128)}), f32[128,2,128]{2,1,0:T(2,128)S(1)}, u32[]{:S(2)}, u32[]{:S(2)}) async-start(f32[128,2,128]{2,1,0:T(2,128)} %request_lists.1), calls=%async_computation | async-start | bytes 262144 | tf_op jit(solution)/shard_map/all_to_all | solution.py:441
  24.2 0.0 copy-start.5
  24.2 0.0 copy-start.6
  24.2 0.0 copy-start.7
  24.2 0.0 all-gather.3.cloned.1.call-start
  24.3 0.0 copy-start
  24.3 5.8 %fusion.7.gram_ref = f32[128,128]{1,0:T(8,128)S(1)} fusion(f32[4096,128]{1,0:T(8,128)} %table_ref.13), kind=kOutput, calls=%fused_computation.27 | convolution fusion | flops 805306368 | bytes 2162688 | tf_op jit(solution)/shard_map/dot_general | solution.py:434
  30.1 0.1 pad_add_fusion
  30.2 0.0 copy-done.5
  30.2 0.0 copy-done.6
  30.2 0.0 copy-done.7
  30.2 0.2 select_reduce_fusion.1
  30.4 0.1 pad_add_fusion.2.plane_ref
  30.5 3.9 %all-to-all-done = f32[128,2,128]{2,1,0:T(2,128)S(1)} async-done(((f32[128,2,128]{2,1,0:T(2,128)}), f32[128,2,128]{2,1,0:T(2,128)S(1)}, u32[]{:S(2)}, u32[]{:S(2)}) %all-to-all-start) | async-done | bytes 131104 | tf_op jit(solution)/shard_map/all_to_all | solution.py:441
  34.4 0.1 fusion.6
  34.5 0.0 copy-done
  34.5 7.8 %partial_sums.6 = f32[2,4,4,264,128]{4,3,2,1,0:T(8,128)} custom-call(s32[16384]{0:T(1024)S(1)} %compare_select_fusion.rows_ref, s32[7]{0:T(128)S(1)} %pad_add_fusion.2.plane_ref, f32[4096,128]{1,0:T(8,128)S(1)} %copy-done, f32[128,128]{1,0:T(8,128)S(1)} %bitcast.26, f32[128,128]{1,0:T(8,128)S(1)} %fusion.7.gram_ref), custom_call_target="tpu_custom_call" | custom-call | tf_op jit(solution)/shard_map/partial_sums/pallas_call | solution.py:185
  42.3 0.5 collective-permute-start
  42.8 7.8 %partial_sums.8 = f32[2,4,4,264,128]{4,3,2,1,0:T(8,128)} custom-call(s32[16384]{0:T(1024)S(1)} %compare_select_fusion.rows_ref, s32[7]{0:T(128)S(1)} %pad_add_fusion.2.plane_ref, f32[4096,128]{1,0:T(8,128)S(1)} %copy-done, f32[128,128]{1,0:T(8,128)S(1)} %bitcast.27, f32[128,128]{1,0:T(8,128)S(1)} %fusion.7.gram_ref), custom_call_target="tpu_custom_call" | custom-call | tf_op jit(solution)/shard_map/partial_sums/pallas_call | solution.py:185
  50.5 0.0 collective-permute-start.1
  50.6 0.1 pad_add_fusion.1.plane_ref
  50.7 0.0 collective-permute-done.refs_0_
  50.7 5.4 %partial_sums.10 = (f32[1,4,4,128,128]{4,3,2,1,0:T(8,128)S(1)}, f32[1,4,4,136,128]{4,3,2,1,0:T(8,128)S(1)}) custom-call(s32[16384]{0:T(1024)S(1)} %compare_select_fusion.rows_ref, s32[7]{0:T(128)S(1)} %pad_add_fusion.1.plane_ref, f32[4096,128]{1,0:T(8,128)S(1)} %copy-done, f32[128,128]{1,0:T(8,128)S(1)} %bitcast.28, f32[128,128]{1,0:T(8,128)S(1)} %fusion.7.gram_ref, ...), custom_call_target="tpu_custom_call" | custom-call | tf_op jit(solution)/shard_map/partial_sums/pallas_call | solution.py:185
  56.1 0.3 collective-permute-start.4
  56.4 1.2 collective-permute-start.2
  57.6 0.6 collective-permute-done.1.refs_0_
  58.2 5.4 %partial_sums.11 = f32[1,4,4,264,128]{4,3,2,1,0:T(8,128)S(1)} custom-call(s32[16384]{0:T(1024)S(1)} %compare_select_fusion.rows_ref, s32[7]{0:T(128)S(1)} %pad_add_fusion.1.plane_ref, f32[4096,128]{1,0:T(8,128)S(1)} %copy-done, f32[128,128]{1,0:T(8,128)S(1)} %bitcast.29, f32[128,128]{1,0:T(8,128)S(1)} %fusion.7.gram_ref, ...), custom_call_target="tpu_custom_call" | custom-call | tf_op jit(solution)/shard_map/partial_sums/pallas_call | solution.py:185
  63.7 5.4 %partial_sums.9 = f32[1,4,4,264,128]{4,3,2,1,0:T(8,128)S(1)} custom-call(s32[16384]{0:T(1024)S(1)} %compare_select_fusion.rows_ref, s32[7]{0:T(128)S(1)} %pad_add_fusion.1.plane_ref, f32[4096,128]{1,0:T(8,128)S(1)} %copy-done, f32[128,128]{1,0:T(8,128)S(1)} %bitcast.30, f32[128,128]{1,0:T(8,128)S(1)} %fusion.7.gram_ref, ...), custom_call_target="tpu_custom_call" | custom-call | tf_op jit(solution)/shard_map/partial_sums/pallas_call | solution.py:185
  69.1 2.5 collective-permute-done.2.part_ref
  71.6 0.2 add_relayed.2
  71.8 0.1 collective-permute-start.3
  71.8 0.0 collective-permute-done.4.part_ref
  71.9 0.2 add_relayed.3
  72.0 2.7 %collective-permute-start.5 = (f32[4,4,264,128]{3,2,1,0:T(8,128)S(1)}, f32[4,4,264,128]{3,2,1,0:T(8,128)S(1)}, u32[]{:S(2)}, u32[]{:S(2)}) collective-permute-start(f32[4,4,264,128]{3,2,1,0:T(8,128)S(1)} %add_relayed.3), channel_id=1, source_target_pairs={{0,96},{1,97},{2,98},{3,99},{4,100},{5,101},{6,102},{7,103},{8,104... | collective-permute-start | bytes 6488072 | tf_op jit(solution)/shard_map/ppermute | solution.py:253
  74.8 5.4 %partial_sums.7 = f32[1,4,4,264,128]{4,3,2,1,0:T(8,128)S(1)} custom-call(s32[16384]{0:T(1024)S(1)} %compare_select_fusion.rows_ref, s32[7]{0:T(128)S(1)} %pad_add_fusion.1.plane_ref, f32[4096,128]{1,0:T(8,128)S(1)} %copy-done, f32[128,128]{1,0:T(8,128)S(1)} %bitcast.31, f32[128,128]{1,0:T(8,128)S(1)} %fusion.7.gram_ref, ...), custom_call_target="tpu_custom_call" | custom-call | tf_op jit(solution)/shard_map/partial_sums/pallas_call | solution.py:185
  80.2 18.7 %collective-permute-done.3.refs_1_ = f32[4,4,264,128]{3,2,1,0:T(8,128)S(1)} collective-permute-done((f32[4,4,264,128]{3,2,1,0:T(8,128)S(1)}, f32[4,4,264,128]{3,2,1,0:T(8,128)S(1)}, u32[]{:S(2)}, u32[]{:S(2)}) %collective-permute-start.3) | collective-permute-done | bytes 2162720 | tf_op jit(solution)/shard_map/ppermute | solution.py:253
  98.9 0.0 collective-permute-done.5.refs_2_
  98.9 0.3 sum_stage_1.1
  99.2 0.5 collective-permute-start.6
  99.7 2.5 collective-permute-start.7
  102.2 1.1 collective-permute-start.8
  103.3 5.7 %collective-permute-done.6.refs_1_ = f32[4,264,128]{2,1,0:T(8,128)S(1)} collective-permute-done((f32[4,264,128]{2,1,0:T(8,128)S(1)}, f32[4,264,128]{2,1,0:T(8,128)S(1)}, u32[]{:S(2)}, u32[]{:S(2)}) %collective-permute-start.6) | collective-permute-done | bytes 540704 | tf_op jit(solution)/shard_map/ppermute | solution.py:253
  109.0 6.0 %collective-permute-done.7.refs_2_ = f32[4,264,128]{2,1,0:T(8,128)S(1)} collective-permute-done((f32[4,264,128]{2,1,0:T(8,128)S(1)}, f32[4,264,128]{2,1,0:T(8,128)S(1)}, u32[]{:S(2)}, u32[]{:S(2)}) %collective-permute-start.7) | collective-permute-done | bytes 540704 | tf_op jit(solution)/shard_map/ppermute | solution.py:253
  115.1 0.4 collective-permute-done.8.refs_3_
  115.4 0.2 sum_stage_2.1
  115.6 0.0 copy-start.1
  115.6 0.6 copy-done.1
  116.3 0.2 collective-permute-start.9
  116.5 2.7 %collective-permute-start.10 = (f32[264,128]{1,0:T(8,128)S(1)}, f32[264,128]{1,0:T(8,128)S(1)}, u32[]{:S(2)}, u32[]{:S(2)}) collective-permute-start(f32[264,128]{1,0:T(8,128)S(1)} %get-tuple-element.20), channel_id=1, source_target_pairs={{0,2},{1,3},{2,0},{3,1},{4,6},{5,7},{6,4},{7,5},{8,10},{9,11},{10,... | collective-permute-start | bytes 405512 | tf_op jit(solution)/shard_map/ppermute | solution.py:253
  119.2 0.9 collective-permute-start.11
  120.1 1.3 collective-permute-done.9.refs_1_
  121.3 0.0 copy-start.2
  121.3 1.7 collective-permute-done.10.refs_2_
  123.1 0.0 copy-start.3
  123.1 0.3 collective-permute-done.11.refs_3_
  123.4 0.0 copy-start.4
  123.4 0.0 copy-done.2
  123.4 0.3 copy-done.3
  123.7 0.3 copy-done.4
  124.0 1.9 user_block.1
  125.9 0.0 all-gather.3.cloned.1.call-update
  125.9 87.4 %all-gather.3.cloned.1.call-done = f32[33792,128]{1,0:T(8,128)} async-done(((f32[264,128]{1,0:T(8,128)}), f32[33792,128]{1,0:T(8,128)}) %all-gather.3.cloned.1.call-update) | async-done | bytes 17301520 | tf_op jit(solution)/shard_map/all_gather | solution.py:448
  213.3 42.6 %update_rows.1 = (f32[4096,128]{1,0:T(8,128)}, f32[4096,128]{1,0:T(8,128)}) custom-call(s32[16384]{0:T(1024)S(1)} %bitcast.34, s32[16384]{0:T(1024)S(1)} %fusion.2.src_idx_ref, f32[128,264,128]{2,1,0:T(8,128)} %bitcast.37, f32[128,33,8,128]{3,2,1,0:T(8,128)} %bitcast.38, f32[4096,128]{1,0:T(8,128)S(1)} %copy-done, f32[4096,128]{1,0:T(8,128)} %state_hbm.1), custom_call_target="tpu_custom_call" | custom-call | tf_op jit(solution)/shard_map/update_rows/pallas_call | solution.py:399
  (3 shorter events, 0.0 us)
Async XLA Ops:
  12.7 21.7 %all-to-all-start = ((f32[128,2,128]{2,1,0:T(2,128)}), f32[128,2,128]{2,1,0:T(2,128)S(1)}, u32[]{:S(2)}, u32[]{:S(2)}) async-start(f32[128,2,128]{2,1,0:T(2,128)} %request_lists.1), calls=%async_computation | async-start | bytes 262144 | tf_op jit(solution)/shard_map/all_to_all | solution.py:441
  24.2 6.0 %copy-start.5 = (s32[3]{0:T(128)S(1)}, s32[3]{0:T(128)}, u32[]{:S(2)}) copy-start(s32[3]{0:T(128)} %constant.64.clone) | copy-start | bytes 40
  24.2 6.0 %copy-start.6 = (s32[3]{0:T(128)S(1)}, s32[3]{0:T(128)}, u32[]{:S(2)}) copy-start(s32[3]{0:T(128)} %constant.63.clone) | copy-start | bytes 40
  24.2 6.0 %copy-start.7 = (s32[4]{0:T(128)S(1)}, s32[4]{0:T(128)}, u32[]{:S(2)}) copy-start(s32[4]{0:T(128)} %constant.62.clone) | copy-start | bytes 52
  24.2 189.1 %all-gather.3.cloned.1.call-start = ((), (), s32[]{:S(2)}) async-start(), calls=%async_computation.1 | async-start | bytes 17436672 | tf_op jit(solution)/shard_map/all_gather | solution.py:448
  24.3 10.2 %copy-start = (f32[4096,128]{1,0:T(8,128)S(1)}, f32[4096,128]{1,0:T(8,128)}, u32[]{:S(2)}) copy-start(f32[4096,128]{1,0:T(8,128)} %table_ref.13) | copy-start | bytes 6291460
  42.3 8.3 %collective-permute-start = (f32[2,4,4,264,128]{4,3,2,1,0:T(8,128)}, f32[2,4,4,264,128]{4,3,2,1,0:T(8,128)}, u32[]{:S(2)}, u32[]{:S(2)}) collective-permute-start(f32[2,4,4,264,128]{4,3,2,1,0:T(8,128)} %partial_sums.6), channel_id=1, source_target_pairs={{0,16},{16,0},{1,17},{17,1},{2,18},{18,2},{3,19},{19,3},{4,20},{20... | collective-permute-start | bytes 12976136 | tf_op jit(solution)/shard_map/ppermute | solution.py:274
  50.5 7.7 %collective-permute-start.1 = (f32[2,4,4,264,128]{4,3,2,1,0:T(8,128)}, f32[2,4,4,264,128]{4,3,2,1,0:T(8,128)}, u32[]{:S(2)}, u32[]{:S(2)}) collective-permute-start(f32[2,4,4,264,128]{4,3,2,1,0:T(8,128)} %partial_sums.8), channel_id=1, source_target_pairs={{0,16},{16,0},{1,17},{17,1},{2,18},{18,2},{3,19},{19,3},{4,20},{20... | collective-permute-start | bytes 12976136 | tf_op jit(solution)/shard_map/ppermute | solution.py:274
  56.1 15.8 %collective-permute-start.4 = (f32[4,4,136,128]{3,2,1,0:T(8,128)S(1)}, f32[4,4,136,128]{3,2,1,0:T(8,128)S(1)}, u32[]{:S(2)}, u32[]{:S(2)}) collective-permute-start(f32[4,4,136,128]{3,2,1,0:T(8,128)S(1)} %bitcast.35), channel_id=1, source_target_pairs={{0,96},{1,97},{2,98},{3,99},{4,100},{5,101},{6,102},{7,103},{8,104... | collective-permute-start | bytes 3342344 | tf_op jit(solution)/shard_map/ppermute | solution.py:253
  56.4 15.2 %collective-permute-start.2 = (f32[4,4,128,128]{3,2,1,0:T(8,128)S(1)}, f32[4,4,128,128]{3,2,1,0:T(8,128)S(1)}, u32[]{:S(2)}, u32[]{:S(2)}) collective-permute-start(f32[4,4,128,128]{3,2,1,0:T(8,128)S(1)} %bitcast.36), channel_id=1, source_target_pairs={{0,32},{1,33},{2,34},{3,35},{4,36},{5,37},{6,38},{7,39},{8,40},{9,... | collective-permute-start | bytes 3145736 | tf_op jit(solution)/shard_map/ppermute | solution.py:253
  71.8 27.2 %collective-permute-start.3 = (f32[4,4,264,128]{3,2,1,0:T(8,128)S(1)}, f32[4,4,264,128]{3,2,1,0:T(8,128)S(1)}, u32[]{:S(2)}, u32[]{:S(2)}) collective-permute-start(f32[4,4,264,128]{3,2,1,0:T(8,128)S(1)} %add_relayed.2), channel_id=1, source_target_pairs={{0,32},{1,33},{2,34},{3,35},{4,36},{5,37},{6,38},{7,39},{8,40},{9,... | collective-permute-start | bytes 6488072 | tf_op jit(solution)/shard_map/ppermute | solution.py:253
  72.0 26.9 %collective-permute-start.5 = (f32[4,4,264,128]{3,2,1,0:T(8,128)S(1)}, f32[4,4,264,128]{3,2,1,0:T(8,128)S(1)}, u32[]{:S(2)}, u32[]{:S(2)}) collective-permute-start(f32[4,4,264,128]{3,2,1,0:T(8,128)S(1)} %add_relayed.3), channel_id=1, source_target_pairs={{0,96},{1,97},{2,98},{3,99},{4,100},{5,101},{6,102},{7,103},{8,104... | collective-permute-start | bytes 6488072 | tf_op jit(solution)/shard_map/ppermute | solution.py:253
  99.2 9.8 %collective-permute-start.6 = (f32[4,264,128]{2,1,0:T(8,128)S(1)}, f32[4,264,128]{2,1,0:T(8,128)S(1)}, u32[]{:S(2)}, u32[]{:S(2)}) collective-permute-start(f32[4,264,128]{2,1,0:T(8,128)S(1)} %get-tuple-element.15), channel_id=1, source_target_pairs={{0,4},{1,5},{2,6},{3,7},{4,8},{5,9},{6,10},{7,11},{8,12},{9,13},{1... | collective-permute-start | bytes 1622024 | tf_op jit(solution)/shard_map/ppermute | solution.py:253
  99.7 15.4 %collective-permute-start.7 = (f32[4,264,128]{2,1,0:T(8,128)S(1)}, f32[4,264,128]{2,1,0:T(8,128)S(1)}, u32[]{:S(2)}, u32[]{:S(2)}) collective-permute-start(f32[4,264,128]{2,1,0:T(8,128)S(1)} %get-tuple-element.16), channel_id=1, source_target_pairs={{0,8},{1,9},{2,10},{3,11},{4,12},{5,13},{6,14},{7,15},{8,0},{9,1},... | collective-permute-start | bytes 1622024 | tf_op jit(solution)/shard_map/ppermute | solution.py:253
  102.2 13.2 %collective-permute-start.8 = (f32[4,264,128]{2,1,0:T(8,128)S(1)}, f32[4,264,128]{2,1,0:T(8,128)S(1)}, u32[]{:S(2)}, u32[]{:S(2)}) collective-permute-start(f32[4,264,128]{2,1,0:T(8,128)S(1)} %get-tuple-element.17), channel_id=1, source_target_pairs={{0,12},{1,13},{2,14},{3,15},{4,0},{5,1},{6,2},{7,3},{8,4},{9,5},{1... | collective-permute-start | bytes 1622024 | tf_op jit(solution)/shard_map/ppermute | solution.py:253
  115.6 0.7 copy-start.1
  116.3 5.1 %collective-permute-start.9 = (f32[264,128]{1,0:T(8,128)S(1)}, f32[264,128]{1,0:T(8,128)S(1)}, u32[]{:S(2)}, u32[]{:S(2)}) collective-permute-start(f32[264,128]{1,0:T(8,128)S(1)} %get-tuple-element.19), channel_id=1, source_target_pairs={{0,1},{1,2},{2,3},{3,0},{4,5},{5,6},{6,7},{7,4},{8,9},{9,10},{10,1... | collective-permute-start | bytes 405512 | tf_op jit(solution)/shard_map/ppermute | solution.py:253
  116.5 6.6 %collective-permute-start.10 = (f32[264,128]{1,0:T(8,128)S(1)}, f32[264,128]{1,0:T(8,128)S(1)}, u32[]{:S(2)}, u32[]{:S(2)}) collective-permute-start(f32[264,128]{1,0:T(8,128)S(1)} %get-tuple-element.20), channel_id=1, source_target_pairs={{0,2},{1,3},{2,0},{3,1},{4,6},{5,7},{6,4},{7,5},{8,10},{9,11},{10,... | collective-permute-start | bytes 405512 | tf_op jit(solution)/shard_map/ppermute | solution.py:253
  119.2 4.1 %collective-permute-start.11 = (f32[264,128]{1,0:T(8,128)S(1)}, f32[264,128]{1,0:T(8,128)S(1)}, u32[]{:S(2)}, u32[]{:S(2)}) collective-permute-start(f32[264,128]{1,0:T(8,128)S(1)} %get-tuple-element.21), channel_id=1, source_target_pairs={{0,3},{1,0},{2,1},{3,2},{4,7},{5,4},{6,5},{7,6},{8,11},{9,8},{10,9... | collective-permute-start | bytes 405512 | tf_op jit(solution)/shard_map/ppermute | solution.py:253
  121.3 2.0 copy-start.2
  123.1 0.7 copy-start.3
  123.4 0.7 copy-start.4
Sparse Core Ops, SparseCore 0:
  126.0 87.2 all-gather.2
